TPU v7x, 256 devices: a whole 4x4x8 slice. The times are simulated.
256 devices in a mesh: depth: 8 (over x_hi, y), row: 32 (over x_lo, z, core).
Axes of the slice: x: 4 (x_hi: 2, x_lo: 2; x = x_hi * 2 + x_lo), y: 4, z: 8, core: 2. Of those that a mesh axis runs over, the one named last changes fastest.
Arguments:
- index_volume: bfloat16 [8, 512, 2048], P('depth', 'row'), may hold values from -4 to 4
- angles: int32 [2], replicated, may hold values from 0 to 15
- offsets: int32 [8], P('depth'), may hold values from -4 to 4, as said below
- measured: bfloat16 [2, 512, 2048], P(None, 'row'), may hold values from 0 to 2
Outputs:
- gradient: float32 [8, 512, 2048], P('depth', 'row')
Inputs may be any that keep to these rules, and one draw needn't show every extreme that they name: `offsets`: each of -4 and 4 is taken by at least one slice.
All inputs are finite; a program needn't handle non-finite values.
Results may differ from a plain program's by a relative error of at most 0.0003.
Values may be sent and summed in bfloat16 or wider, within the bound.
A program may use at most 64 MiB of HBM per device.

v0:
```python
import math

import jax
import jax.numpy as jnp
from jax import lax
from jax.sharding import PartitionSpec as P

TILTS = 16
HALF = 10
SHIFT = 4
HALFCOL = 64
COLBLK = 128


PHASE_SCALE = 0.5
CHIRP_ROW = 1.3
CHIRP_COL = 1.7


def padded_2(shard, sides, width):
    for axis, dim in sides:
        size, length = (lax.axis_size(axis), shard.shape[dim])
        up = [(i, (i + 1) % size) for i in range(size - 1)]
        down = [(j, i) for i, j in up]
        last = lax.slice_in_dim(shard, length - width, length, axis=dim)
        initial = lax.slice_in_dim(shard, 0, width, axis=dim)
        before = lax.ppermute(last, axis, up)
        after = lax.ppermute(initial, axis, down)
        shard = jnp.concatenate([before, shard, after], axis=dim)
    return shard


def from_behind(shard, axis, by):
    length = lax.axis_size(axis)
    pairs = [(i, i + by) for i in range(length) if 0 <= i + by < length]
    return lax.ppermute(shard, axis, pairs)


def kernel_values(distance, radius, chirp_rate):
    inside = jnp.abs(distance) <= radius
    phase_arg = chirp_rate / radius * distance * distance
    weight = 1.0 / math.sqrt(2 * radius + 1)
    real_part = jnp.where(inside, jnp.cos(phase_arg) * weight, 0.0)
    imag_part = jnp.where(inside, jnp.sin(phase_arg) * weight, 0.0)
    return (real_part, imag_part)


def row_band(offset, height, margin, conjugate):
    extent = (height, height + 2 * margin)
    target = lax.broadcasted_iota(jnp.int32, extent, 0)
    source = lax.broadcasted_iota(jnp.int32, extent, 1)
    offset_used = -offset if conjugate else offset
    distance = (source - target - margin - offset_used).astype(jnp.float32)
    real_part, imag_part = kernel_values(distance, HALF, CHIRP_ROW)
    return (real_part, -imag_part) if conjugate else (real_part, imag_part)


def column_band(conjugate, block_width):
    extent = (block_width + 2 * HALFCOL, block_width)
    source = lax.broadcasted_iota(jnp.int32, extent, 0)
    target = lax.broadcasted_iota(jnp.int32, extent, 1)
    distance = (source - target - HALFCOL).astype(jnp.float32)
    real_part, imag_part = kernel_values(distance, HALFCOL, CHIRP_COL)
    return (real_part, -imag_part) if conjugate else (real_part, imag_part)


def mix_rows(band, extended):

    def product(matrix, operand):
        return jnp.einsum("ij,mjc->mic", matrix, operand, precision=lax.Precision.HIGHEST)

    real_part = product(band[0], extended[:, 0]) - product(band[1], extended[:, 1])
    imag_part = product(band[0], extended[:, 1]) + product(band[1], extended[:, 0])
    return jnp.stack([real_part, imag_part], axis=1)


def block_product(window, band):

    def product(operand, matrix):
        return jnp.einsum("mrbj,ji->mrbi", operand, matrix, precision=lax.Precision.HIGHEST)

    real_part = product(window[:, 0], band[0]) - product(window[:, 1], band[1])
    imag_part = product(window[:, 1], band[0]) + product(window[:, 0], band[1])
    return jnp.stack([real_part, imag_part], axis=1)


def mix_columns(band, field):
    amount, _, height, columns = field.shape
    blocks = columns // COLBLK
    padded = jnp.pad(field, ((0, 0), (0, 0), (0, 0), (HALFCOL, COLBLK - HALFCOL)))
    middle = padded[..., :columns].reshape(amount, 2, height, blocks, COLBLK)
    beyond = padded[..., COLBLK : columns + COLBLK].reshape(amount, 2, height, blocks, COLBLK)
    window = jnp.concatenate([middle, beyond], axis=4)
    return block_product(window, band).reshape(amount, 2, height, columns)


def rotate(field, cosine, sine):
    real_part = cosine * field[:, 0] - sine * field[:, 1]
    imag_part = cosine * field[:, 1] + sine * field[:, 0]
    return jnp.stack([real_part, imag_part], axis=1)


def slab_forward(field, index_volume, offsets, active):
    margin = HALF + SHIFT
    height = field.shape[2]
    col_band = column_band(False, COLBLK)
    phase_arg = PHASE_SCALE * index_volume[0].astype(jnp.float32)
    transmitted = rotate(field, jnp.cos(phase_arg), jnp.sin(phase_arg))
    stored_fields = [transmitted]
    extended = padded_2(transmitted, (("row", 2),), margin)
    band = row_band(offsets[0], height, margin, False)

    def advance(operand, band=band):
        return mix_columns(col_band, mix_rows(band, operand))

    def remain(operand):
        return operand[:, :, margin : margin + height, :]

    field = lax.cond(active, advance, remain, extended)
    return (field, jnp.stack(stored_fields, axis=0))


def slab_adjoint(adjoint, stored, index_volume, offsets, active):
    margin = HALF + SHIFT
    height = adjoint.shape[2]
    col_band = column_band(True, COLBLK)
    layers = index_volume.shape[0]
    slab_grads = [None] * layers

    def column_step(operand):
        return mix_columns(col_band, operand)

    def unchanged(operand):
        return operand

    def remain(operand):
        return operand[:, :, margin : margin + height, :]

    for layer_no in reversed(range(layers)):
        returned = lax.cond(active, column_step, unchanged, adjoint)
        extended = padded_2(returned, (("row", 2),), margin)
        band = row_band(offsets[layer_no], height, margin, True)

        def row_step(operand, band=band):
            return mix_rows(band, operand)

        returned = lax.cond(active, row_step, remain, extended)
        transmitted = stored[layer_no]
        slab_grads[layer_no] = PHASE_SCALE * jnp.sum(
            transmitted[:, 0] * returned[:, 1] - transmitted[:, 1] * returned[:, 0], axis=0
        )
        phase_arg = PHASE_SCALE * index_volume[layer_no].astype(jnp.float32)
        adjoint = rotate(returned, jnp.cos(phase_arg), -jnp.sin(phase_arg))
    return (adjoint, jnp.stack(slab_grads, axis=0))


def plane_waves(angles, row_start, height, columns, total_rows, total_cols):
    across = angles - TILTS // 2
    along = jnp.mod(3 * angles, TILTS) - TILTS // 2
    row_index = row_start + lax.broadcasted_iota(jnp.int32, (height, columns), 0)
    col_index = lax.broadcasted_iota(jnp.int32, (height, columns), 1)
    period = total_cols * total_rows
    cycles_int = jnp.mod(
        across[:, None, None] * col_index[None] * total_rows
        + along[:, None, None] * row_index[None] * total_cols,
        period,
    )
    phase_arg = 2.0 * math.pi / period * cycles_int.astype(jnp.float32)
    return jnp.stack([jnp.cos(phase_arg), jnp.sin(phase_arg)], axis=1)


def body(index_volume, angles, offsets, measured):
    sections = lax.axis_size("depth")
    section_no = lax.axis_index("depth")
    layers = index_volume.shape[0]
    height = index_volume.shape[1]
    columns = index_volume.shape[2]
    row_start = lax.axis_index("row") * height
    total_rows = height * lax.axis_size("row")
    intensity = measured.astype(jnp.float32)
    grad_init = jnp.zeros((layers, height, columns), jnp.float32)
    incident = plane_waves(angles, row_start, height, columns, total_rows, columns)
    kept_init = jnp.zeros((layers,) + incident.shape, jnp.float32)

    def forward_compute(counter, received, stored):
        entering = jnp.where(section_no == 0, incident, received)
        active = section_no == counter
        result, kept = slab_forward(entering, index_volume, offsets, active)
        return (result, jnp.where(active, kept, stored))

    def forward_turn(counter, carried):
        result, stored = forward_compute(counter, carried[0], carried[1])
        return (from_behind(result, "depth", 1), stored)

    zero_field = jnp.zeros_like(incident)
    received, stored = lax.fori_loop(0, sections - 1, forward_turn, (zero_field, kept_init))
    exit_field, stored = forward_compute(sections - 1, received, stored)
    errors = exit_field[:, 0] * exit_field[:, 0] + exit_field[:, 1] * exit_field[:, 1] - intensity
    exit_adjoint = 2.0 * errors[:, None] * exit_field

    def backward_compute(counter, received, gradient):
        entering = jnp.where(section_no == sections - 1, exit_adjoint, received)
        active = section_no == sections - 1 - counter
        result, slab_terms = slab_adjoint(entering, stored, index_volume, offsets, active)
        return (result, jnp.where(active, slab_terms, gradient))

    def backward_turn(counter, carried):
        result, gradient = backward_compute(counter, carried[0], carried[1])
        return (from_behind(result, "depth", -1), gradient)

    received, gradient = lax.fori_loop(0, sections - 1, backward_turn, (zero_field, grad_init))
    leftover, gradient = backward_compute(sections - 1, received, gradient)
    return gradient


def solution(mesh):
    in_specs = (P("depth", "row", None), P(), P("depth"), P(None, "row", None))
    out_specs = P("depth", "row", None)
    return jax.shard_map(body, mesh=mesh, in_specs=in_specs, out_specs=out_specs, check_vma=False)
```

profile of v0, /device:TPU:2, one launch (start us, length us, event | category | flops | bytes accessed | tf_op | source)
XLA Modules:
  0.0 568.1 jit_solution(13488313921636322094)
XLA Ops:
  4.7 240.2 %while.36 = (s32[]{:T(128)}, f32[2,2,16,2048]{3,2,0,1:T(8,128)S(1)}, f32[1,2,2,16,2048]{4,3,1,2,0:T(8,128)S(1)}, s32[]{:T(128)}, bf16[1,16,2048]{2,1,0:T(8,128)(...) while((s32[]{:T(128)}, ...), condition=%wide.region_3.4_spmd.clone, body=%wide.region_0.3_spmd.clone.sunk | while | flops 948276480 | bytes 38669416 | solution.py:196
  5.6 7.2 %collective-permute-start = (f32[2,2,14,2048]{3,2,0,1:T(8,128)S(1)}, f32[2,2,14,2048]{3,2,0,1:T(8,128)}, u32[]{:S(2)}, u32[]{:S(2)}) collective-permute-start(f32[2,2,14,2048]{3,2,0,1:T(8,128)S(1)} %get-tuple-element.1068), channel_id=1, source_target_pairs={{1,0},{2,1},{3,2},{4,3},{5,4},{6,5},{7,6},{8,7},{9,8},{10,9},{11,1... | collective-permute-start | bytes 1376264 | tf_op jit(solution)/shard_map/while/body/eval_jaxpr/ppermute | solution.py:28
  19.4 6.0 %collective-permute-done.1 = f32[2,2,14,2048]{3,2,0,1:T(8,128)} collective-permute-done((f32[2,2,14,2048]{3,2,0,1:T(8,128)S(1)}, f32[2,2,14,2048]{3,2,0,1:T(8,128)}, u32[]{:S(2)}, u32[]{:S(2)}) %collective-permute-start.1) | collective-permute-done | bytes 458784 | tf_op jit(solution)/shard_map/while/body/eval_jaxpr/ppermute | solution.py:27
  26.9 7.0 %conditional.15 = (f32[2,2,16,2048]{3,2,0,1:T(8,128)S(1)}) conditional(s32[]{:T(128)} %convert_element_type.243, f32[2,2,16,2048]{3,2,0,1:T(8,128)S(1)} %pad_maximum_fusion.18, (f32[16,44]{1,0:T(8,128)S(1)}, f32[2,2,44,2048]{3,2,0,1:T(8,128)S(1)}, f32[256,128]{1,0:T(8,128)S(1)}, f32[256,128]{1,0:T(8,128)S(1)}, f32[256,128]{1,0:T(8,128)S(1)}, ...), branch_computations={%region_1.1_spmd, %region_2.2_spmd} | conditional | flops 945750528 | bytes 18415624 | solution.py:119
  35.6 6.5 %collective-permute-done.2 = f32[2,2,16,2048]{3,2,0,1:T(8,128)S(1)} collective-permute-done((f32[2,2,16,2048]{3,2,0,1:T(8,128)S(1)}, f32[2,2,16,2048]{3,2,0,1:T(8,128)S(1)}, u32[]{:S(2)}, u32[]{:S(2)}) %collective-permute-start.2) | collective-permute-done | bytes 524320 | tf_op jit(solution)/shard_map/while/body/eval_jaxpr/ppermute | solution.py:36
  42.9 6.1 %collective-permute-start = (f32[2,2,14,2048]{3,2,0,1:T(8,128)S(1)}, f32[2,2,14,2048]{3,2,0,1:T(8,128)}, u32[]{:S(2)}, u32[]{:S(2)}) collective-permute-start(f32[2,2,14,2048]{3,2,0,1:T(8,128)S(1)} %get-tuple-element.1068), channel_id=1, source_target_pairs={{1,0},{2,1},{3,2},{4,3},{5,4},{6,5},{7,6},{8,7},{9,8},{10,9},{11,1... | collective-permute-start | bytes 1376264 | tf_op jit(solution)/shard_map/while/body/eval_jaxpr/ppermute | solution.py:28
  55.7 6.0 %collective-permute-done.1 = f32[2,2,14,2048]{3,2,0,1:T(8,128)} collective-permute-done((f32[2,2,14,2048]{3,2,0,1:T(8,128)S(1)}, f32[2,2,14,2048]{3,2,0,1:T(8,128)}, u32[]{:S(2)}, u32[]{:S(2)}) %collective-permute-start.1) | collective-permute-done | bytes 458784 | tf_op jit(solution)/shard_map/while/body/eval_jaxpr/ppermute | solution.py:27
  63.2 11.6 %collective-permute-start.2 = (f32[2,2,16,2048]{3,2,0,1:T(8,128)S(1)}, f32[2,2,16,2048]{3,2,0,1:T(8,128)S(1)}, u32[]{:S(2)}, u32[]{:S(2)}) collective-permute-start(f32[2,2,16,2048]{3,2,0,1:T(8,128)S(1)} %get-tuple-element.1158), channel_id=1, source_target_pairs={{0,32},{32,64},{64,96},{96,128},{128,160},{160,192},{192,224},{1,3... | collective-permute-start | bytes 1572872 | tf_op jit(solution)/shard_map/while/body/eval_jaxpr/ppermute | solution.py:36
  74.9 6.5 %collective-permute-done.2 = f32[2,2,16,2048]{3,2,0,1:T(8,128)S(1)} collective-permute-done((f32[2,2,16,2048]{3,2,0,1:T(8,128)S(1)}, f32[2,2,16,2048]{3,2,0,1:T(8,128)S(1)}, u32[]{:S(2)}, u32[]{:S(2)}) %collective-permute-start.2) | collective-permute-done | bytes 524320 | tf_op jit(solution)/shard_map/while/body/eval_jaxpr/ppermute | solution.py:36
  106.4 6.5 %collective-permute-done.2 = f32[2,2,16,2048]{3,2,0,1:T(8,128)S(1)} collective-permute-done((f32[2,2,16,2048]{3,2,0,1:T(8,128)S(1)}, f32[2,2,16,2048]{3,2,0,1:T(8,128)S(1)}, u32[]{:S(2)}, u32[]{:S(2)}) %collective-permute-start.2) | collective-permute-done | bytes 524320 | tf_op jit(solution)/shard_map/while/body/eval_jaxpr/ppermute | solution.py:36
  133.3 8.8 %collective-permute-start.2 = (f32[2,2,16,2048]{3,2,0,1:T(8,128)S(1)}, f32[2,2,16,2048]{3,2,0,1:T(8,128)S(1)}, u32[]{:S(2)}, u32[]{:S(2)}) collective-permute-start(f32[2,2,16,2048]{3,2,0,1:T(8,128)S(1)} %get-tuple-element.1158), channel_id=1, source_target_pairs={{0,32},{32,64},{64,96},{96,128},{128,160},{160,192},{192,224},{1,3... | collective-permute-start | bytes 1572872 | tf_op jit(solution)/shard_map/while/body/eval_jaxpr/ppermute | solution.py:36
  142.3 6.5 %collective-permute-done.2 = f32[2,2,16,2048]{3,2,0,1:T(8,128)S(1)} collective-permute-done((f32[2,2,16,2048]{3,2,0,1:T(8,128)S(1)}, f32[2,2,16,2048]{3,2,0,1:T(8,128)S(1)}, u32[]{:S(2)}, u32[]{:S(2)}) %collective-permute-start.2) | collective-permute-done | bytes 524320 | tf_op jit(solution)/shard_map/while/body/eval_jaxpr/ppermute | solution.py:36
  173.3 6.5 %collective-permute-done.2 = f32[2,2,16,2048]{3,2,0,1:T(8,128)S(1)} collective-permute-done((f32[2,2,16,2048]{3,2,0,1:T(8,128)S(1)}, f32[2,2,16,2048]{3,2,0,1:T(8,128)S(1)}, u32[]{:S(2)}, u32[]{:S(2)}) %collective-permute-start.2) | collective-permute-done | bytes 524320 | tf_op jit(solution)/shard_map/while/body/eval_jaxpr/ppermute | solution.py:36
  199.5 8.4 %collective-permute-start.2 = (f32[2,2,16,2048]{3,2,0,1:T(8,128)S(1)}, f32[2,2,16,2048]{3,2,0,1:T(8,128)S(1)}, u32[]{:S(2)}, u32[]{:S(2)}) collective-permute-start(f32[2,2,16,2048]{3,2,0,1:T(8,128)S(1)} %get-tuple-element.1158), channel_id=1, source_target_pairs={{0,32},{32,64},{64,96},{96,128},{128,160},{160,192},{192,224},{1,3... | collective-permute-start | bytes 1572872 | tf_op jit(solution)/shard_map/while/body/eval_jaxpr/ppermute | solution.py:36
  208.1 6.5 %collective-permute-done.2 = f32[2,2,16,2048]{3,2,0,1:T(8,128)S(1)} collective-permute-done((f32[2,2,16,2048]{3,2,0,1:T(8,128)S(1)}, f32[2,2,16,2048]{3,2,0,1:T(8,128)S(1)}, u32[]{:S(2)}, u32[]{:S(2)}) %collective-permute-start.2) | collective-permute-done | bytes 524320 | tf_op jit(solution)/shard_map/while/body/eval_jaxpr/ppermute | solution.py:36
  238.5 6.5 %collective-permute-done.2 = f32[2,2,16,2048]{3,2,0,1:T(8,128)S(1)} collective-permute-done((f32[2,2,16,2048]{3,2,0,1:T(8,128)S(1)}, f32[2,2,16,2048]{3,2,0,1:T(8,128)S(1)}, u32[]{:S(2)}, u32[]{:S(2)}) %collective-permute-start.2) | collective-permute-done | bytes 524320 | tf_op jit(solution)/shard_map/while/body/eval_jaxpr/ppermute | solution.py:36
  266.1 276.1 %while.37 = (s32[]{:T(128)}, f32[2,2,16,2048]{3,2,0,1:T(8,128)S(1)}, f32[1,16,2048]{2,1,0:T(8,128)}, bf16[1,16,2048]{2,1,0:T(8,128)(2,1)S(1)}, s32[]{:T(128)}, /...) while((s32[]{:T(128)}, ...), condition=%wide.region_12.13_spmd.clone, body=%wide.region_6.12_spmd.clone.sunk | while | flops 946623104 | bytes 39718116 | solution.py:211
  287.6 17.7 %collective-permute-done.5 = f32[2,2,16,2048]{3,2,0,1:T(8,128)S(1)} collective-permute-done((f32[2,2,16,2048]{3,2,0,1:T(8,128)S(1)}, f32[2,2,16,2048]{3,2,0,1:T(8,128)S(1)}, u32[]{:S(2)}, u32[]{:S(2)}) %collective-permute-start.5) | collective-permute-done | bytes 524320 | tf_op jit(solution)/shard_map/while/body/eval_jaxpr/ppermute | solution.py:36
  322.7 14.7 %collective-permute-done.5 = f32[2,2,16,2048]{3,2,0,1:T(8,128)S(1)} collective-permute-done((f32[2,2,16,2048]{3,2,0,1:T(8,128)S(1)}, f32[2,2,16,2048]{3,2,0,1:T(8,128)S(1)}, u32[]{:S(2)}, u32[]{:S(2)}) %collective-permute-start.5) | collective-permute-done | bytes 524320 | tf_op jit(solution)/shard_map/while/body/eval_jaxpr/ppermute | solution.py:36
  354.8 13.6 %collective-permute-done.5 = f32[2,2,16,2048]{3,2,0,1:T(8,128)S(1)} collective-permute-done((f32[2,2,16,2048]{3,2,0,1:T(8,128)S(1)}, f32[2,2,16,2048]{3,2,0,1:T(8,128)S(1)}, u32[]{:S(2)}, u32[]{:S(2)}) %collective-permute-start.5) | collective-permute-done | bytes 524320 | tf_op jit(solution)/shard_map/while/body/eval_jaxpr/ppermute | solution.py:36
  385.8 14.7 %collective-permute-done.5 = f32[2,2,16,2048]{3,2,0,1:T(8,128)S(1)} collective-permute-done((f32[2,2,16,2048]{3,2,0,1:T(8,128)S(1)}, f32[2,2,16,2048]{3,2,0,1:T(8,128)S(1)}, u32[]{:S(2)}, u32[]{:S(2)}) %collective-permute-start.5) | collective-permute-done | bytes 524320 | tf_op jit(solution)/shard_map/while/body/eval_jaxpr/ppermute | solution.py:36
  417.8 13.9 %collective-permute-done.5 = f32[2,2,16,2048]{3,2,0,1:T(8,128)S(1)} collective-permute-done((f32[2,2,16,2048]{3,2,0,1:T(8,128)S(1)}, f32[2,2,16,2048]{3,2,0,1:T(8,128)S(1)}, u32[]{:S(2)}, u32[]{:S(2)}) %collective-permute-start.5) | collective-permute-done | bytes 524320 | tf_op jit(solution)/shard_map/while/body/eval_jaxpr/ppermute | solution.py:36
  449.1 14.3 %collective-permute-done.5 = f32[2,2,16,2048]{3,2,0,1:T(8,128)S(1)} collective-permute-done((f32[2,2,16,2048]{3,2,0,1:T(8,128)S(1)}, f32[2,2,16,2048]{3,2,0,1:T(8,128)S(1)}, u32[]{:S(2)}, u32[]{:S(2)}) %collective-permute-start.5) | collective-permute-done | bytes 524320 | tf_op jit(solution)/shard_map/while/body/eval_jaxpr/ppermute | solution.py:36
  480.8 61.5 %collective-permute-done.5 = f32[2,2,16,2048]{3,2,0,1:T(8,128)S(1)} collective-permute-done((f32[2,2,16,2048]{3,2,0,1:T(8,128)S(1)}, f32[2,2,16,2048]{3,2,0,1:T(8,128)S(1)}, u32[]{:S(2)}, u32[]{:S(2)}) %collective-permute-start.5) | collective-permute-done | bytes 524320 | tf_op jit(solution)/shard_map/while/body/eval_jaxpr/ppermute | solution.py:36
  (397 shorter events, 322.8 us)
Async XLA Ops:
  5.6 13.9 %collective-permute-start = (f32[2,2,14,2048]{3,2,0,1:T(8,128)S(1)}, f32[2,2,14,2048]{3,2,0,1:T(8,128)}, u32[]{:S(2)}, u32[]{:S(2)}) collective-permute-start(f32[2,2,14,2048]{3,2,0,1:T(8,128)S(1)} %get-tuple-element.1068), channel_id=1, source_target_pairs={{1,0},{2,1},{3,2},{4,3},{5,4},{6,5},{7,6},{8,7},{9,8},{10,9},{11,1... | collective-permute-start | bytes 1376264 | tf_op jit(solution)/shard_map/while/body/eval_jaxpr/ppermute | solution.py:28
  12.8 12.7 %collective-permute-start.1 = (f32[2,2,14,2048]{3,2,0,1:T(8,128)S(1)}, f32[2,2,14,2048]{3,2,0,1:T(8,128)}, u32[]{:S(2)}, u32[]{:S(2)}) collective-permute-start(f32[2,2,14,2048]{3,2,0,1:T(8,128)S(1)} %get-tuple-element.1069), channel_id=1, source_target_pairs={{0,1},{1,2},{2,3},{3,4},{4,5},{5,6},{6,7},{7,8},{8,9},{9,10},{10,1... | collective-permute-start | bytes 1376264 | tf_op jit(solution)/shard_map/while/body/eval_jaxpr/ppermute | solution.py:27
  42.9 12.8 %collective-permute-start = (f32[2,2,14,2048]{3,2,0,1:T(8,128)S(1)}, f32[2,2,14,2048]{3,2,0,1:T(8,128)}, u32[]{:S(2)}, u32[]{:S(2)}) collective-permute-start(f32[2,2,14,2048]{3,2,0,1:T(8,128)S(1)} %get-tuple-element.1068), channel_id=1, source_target_pairs={{1,0},{2,1},{3,2},{4,3},{5,4},{6,5},{7,6},{8,7},{9,8},{10,9},{11,1... | collective-permute-start | bytes 1376264 | tf_op jit(solution)/shard_map/while/body/eval_jaxpr/ppermute | solution.py:28
  49.0 12.7 %collective-permute-start.1 = (f32[2,2,14,2048]{3,2,0,1:T(8,128)S(1)}, f32[2,2,14,2048]{3,2,0,1:T(8,128)}, u32[]{:S(2)}, u32[]{:S(2)}) collective-permute-start(f32[2,2,14,2048]{3,2,0,1:T(8,128)S(1)} %get-tuple-element.1069), channel_id=1, source_target_pairs={{0,1},{1,2},{2,3},{3,4},{4,5},{5,6},{6,7},{7,8},{8,9},{9,10},{10,1... | collective-permute-start | bytes 1376264 | tf_op jit(solution)/shard_map/while/body/eval_jaxpr/ppermute | solution.py:27
  63.2 18.2 %collective-permute-start.2 = (f32[2,2,16,2048]{3,2,0,1:T(8,128)S(1)}, f32[2,2,16,2048]{3,2,0,1:T(8,128)S(1)}, u32[]{:S(2)}, u32[]{:S(2)}) collective-permute-start(f32[2,2,16,2048]{3,2,0,1:T(8,128)S(1)} %get-tuple-element.1158), channel_id=1, source_target_pairs={{0,32},{32,64},{64,96},{96,128},{128,160},{160,192},{192,224},{1,3... | collective-permute-start | bytes 1572872 | tf_op jit(solution)/shard_map/while/body/eval_jaxpr/ppermute | solution.py:36
  87.8 12.7 %collective-permute-start.1 = (f32[2,2,14,2048]{3,2,0,1:T(8,128)S(1)}, f32[2,2,14,2048]{3,2,0,1:T(8,128)}, u32[]{:S(2)}, u32[]{:S(2)}) collective-permute-start(f32[2,2,14,2048]{3,2,0,1:T(8,128)S(1)} %get-tuple-element.1069), channel_id=1, source_target_pairs={{0,1},{1,2},{2,3},{3,4},{4,5},{5,6},{6,7},{7,8},{8,9},{9,10},{10,1... | collective-permute-start | bytes 1376264 | tf_op jit(solution)/shard_map/while/body/eval_jaxpr/ppermute | solution.py:27
  119.2 12.7 %collective-permute-start.1 = (f32[2,2,14,2048]{3,2,0,1:T(8,128)S(1)}, f32[2,2,14,2048]{3,2,0,1:T(8,128)}, u32[]{:S(2)}, u32[]{:S(2)}) collective-permute-start(f32[2,2,14,2048]{3,2,0,1:T(8,128)S(1)} %get-tuple-element.1069), channel_id=1, source_target_pairs={{0,1},{1,2},{2,3},{3,4},{4,5},{5,6},{6,7},{7,8},{8,9},{9,10},{10,1... | collective-permute-start | bytes 1376264 | tf_op jit(solution)/shard_map/while/body/eval_jaxpr/ppermute | solution.py:27
  133.3 15.5 %collective-permute-start.2 = (f32[2,2,16,2048]{3,2,0,1:T(8,128)S(1)}, f32[2,2,16,2048]{3,2,0,1:T(8,128)S(1)}, u32[]{:S(2)}, u32[]{:S(2)}) collective-permute-start(f32[2,2,16,2048]{3,2,0,1:T(8,128)S(1)} %get-tuple-element.1158), channel_id=1, source_target_pairs={{0,32},{32,64},{64,96},{96,128},{128,160},{160,192},{192,224},{1,3... | collective-permute-start | bytes 1572872 | tf_op jit(solution)/shard_map/while/body/eval_jaxpr/ppermute | solution.py:36
  154.5 12.7 %collective-permute-start.1 = (f32[2,2,14,2048]{3,2,0,1:T(8,128)S(1)}, f32[2,2,14,2048]{3,2,0,1:T(8,128)}, u32[]{:S(2)}, u32[]{:S(2)}) collective-permute-start(f32[2,2,14,2048]{3,2,0,1:T(8,128)S(1)} %get-tuple-element.1069), channel_id=1, source_target_pairs={{0,1},{1,2},{2,3},{3,4},{4,5},{5,6},{6,7},{7,8},{8,9},{9,10},{10,1... | collective-permute-start | bytes 1376264 | tf_op jit(solution)/shard_map/while/body/eval_jaxpr/ppermute | solution.py:27
  185.4 12.7 %collective-permute-start.1 = (f32[2,2,14,2048]{3,2,0,1:T(8,128)S(1)}, f32[2,2,14,2048]{3,2,0,1:T(8,128)}, u32[]{:S(2)}, u32[]{:S(2)}) collective-permute-start(f32[2,2,14,2048]{3,2,0,1:T(8,128)S(1)} %get-tuple-element.1069), channel_id=1, source_target_pairs={{0,1},{1,2},{2,3},{3,4},{4,5},{5,6},{6,7},{7,8},{8,9},{9,10},{10,1... | collective-permute-start | bytes 1376264 | tf_op jit(solution)/shard_map/while/body/eval_jaxpr/ppermute | solution.py:27
  199.5 15.0 %collective-permute-start.2 = (f32[2,2,16,2048]{3,2,0,1:T(8,128)S(1)}, f32[2,2,16,2048]{3,2,0,1:T(8,128)S(1)}, u32[]{:S(2)}, u32[]{:S(2)}) collective-permute-start(f32[2,2,16,2048]{3,2,0,1:T(8,128)S(1)} %get-tuple-element.1158), channel_id=1, source_target_pairs={{0,32},{32,64},{64,96},{96,128},{128,160},{160,192},{192,224},{1,3... | collective-permute-start | bytes 1572872 | tf_op jit(solution)/shard_map/while/body/eval_jaxpr/ppermute | solution.py:36
  219.3 12.7 %collective-permute-start.1 = (f32[2,2,14,2048]{3,2,0,1:T(8,128)S(1)}, f32[2,2,14,2048]{3,2,0,1:T(8,128)}, u32[]{:S(2)}, u32[]{:S(2)}) collective-permute-start(f32[2,2,14,2048]{3,2,0,1:T(8,128)S(1)} %get-tuple-element.1069), channel_id=1, source_target_pairs={{0,1},{1,2},{2,3},{3,4},{4,5},{5,6},{6,7},{7,8},{8,9},{9,10},{10,1... | collective-permute-start | bytes 1376264 | tf_op jit(solution)/shard_map/while/body/eval_jaxpr/ppermute | solution.py:27
  247.0 12.9 %collective-permute-start.6 = (f32[2,2,14,2048]{3,2,0,1:T(8,128)}, f32[2,2,14,2048]{3,2,0,1:T(8,128)}, u32[]{:S(2)}, u32[]{:S(2)}) collective-permute-start(f32[2,2,14,2048]{3,2,0,1:T(8,128)} %get-tuple-element.946), channel_id=1, source_target_pairs={{0,1},{1,2},{2,3},{3,4},{4,5},{5,6},{6,7},{7,8},{8,9},{9,10},{10,1... | collective-permute-start | bytes 1376264 | tf_op jit(solution)/shard_map/ppermute | solution.py:27
  267.0 12.7 %collective-permute-start.3 = (f32[2,2,14,2048]{3,2,0,1:T(8,128)S(1)}, f32[2,2,14,2048]{3,2,0,1:T(8,128)S(1)}, u32[]{:S(2)}, u32[]{:S(2)}) collective-permute-start(f32[2,2,14,2048]{3,2,0,1:T(8,128)S(1)} %get-tuple-element.1079), channel_id=1, source_target_pairs={{1,0},{2,1},{3,2},{4,3},{5,4},{6,5},{7,6},{8,7},{9,8},{10,9},{11,1... | collective-permute-start | bytes 1376264 | tf_op jit(solution)/shard_map/while/body/eval_jaxpr/ppermute | solution.py:28
  273.1 12.6 %collective-permute-start.4 = (f32[2,2,14,2048]{3,2,0,1:T(8,128)S(1)}, f32[2,2,14,2048]{3,2,0,1:T(8,128)S(1)}, u32[]{:S(2)}, u32[]{:S(2)}) collective-permute-start(f32[2,2,14,2048]{3,2,0,1:T(8,128)S(1)} %get-tuple-element.1080), channel_id=1, source_target_pairs={{0,1},{1,2},{2,3},{3,4},{4,5},{5,6},{6,7},{7,8},{8,9},{9,10},{10,1... | collective-permute-start | bytes 1376264 | tf_op jit(solution)/shard_map/while/body/eval_jaxpr/ppermute | solution.py:27
  286.1 19.2 %collective-permute-start.5 = (f32[2,2,16,2048]{3,2,0,1:T(8,128)S(1)}, f32[2,2,16,2048]{3,2,0,1:T(8,128)S(1)}, u32[]{:S(2)}, u32[]{:S(2)}) collective-permute-start(f32[2,2,16,2048]{3,2,0,1:T(8,128)S(1)} %pad_maximum_fusion.21), channel_id=1, source_target_pairs={{32,0},{64,32},{96,64},{128,96},{160,128},{192,160},{224,192},{33,... | collective-permute-start | bytes 1572872 | tf_op jit(solution)/shard_map/while/body/eval_jaxpr/ppermute | solution.py:36
  321.2 16.2 %collective-permute-start.5 = (f32[2,2,16,2048]{3,2,0,1:T(8,128)S(1)}, f32[2,2,16,2048]{3,2,0,1:T(8,128)S(1)}, u32[]{:S(2)}, u32[]{:S(2)}) collective-permute-start(f32[2,2,16,2048]{3,2,0,1:T(8,128)S(1)} %pad_maximum_fusion.21), channel_id=1, source_target_pairs={{32,0},{64,32},{96,64},{128,96},{160,128},{192,160},{224,192},{33,... | collective-permute-start | bytes 1572872 | tf_op jit(solution)/shard_map/while/body/eval_jaxpr/ppermute | solution.py:36
  340.2 12.6 %collective-permute-start.4 = (f32[2,2,14,2048]{3,2,0,1:T(8,128)S(1)}, f32[2,2,14,2048]{3,2,0,1:T(8,128)S(1)}, u32[]{:S(2)}, u32[]{:S(2)}) collective-permute-start(f32[2,2,14,2048]{3,2,0,1:T(8,128)S(1)} %get-tuple-element.1080), channel_id=1, source_target_pairs={{0,1},{1,2},{2,3},{3,4},{4,5},{5,6},{6,7},{7,8},{8,9},{9,10},{10,1... | collective-permute-start | bytes 1376264 | tf_op jit(solution)/shard_map/while/body/eval_jaxpr/ppermute | solution.py:27
  353.2 15.1 %collective-permute-start.5 = (f32[2,2,16,2048]{3,2,0,1:T(8,128)S(1)}, f32[2,2,16,2048]{3,2,0,1:T(8,128)S(1)}, u32[]{:S(2)}, u32[]{:S(2)}) collective-permute-start(f32[2,2,16,2048]{3,2,0,1:T(8,128)S(1)} %pad_maximum_fusion.21), channel_id=1, source_target_pairs={{32,0},{64,32},{96,64},{128,96},{160,128},{192,160},{224,192},{33,... | collective-permute-start | bytes 1572872 | tf_op jit(solution)/shard_map/while/body/eval_jaxpr/ppermute | solution.py:36
  384.3 16.2 %collective-permute-start.5 = (f32[2,2,16,2048]{3,2,0,1:T(8,128)S(1)}, f32[2,2,16,2048]{3,2,0,1:T(8,128)S(1)}, u32[]{:S(2)}, u32[]{:S(2)}) collective-permute-start(f32[2,2,16,2048]{3,2,0,1:T(8,128)S(1)} %pad_maximum_fusion.21), channel_id=1, source_target_pairs={{32,0},{64,32},{96,64},{128,96},{160,128},{192,160},{224,192},{33,... | collective-permute-start | bytes 1572872 | tf_op jit(solution)/shard_map/while/body/eval_jaxpr/ppermute | solution.py:36
  416.3 15.4 %collective-permute-start.5 = (f32[2,2,16,2048]{3,2,0,1:T(8,128)S(1)}, f32[2,2,16,2048]{3,2,0,1:T(8,128)S(1)}, u32[]{:S(2)}, u32[]{:S(2)}) collective-permute-start(f32[2,2,16,2048]{3,2,0,1:T(8,128)S(1)} %pad_maximum_fusion.21), channel_id=1, source_target_pairs={{32,0},{64,32},{96,64},{128,96},{160,128},{192,160},{224,192},{33,... | collective-permute-start | bytes 1572872 | tf_op jit(solution)/shard_map/while/body/eval_jaxpr/ppermute | solution.py:36
  447.6 15.8 %collective-permute-start.5 = (f32[2,2,16,2048]{3,2,0,1:T(8,128)S(1)}, f32[2,2,16,2048]{3,2,0,1:T(8,128)S(1)}, u32[]{:S(2)}, u32[]{:S(2)}) collective-permute-start(f32[2,2,16,2048]{3,2,0,1:T(8,128)S(1)} %pad_maximum_fusion.21), channel_id=1, source_target_pairs={{32,0},{64,32},{96,64},{128,96},{160,128},{192,160},{224,192},{33,... | collective-permute-start | bytes 1572872 | tf_op jit(solution)/shard_map/while/body/eval_jaxpr/ppermute | solution.py:36
  479.2 63.0 %collective-permute-start.5 = (f32[2,2,16,2048]{3,2,0,1:T(8,128)S(1)}, f32[2,2,16,2048]{3,2,0,1:T(8,128)S(1)}, u32[]{:S(2)}, u32[]{:S(2)}) collective-permute-start(f32[2,2,16,2048]{3,2,0,1:T(8,128)S(1)} %pad_maximum_fusion.21), channel_id=1, source_target_pairs={{32,0},{64,32},{96,64},{128,96},{160,128},{192,160},{224,192},{33,... | collective-permute-start | bytes 1572872 | tf_op jit(solution)/shard_map/while/body/eval_jaxpr/ppermute | solution.py:36
  548.7 12.7 %collective-permute-start.9 = (f32[2,2,14,2048]{3,2,0,1:T(8,128)S(1)}, f32[2,2,14,2048]{3,2,0,1:T(8,128)S(1)}, u32[]{:S(2)}, u32[]{:S(2)}) collective-permute-start(f32[2,2,14,2048]{3,2,0,1:T(8,128)S(1)} %get-tuple-element.945), channel_id=1, source_target_pairs={{1,0},{2,1},{3,2},{4,3},{5,4},{6,5},{7,6},{8,7},{9,8},{10,9},{11,1... | collective-permute-start | bytes 1376264 | tf_op jit(solution)/shard_map/ppermute | solution.py:28
  (78 other events, 726.4 us)
where the time goes:
time: 570 us; the launch traced here: 568 us
  waiting for transfers between devices  346 us (61%)
  starting transfers between devices  154 us (27%)
  other arithmetic  41.2 us (7%)
  matrix products  12.9 us (2%)
  local copies, waits for them, and re-layouts  9.96 us (2%)
    ppermute x14, waiting for transfers between devices, from_behind(): return lax.ppermute(shard, axis, pairs)  196 us
    ppermute x16, waiting for transfers between devices, padded_2(): before = lax.ppermute(last, axis, up)  92.3 us
    ppermute x16, starting transfers between devices, padded_2(): after = lax.ppermute(initial, axis, down)  66.8 us
    ppermute x16, waiting for transfers between devices, padded_2(): after = lax.ppermute(initial, axis, down)  58.4 us
    ppermute x14, starting transfers between devices, from_behind(): return lax.ppermute(shard, axis, pairs)  53.8 us
    ppermute x16, starting transfers between devices, padded_2(): before = lax.ppermute(last, axis, up)  33.6 us
    concatenate x16, other arithmetic, padded_2(): shard = jnp.concatenate([before, shard, after], axis=dim)  15.1 us
  transfers between devices with their start and end apart: 46, of which 46 were waited for; matrix products, arithmetic and copies ran while one was open for 2% of the time, Pallas kernels for 0%

commit v1 on v0

v1 whole, which is shorter than its diff:
```python
import math

import jax
import jax.numpy as jnp
from jax import lax
from jax.sharding import PartitionSpec as P

TILTS = 16
HALF = 10
SHIFT = 4
HALFCOL = 64
COLBLK = 128


PHASE_SCALE = 0.5
CHIRP_ROW = 1.3
CHIRP_COL = 1.7


def halo_rows(shard, axis, width):
    size, length = (lax.axis_size(axis), shard.shape[-2])
    up = [(i, i + 1) for i in range(size - 1)]
    down = [(j, i) for i, j in up]
    last = shard[..., length - width :, :]
    initial = shard[..., :width, :]
    before = lax.ppermute(last, axis, up)
    after = lax.ppermute(initial, axis, down)
    return jnp.concatenate([before, shard, after], axis=-2)


def kernel_values(distance, radius, chirp_rate):
    inside = jnp.abs(distance) <= radius
    phase_arg = chirp_rate / radius * distance * distance
    weight = 1.0 / math.sqrt(2 * radius + 1)
    real_part = jnp.where(inside, jnp.cos(phase_arg) * weight, 0.0)
    imag_part = jnp.where(inside, jnp.sin(phase_arg) * weight, 0.0)
    return (real_part, imag_part)


def row_band(offset, height, margin, conjugate):
    extent = (height, height + 2 * margin)
    target = lax.broadcasted_iota(jnp.int32, extent, 0)
    source = lax.broadcasted_iota(jnp.int32, extent, 1)
    offset_used = -offset if conjugate else offset
    distance = (source - target - margin - offset_used).astype(jnp.float32)
    real_part, imag_part = kernel_values(distance, HALF, CHIRP_ROW)
    return (real_part, -imag_part) if conjugate else (real_part, imag_part)


def column_band(conjugate, block_width):
    extent = (block_width + 2 * HALFCOL, block_width)
    source = lax.broadcasted_iota(jnp.int32, extent, 0)
    target = lax.broadcasted_iota(jnp.int32, extent, 1)
    distance = (source - target - HALFCOL).astype(jnp.float32)
    real_part, imag_part = kernel_values(distance, HALFCOL, CHIRP_COL)
    return (real_part, -imag_part) if conjugate else (real_part, imag_part)


def mix_rows(band, extended):

    def product(matrix, operand):
        return jnp.einsum("ij,jc->ic", matrix, operand, precision=lax.Precision.HIGHEST)

    real_part = product(band[0], extended[0]) - product(band[1], extended[1])
    imag_part = product(band[0], extended[1]) + product(band[1], extended[0])
    return jnp.stack([real_part, imag_part], axis=0)


def mix_columns(band, field):
    _, height, columns = field.shape
    blocks = columns // COLBLK
    padded = jnp.pad(field, ((0, 0), (0, 0), (HALFCOL, COLBLK - HALFCOL)))
    middle = padded[..., :columns].reshape(2, height, blocks, COLBLK)
    beyond = padded[..., COLBLK : columns + COLBLK].reshape(2, height, blocks, COLBLK)
    window = jnp.concatenate([middle, beyond], axis=3)

    def product(operand, matrix):
        return jnp.einsum("rbj,ji->rbi", operand, matrix, precision=lax.Precision.HIGH)

    real_part = product(window[0], band[0]) - product(window[1], band[1])
    imag_part = product(window[1], band[0]) + product(window[0], band[1])
    return jnp.stack([real_part, imag_part], axis=0).reshape(2, height, columns)


def rotate(field, cosine, sine):
    real_part = cosine * field[0] - sine * field[1]
    imag_part = cosine * field[1] + sine * field[0]
    return jnp.stack([real_part, imag_part], axis=0)


def plane_wave(angle, row_start, height, columns, total_rows, total_cols):
    across = angle - TILTS // 2
    along = jnp.mod(3 * angle, TILTS) - TILTS // 2
    row_index = row_start + lax.broadcasted_iota(jnp.int32, (height, columns), 0)
    col_index = lax.broadcasted_iota(jnp.int32, (height, columns), 1)
    period = total_cols * total_rows
    cycles_int = jnp.mod(across * col_index * total_rows + along * row_index * total_cols, period)
    phase_arg = 2.0 * math.pi / period * cycles_int.astype(jnp.float32)
    return jnp.stack([jnp.cos(phase_arg), jnp.sin(phase_arg)], axis=0)


def body(index_volume, angles, offsets, measured):
    sections = lax.axis_size("depth")
    section_no = lax.axis_index("depth")
    height = index_volume.shape[1]
    columns = index_volume.shape[2]
    margin = HALF + SHIFT
    row_start = lax.axis_index("row") * height
    total_rows = height * lax.axis_size("row")
    angle_count = angles.shape[0]
    angle_no = section_no % angle_count
    volume = lax.all_gather(index_volume, "depth", axis=0, tiled=True)
    shifts = lax.all_gather(offsets, "depth", axis=0, tiled=True)
    layers = volume.shape[0]
    intensity = lax.dynamic_index_in_dim(measured, angle_no, 0, keepdims=False).astype(jnp.float32)
    angle = lax.dynamic_index_in_dim(angles, angle_no, 0, keepdims=False)
    field = plane_wave(angle, row_start, height, columns, total_rows, columns)
    col_fwd = column_band(False, COLBLK)
    col_adj = column_band(True, COLBLK)

    phases = PHASE_SCALE * volume.astype(jnp.float32)
    cosines = jnp.cos(phases)
    sines = jnp.sin(phases)
    def forward_step(layer_no, carried):
        field, stored = carried
        transmitted = rotate(field, cosines[layer_no], sines[layer_no])
        stored = lax.dynamic_update_index_in_dim(stored, transmitted, layer_no, 0)
        extended = halo_rows(transmitted, "row", margin)
        band = row_band(shifts[layer_no], height, margin, False)
        return (mix_columns(col_fwd, mix_rows(band, extended)), stored)

    stored = jnp.zeros((layers,) + field.shape, jnp.float32)
    field, stored = lax.fori_loop(0, layers, forward_step, (field, stored))
    errors = field[0] * field[0] + field[1] * field[1] - intensity
    adjoint = 2.0 * errors[None] * field

    def backward_step(step, carried):
        adjoint, terms = carried
        layer_no = layers - 1 - step
        returned = mix_columns(col_adj, adjoint)
        extended = halo_rows(returned, "row", margin)
        band = row_band(shifts[layer_no], height, margin, True)
        returned = mix_rows(band, extended)
        transmitted = stored[layer_no]
        term = PHASE_SCALE * (transmitted[0] * returned[1] - transmitted[1] * returned[0])
        terms = lax.dynamic_update_index_in_dim(terms, term, layer_no, 0)
        return (rotate(returned, cosines[layer_no], -sines[layer_no]), terms)

    terms = jnp.zeros((layers, height, columns), jnp.float32)
    adjoint, terms = lax.fori_loop(0, layers, backward_step, (adjoint, terms))
    own = lax.dynamic_index_in_dim(terms, section_no, 0, keepdims=True)
    partner_slice = section_no ^ 1
    for_partner = lax.dynamic_index_in_dim(terms, partner_slice, 0, keepdims=True)
    pairs = [(i, i ^ 1) for i in range(sections)]
    received = lax.ppermute(for_partner, "depth", pairs)
    first = jnp.where(angle_no == 0, own, received)
    second = jnp.where(angle_no == 0, received, own)
    return first + second


def solution(mesh):
    in_specs = (P("depth", "row", None), P(), P("depth"), P(None, "row", None))
    out_specs = P("depth", "row", None)
    return jax.shard_map(body, mesh=mesh, in_specs=in_specs, out_specs=out_specs, check_vma=False)
```

time: 570 us -> 370 us (0.65)
  waiting for transfers between devices: 346 us -> 105 us
  matrix products: 12.9 us -> 100 us
  starting transfers between devices: 154 us -> 69.3 us
  blocking collectives: 0 us -> 47.8 us
  other arithmetic: 41.2 us -> 15.5 us
  local copies, waits for them, and re-layouts: 9.96 us -> 20.5 us
    ppermute x46 -> x33, waiting for transfers between devices: 346 us -> 105 us  [the longest x16 97.9 us: halo_rows(): before = lax.ppermute(last, axis, up)]
    dot_general x16 -> x128, matrix products: 12.9 us -> 100 us  [the longest x64 53.2 us: product(): jnp.einsum('ij,jc->ic', matrix, operand, precision=lax.Precision.HIGHEST)]
    ppermute x46 -> x33, starting transfers between devices: 154 us -> 69.3 us  [the longest x16 38.5 us: halo_rows(): before = lax.ppermute(last, axis, up)]
    all_gather x0 -> x1, blocking collectives: none -> 35.1 us  [body(): volume = lax.all_gather(index_volume, 'depth', axis=0, tiled=True)]
    concatenate x16, other arithmetic: 15.1 us -> 1.33 us  [halo_rows(): return jnp.concatenate([before, shard, after], axis=-2)]
    unnamed x0 -> x1, blocking collectives: none -> 12.8 us
    dynamic_slice x0 -> x18, local copies, waits for them, and re-layouts: none -> 11.9 us  [the longest x8 5.13 us: backward_step(): band = row_band(shifts[layer_no], height, margin, True)]
    cos x15 -> x1, other arithmetic: 7.76 us -> 0.59 us  [plane_wave(): return jnp.stack([jnp.cos(phase_arg), jnp.sin(phase_arg)], axis=0)]
  transfers between devices with their start and end apart: 46 -> 33, of which waited for: 46 -> 33; matrix products, arithmetic and copies ran while one was open for 2% -> 4% of each run, Pallas kernels for 0% -> 0%
where the time goes in v1:
time: 370 us; the launch traced here: 369 us
  waiting for transfers between devices  105 us (28%)
  matrix products  100 us (27%)
  starting transfers between devices  69.3 us (19%)
  blocking collectives  47.8 us (13%)
  local copies, waits for them, and re-layouts  20.5 us (6%)
  other arithmetic  15.5 us (4%)
  loops' own time  7.87 us (2%)
    ppermute x16, waiting for transfers between devices, halo_rows(): before = lax.ppermute(last, axis, up)  97.9 us
    dot_general x64, matrix products, product(): jnp.einsum('ij,jc->ic', matrix, operand, precision=lax.Precision.HIGHEST)  53.2 us
    dot_general x64, matrix products, product(): jnp.einsum('rbj,ji->rbi', operand, matrix, precision=lax.Precision.HIGH)  47.2 us
    ppermute x16, starting transfers between devices, halo_rows(): before = lax.ppermute(last, axis, up)  38.5 us
    all_gather x1, blocking collectives, body(): volume = lax.all_gather(index_volume, 'depth', axis=0, tiled=True)  35.1 us
    ppermute x16, starting transfers between devices, halo_rows(): after = lax.ppermute(initial, axis, down)  30.7 us
    unnamed x1, blocking collectives  12.8 us
  transfers between devices with their start and end apart: 33, of which 33 were waited for; matrix products, arithmetic and copies ran while one was open for 4% of the time, Pallas kernels for 0%

profile of v1, /device:TPU:2, one launch (start us, length us, event | category | flops | bytes accessed | tf_op | source)
XLA Modules:
  0.0 368.7 jit_solution(4456685893062569715)
XLA Ops:
  5.0 12.8 %all-reduce.2 = s32[8]{0:T(128)S(1)} all-reduce(s32[8]{0:T(128)S(1)} %dynamic-update-slice), channel_id=1, replica_groups=mesh['depth'=8,'row'=32] {'depth'}, use_global_device_ids=true, to_apply=%add.2 | all-reduce | flops 8 | bytes 64
  17.7 35.1 %all_gather.7 = bf16[8,16,2048]{2,1,0:T(8,128)(2,1)S(1)} all-gather(bf16[1,16,2048]{2,1,0:T(8,128)(2,1)} %param.8), channel_id=1, replica_groups=mesh['depth'=8,'row'=32] {'depth'}, dimensions={0}, use_global_device_ids=true | all-gather | bytes 589824 | tf_op jit(solution)/shard_map/all_gather | solution.py:112
  52.8 3.7 %fusion.193 = (f32[8,16,2048]{2,1,0:T(8,128)S(1)}, f32[8,16,2048]{2,1,0:T(8,128)S(1)}) fusion(bf16[8,16,2048]{2,1,0:T(8,128)(2,1)S(1)} %all_gather.7), kind=kLoop, calls=%fused_computation.255 | loop fusion | flops 524288 | bytes 2621440 | tf_op jit(solution)/shard_map/sin | solution.py:123
  57.2 155.0 %while.38 = (s32[]{:T(128)}, f32[2,16,2048]{2,1,0:T(8,128)S(1)}, f32[8,2,16,2048]{3,2,1,0:T(8,128)}, s32[8]{0:T(128)S(1)}, f32[8,16,2048]{2,1,0:T(8,128)S(1)}, /*index=5*/f32[8,16,2048]{2,1,0:T(8,128)S(1)}, s32[]{:T(128)}) while((s32[]{:T(128)}, f32[2,16,2048]{2,1,0:T(8,128)S(1)}, f32[8,2,16,2048]{3,2,1,0:T(8,128)}, ...), condition=%wide.region_1.2_spmd.clone.clone, body=%wide.region_0.1_spmd.clone.clone.sunk | while | flops 273272320 | bytes 14237897 | solution.py:133
  59.2 2.4 collective-permute-start.1
  63.1 8.9 %collective-permute-done.1 = f32[2,14,2048]{2,1,0:T(8,128)S(1)} collective-permute-done((f32[2,14,2048]{2,1,0:T(8,128)S(1)}, f32[2,14,2048]{2,1,0:T(8,128)S(1)}, u32[]{:S(2)}, u32[]{:S(2)}) %collective-permute-start.1) | collective-permute-done | bytes 229408 | tf_op jit(solution)/shard_map/while/body/eval_jaxpr/ppermute | solution.py:26
  81.2 2.4 collective-permute-start.1
  85.1 5.9 %collective-permute-done.1 = f32[2,14,2048]{2,1,0:T(8,128)S(1)} collective-permute-done((f32[2,14,2048]{2,1,0:T(8,128)S(1)}, f32[2,14,2048]{2,1,0:T(8,128)S(1)}, u32[]{:S(2)}, u32[]{:S(2)}) %collective-permute-start.1) | collective-permute-done | bytes 229408 | tf_op jit(solution)/shard_map/while/body/eval_jaxpr/ppermute | solution.py:26
  104.1 5.9 %collective-permute-done.1 = f32[2,14,2048]{2,1,0:T(8,128)S(1)} collective-permute-done((f32[2,14,2048]{2,1,0:T(8,128)S(1)}, f32[2,14,2048]{2,1,0:T(8,128)S(1)}, u32[]{:S(2)}, u32[]{:S(2)}) %collective-permute-start.1) | collective-permute-done | bytes 229408 | tf_op jit(solution)/shard_map/while/body/eval_jaxpr/ppermute | solution.py:26
  123.1 5.9 %collective-permute-done.1 = f32[2,14,2048]{2,1,0:T(8,128)S(1)} collective-permute-done((f32[2,14,2048]{2,1,0:T(8,128)S(1)}, f32[2,14,2048]{2,1,0:T(8,128)S(1)}, u32[]{:S(2)}, u32[]{:S(2)}) %collective-permute-start.1) | collective-permute-done | bytes 229408 | tf_op jit(solution)/shard_map/while/body/eval_jaxpr/ppermute | solution.py:26
  142.1 5.9 %collective-permute-done.1 = f32[2,14,2048]{2,1,0:T(8,128)S(1)} collective-permute-done((f32[2,14,2048]{2,1,0:T(8,128)S(1)}, f32[2,14,2048]{2,1,0:T(8,128)S(1)}, u32[]{:S(2)}, u32[]{:S(2)}) %collective-permute-start.1) | collective-permute-done | bytes 229408 | tf_op jit(solution)/shard_map/while/body/eval_jaxpr/ppermute | solution.py:26
  161.1 5.9 %collective-permute-done.1 = f32[2,14,2048]{2,1,0:T(8,128)S(1)} collective-permute-done((f32[2,14,2048]{2,1,0:T(8,128)S(1)}, f32[2,14,2048]{2,1,0:T(8,128)S(1)}, u32[]{:S(2)}, u32[]{:S(2)}) %collective-permute-start.1) | collective-permute-done | bytes 229408 | tf_op jit(solution)/shard_map/while/body/eval_jaxpr/ppermute | solution.py:26
  180.1 5.9 %collective-permute-done.1 = f32[2,14,2048]{2,1,0:T(8,128)S(1)} collective-permute-done((f32[2,14,2048]{2,1,0:T(8,128)S(1)}, f32[2,14,2048]{2,1,0:T(8,128)S(1)}, u32[]{:S(2)}, u32[]{:S(2)}) %collective-permute-start.1) | collective-permute-done | bytes 229408 | tf_op jit(solution)/shard_map/while/body/eval_jaxpr/ppermute | solution.py:26
  199.1 5.9 %collective-permute-done.1 = f32[2,14,2048]{2,1,0:T(8,128)S(1)} collective-permute-done((f32[2,14,2048]{2,1,0:T(8,128)S(1)}, f32[2,14,2048]{2,1,0:T(8,128)S(1)}, u32[]{:S(2)}, u32[]{:S(2)}) %collective-permute-start.1) | collective-permute-done | bytes 229408 | tf_op jit(solution)/shard_map/while/body/eval_jaxpr/ppermute | solution.py:26
  213.3 147.8 %while.39 = (s32[]{:T(128)}, f32[2,16,2048]{2,1,0:T(8,128)S(1)}, f32[8,16,2048]{2,1,0:T(8,128)}, f32[8,16,2048]{2,1,0:T(8,128)S(1)}, s32[8]{0:T(128)S(1)}, /*ind...) while((s32[]{:T(128)}, f32[2,16,2048]{2,1,0:T(8,128)S(1)}, ...), condition=%wide.region_3.4_spmd.clone.clone, body=%wide.region_2.3_spmd.clone.clone.sunk | while | flops 272724864 | bytes 14156587 | solution.py:150
  222.6 5.9 %collective-permute-done.3 = f32[2,14,2048]{2,1,0:T(8,128)S(1)} collective-permute-done((f32[2,14,2048]{2,1,0:T(8,128)S(1)}, f32[2,14,2048]{2,1,0:T(8,128)S(1)}, u32[]{:S(2)}, u32[]{:S(2)}) %collective-permute-start.3) | collective-permute-done | bytes 229408 | tf_op jit(solution)/shard_map/while/body/eval_jaxpr/ppermute | solution.py:26
  241.1 5.9 %collective-permute-done.3 = f32[2,14,2048]{2,1,0:T(8,128)S(1)} collective-permute-done((f32[2,14,2048]{2,1,0:T(8,128)S(1)}, f32[2,14,2048]{2,1,0:T(8,128)S(1)}, u32[]{:S(2)}, u32[]{:S(2)}) %collective-permute-start.3) | collective-permute-done | bytes 229408 | tf_op jit(solution)/shard_map/while/body/eval_jaxpr/ppermute | solution.py:26
  259.6 5.9 %collective-permute-done.3 = f32[2,14,2048]{2,1,0:T(8,128)S(1)} collective-permute-done((f32[2,14,2048]{2,1,0:T(8,128)S(1)}, f32[2,14,2048]{2,1,0:T(8,128)S(1)}, u32[]{:S(2)}, u32[]{:S(2)}) %collective-permute-start.3) | collective-permute-done | bytes 229408 | tf_op jit(solution)/shard_map/while/body/eval_jaxpr/ppermute | solution.py:26
  278.1 5.9 %collective-permute-done.3 = f32[2,14,2048]{2,1,0:T(8,128)S(1)} collective-permute-done((f32[2,14,2048]{2,1,0:T(8,128)S(1)}, f32[2,14,2048]{2,1,0:T(8,128)S(1)}, u32[]{:S(2)}, u32[]{:S(2)}) %collective-permute-start.3) | collective-permute-done | bytes 229408 | tf_op jit(solution)/shard_map/while/body/eval_jaxpr/ppermute | solution.py:26
  296.5 5.9 %collective-permute-done.3 = f32[2,14,2048]{2,1,0:T(8,128)S(1)} collective-permute-done((f32[2,14,2048]{2,1,0:T(8,128)S(1)}, f32[2,14,2048]{2,1,0:T(8,128)S(1)}, u32[]{:S(2)}, u32[]{:S(2)}) %collective-permute-start.3) | collective-permute-done | bytes 229408 | tf_op jit(solution)/shard_map/while/body/eval_jaxpr/ppermute | solution.py:26
  315.0 5.9 %collective-permute-done.3 = f32[2,14,2048]{2,1,0:T(8,128)S(1)} collective-permute-done((f32[2,14,2048]{2,1,0:T(8,128)S(1)}, f32[2,14,2048]{2,1,0:T(8,128)S(1)}, u32[]{:S(2)}, u32[]{:S(2)}) %collective-permute-start.3) | collective-permute-done | bytes 229408 | tf_op jit(solution)/shard_map/while/body/eval_jaxpr/ppermute | solution.py:26
  333.5 5.9 %collective-permute-done.3 = f32[2,14,2048]{2,1,0:T(8,128)S(1)} collective-permute-done((f32[2,14,2048]{2,1,0:T(8,128)S(1)}, f32[2,14,2048]{2,1,0:T(8,128)S(1)}, u32[]{:S(2)}, u32[]{:S(2)}) %collective-permute-start.3) | collective-permute-done | bytes 229408 | tf_op jit(solution)/shard_map/while/body/eval_jaxpr/ppermute | solution.py:26
  352.0 5.9 %collective-permute-done.3 = f32[2,14,2048]{2,1,0:T(8,128)S(1)} collective-permute-done((f32[2,14,2048]{2,1,0:T(8,128)S(1)}, f32[2,14,2048]{2,1,0:T(8,128)S(1)}, u32[]{:S(2)}, u32[]{:S(2)}) %collective-permute-start.3) | collective-permute-done | bytes 229408 | tf_op jit(solution)/shard_map/while/body/eval_jaxpr/ppermute | solution.py:26
  362.1 4.9 %collective-permute-done.4 = f32[1,16,2048]{2,1,0:T(8,128)S(1)} collective-permute-done((f32[1,16,2048]{2,1,0:T(8,128)S(1)}, f32[1,16,2048]{2,1,0:T(8,128)S(1)}, u32[]{:S(2)}, u32[]{:S(2)}) %collective-permute-start.4) | collective-permute-done | bytes 131104 | tf_op jit(solution)/shard_map/ppermute | solution.py:155
  (415 shorter events, 199.7 us)
Async XLA Ops:
  57.3 5.8 %collective-permute-start = (f32[2,14,2048]{2,1,0:T(8,128)S(1)}, f32[2,14,2048]{2,1,0:T(8,128)S(1)}, u32[]{:S(2)}, u32[]{:S(2)}) collective-permute-start(f32[2,14,2048]{2,1,0:T(8,128)S(1)} %get-tuple-element.655), channel_id=1, source_target_pairs={{1,0},{2,1},{3,2},{4,3},{5,4},{6,5},{7,6},{8,7},{9,8},{10,9},{11,1... | collective-permute-start | bytes 688136 | tf_op jit(solution)/shard_map/while/body/eval_jaxpr/ppermute | solution.py:27
  59.2 12.8 %collective-permute-start.1 = (f32[2,14,2048]{2,1,0:T(8,128)S(1)}, f32[2,14,2048]{2,1,0:T(8,128)S(1)}, u32[]{:S(2)}, u32[]{:S(2)}) collective-permute-start(f32[2,14,2048]{2,1,0:T(8,128)S(1)} %get-tuple-element.656), channel_id=1, source_target_pairs={{0,1},{1,2},{2,3},{3,4},{4,5},{5,6},{6,7},{7,8},{8,9},{9,10},{10,1... | collective-permute-start | bytes 688136 | tf_op jit(solution)/shard_map/while/body/eval_jaxpr/ppermute | solution.py:26
  79.3 5.8 %collective-permute-start = (f32[2,14,2048]{2,1,0:T(8,128)S(1)}, f32[2,14,2048]{2,1,0:T(8,128)S(1)}, u32[]{:S(2)}, u32[]{:S(2)}) collective-permute-start(f32[2,14,2048]{2,1,0:T(8,128)S(1)} %get-tuple-element.655), channel_id=1, source_target_pairs={{1,0},{2,1},{3,2},{4,3},{5,4},{6,5},{7,6},{8,7},{9,8},{10,9},{11,1... | collective-permute-start | bytes 688136 | tf_op jit(solution)/shard_map/while/body/eval_jaxpr/ppermute | solution.py:27
  81.2 9.8 %collective-permute-start.1 = (f32[2,14,2048]{2,1,0:T(8,128)S(1)}, f32[2,14,2048]{2,1,0:T(8,128)S(1)}, u32[]{:S(2)}, u32[]{:S(2)}) collective-permute-start(f32[2,14,2048]{2,1,0:T(8,128)S(1)} %get-tuple-element.656), channel_id=1, source_target_pairs={{0,1},{1,2},{2,3},{3,4},{4,5},{5,6},{6,7},{7,8},{8,9},{9,10},{10,1... | collective-permute-start | bytes 688136 | tf_op jit(solution)/shard_map/while/body/eval_jaxpr/ppermute | solution.py:26
  98.3 5.8 %collective-permute-start = (f32[2,14,2048]{2,1,0:T(8,128)S(1)}, f32[2,14,2048]{2,1,0:T(8,128)S(1)}, u32[]{:S(2)}, u32[]{:S(2)}) collective-permute-start(f32[2,14,2048]{2,1,0:T(8,128)S(1)} %get-tuple-element.655), channel_id=1, source_target_pairs={{1,0},{2,1},{3,2},{4,3},{5,4},{6,5},{7,6},{8,7},{9,8},{10,9},{11,1... | collective-permute-start | bytes 688136 | tf_op jit(solution)/shard_map/while/body/eval_jaxpr/ppermute | solution.py:27
  100.2 9.8 %collective-permute-start.1 = (f32[2,14,2048]{2,1,0:T(8,128)S(1)}, f32[2,14,2048]{2,1,0:T(8,128)S(1)}, u32[]{:S(2)}, u32[]{:S(2)}) collective-permute-start(f32[2,14,2048]{2,1,0:T(8,128)S(1)} %get-tuple-element.656), channel_id=1, source_target_pairs={{0,1},{1,2},{2,3},{3,4},{4,5},{5,6},{6,7},{7,8},{8,9},{9,10},{10,1... | collective-permute-start | bytes 688136 | tf_op jit(solution)/shard_map/while/body/eval_jaxpr/ppermute | solution.py:26
  117.3 5.8 %collective-permute-start = (f32[2,14,2048]{2,1,0:T(8,128)S(1)}, f32[2,14,2048]{2,1,0:T(8,128)S(1)}, u32[]{:S(2)}, u32[]{:S(2)}) collective-permute-start(f32[2,14,2048]{2,1,0:T(8,128)S(1)} %get-tuple-element.655), channel_id=1, source_target_pairs={{1,0},{2,1},{3,2},{4,3},{5,4},{6,5},{7,6},{8,7},{9,8},{10,9},{11,1... | collective-permute-start | bytes 688136 | tf_op jit(solution)/shard_map/while/body/eval_jaxpr/ppermute | solution.py:27
  119.2 9.8 %collective-permute-start.1 = (f32[2,14,2048]{2,1,0:T(8,128)S(1)}, f32[2,14,2048]{2,1,0:T(8,128)S(1)}, u32[]{:S(2)}, u32[]{:S(2)}) collective-permute-start(f32[2,14,2048]{2,1,0:T(8,128)S(1)} %get-tuple-element.656), channel_id=1, source_target_pairs={{0,1},{1,2},{2,3},{3,4},{4,5},{5,6},{6,7},{7,8},{8,9},{9,10},{10,1... | collective-permute-start | bytes 688136 | tf_op jit(solution)/shard_map/while/body/eval_jaxpr/ppermute | solution.py:26
  136.3 5.8 %collective-permute-start = (f32[2,14,2048]{2,1,0:T(8,128)S(1)}, f32[2,14,2048]{2,1,0:T(8,128)S(1)}, u32[]{:S(2)}, u32[]{:S(2)}) collective-permute-start(f32[2,14,2048]{2,1,0:T(8,128)S(1)} %get-tuple-element.655), channel_id=1, source_target_pairs={{1,0},{2,1},{3,2},{4,3},{5,4},{6,5},{7,6},{8,7},{9,8},{10,9},{11,1... | collective-permute-start | bytes 688136 | tf_op jit(solution)/shard_map/while/body/eval_jaxpr/ppermute | solution.py:27
  138.2 9.8 %collective-permute-start.1 = (f32[2,14,2048]{2,1,0:T(8,128)S(1)}, f32[2,14,2048]{2,1,0:T(8,128)S(1)}, u32[]{:S(2)}, u32[]{:S(2)}) collective-permute-start(f32[2,14,2048]{2,1,0:T(8,128)S(1)} %get-tuple-element.656), channel_id=1, source_target_pairs={{0,1},{1,2},{2,3},{3,4},{4,5},{5,6},{6,7},{7,8},{8,9},{9,10},{10,1... | collective-permute-start | bytes 688136 | tf_op jit(solution)/shard_map/while/body/eval_jaxpr/ppermute | solution.py:26
  155.3 5.8 %collective-permute-start = (f32[2,14,2048]{2,1,0:T(8,128)S(1)}, f32[2,14,2048]{2,1,0:T(8,128)S(1)}, u32[]{:S(2)}, u32[]{:S(2)}) collective-permute-start(f32[2,14,2048]{2,1,0:T(8,128)S(1)} %get-tuple-element.655), channel_id=1, source_target_pairs={{1,0},{2,1},{3,2},{4,3},{5,4},{6,5},{7,6},{8,7},{9,8},{10,9},{11,1... | collective-permute-start | bytes 688136 | tf_op jit(solution)/shard_map/while/body/eval_jaxpr/ppermute | solution.py:27
  157.2 9.8 %collective-permute-start.1 = (f32[2,14,2048]{2,1,0:T(8,128)S(1)}, f32[2,14,2048]{2,1,0:T(8,128)S(1)}, u32[]{:S(2)}, u32[]{:S(2)}) collective-permute-start(f32[2,14,2048]{2,1,0:T(8,128)S(1)} %get-tuple-element.656), channel_id=1, source_target_pairs={{0,1},{1,2},{2,3},{3,4},{4,5},{5,6},{6,7},{7,8},{8,9},{9,10},{10,1... | collective-permute-start | bytes 688136 | tf_op jit(solution)/shard_map/while/body/eval_jaxpr/ppermute | solution.py:26
  174.3 5.8 %collective-permute-start = (f32[2,14,2048]{2,1,0:T(8,128)S(1)}, f32[2,14,2048]{2,1,0:T(8,128)S(1)}, u32[]{:S(2)}, u32[]{:S(2)}) collective-permute-start(f32[2,14,2048]{2,1,0:T(8,128)S(1)} %get-tuple-element.655), channel_id=1, source_target_pairs={{1,0},{2,1},{3,2},{4,3},{5,4},{6,5},{7,6},{8,7},{9,8},{10,9},{11,1... | collective-permute-start | bytes 688136 | tf_op jit(solution)/shard_map/while/body/eval_jaxpr/ppermute | solution.py:27
  176.2 9.8 %collective-permute-start.1 = (f32[2,14,2048]{2,1,0:T(8,128)S(1)}, f32[2,14,2048]{2,1,0:T(8,128)S(1)}, u32[]{:S(2)}, u32[]{:S(2)}) collective-permute-start(f32[2,14,2048]{2,1,0:T(8,128)S(1)} %get-tuple-element.656), channel_id=1, source_target_pairs={{0,1},{1,2},{2,3},{3,4},{4,5},{5,6},{6,7},{7,8},{8,9},{9,10},{10,1... | collective-permute-start | bytes 688136 | tf_op jit(solution)/shard_map/while/body/eval_jaxpr/ppermute | solution.py:26
  195.2 9.8 %collective-permute-start.1 = (f32[2,14,2048]{2,1,0:T(8,128)S(1)}, f32[2,14,2048]{2,1,0:T(8,128)S(1)}, u32[]{:S(2)}, u32[]{:S(2)}) collective-permute-start(f32[2,14,2048]{2,1,0:T(8,128)S(1)} %get-tuple-element.656), channel_id=1, source_target_pairs={{0,1},{1,2},{2,3},{3,4},{4,5},{5,6},{6,7},{7,8},{8,9},{9,10},{10,1... | collective-permute-start | bytes 688136 | tf_op jit(solution)/shard_map/while/body/eval_jaxpr/ppermute | solution.py:26
  218.8 9.8 %collective-permute-start.3 = (f32[2,14,2048]{2,1,0:T(8,128)S(1)}, f32[2,14,2048]{2,1,0:T(8,128)S(1)}, u32[]{:S(2)}, u32[]{:S(2)}) collective-permute-start(f32[2,14,2048]{2,1,0:T(8,128)S(1)} %get-tuple-element.669), channel_id=1, source_target_pairs={{0,1},{1,2},{2,3},{3,4},{4,5},{5,6},{6,7},{7,8},{8,9},{9,10},{10,1... | collective-permute-start | bytes 688136 | tf_op jit(solution)/shard_map/while/body/eval_jaxpr/ppermute | solution.py:26
  237.2 9.8 %collective-permute-start.3 = (f32[2,14,2048]{2,1,0:T(8,128)S(1)}, f32[2,14,2048]{2,1,0:T(8,128)S(1)}, u32[]{:S(2)}, u32[]{:S(2)}) collective-permute-start(f32[2,14,2048]{2,1,0:T(8,128)S(1)} %get-tuple-element.669), channel_id=1, source_target_pairs={{0,1},{1,2},{2,3},{3,4},{4,5},{5,6},{6,7},{7,8},{8,9},{9,10},{10,1... | collective-permute-start | bytes 688136 | tf_op jit(solution)/shard_map/while/body/eval_jaxpr/ppermute | solution.py:26
  253.8 5.8 %collective-permute-start.2 = (f32[2,14,2048]{2,1,0:T(8,128)S(1)}, f32[2,14,2048]{2,1,0:T(8,128)S(1)}, u32[]{:S(2)}, u32[]{:S(2)}) collective-permute-start(f32[2,14,2048]{2,1,0:T(8,128)S(1)} %get-tuple-element.668), channel_id=1, source_target_pairs={{1,0},{2,1},{3,2},{4,3},{5,4},{6,5},{7,6},{8,7},{9,8},{10,9},{11,1... | collective-permute-start | bytes 688136 | tf_op jit(solution)/shard_map/while/body/eval_jaxpr/ppermute | solution.py:27
  255.7 9.8 %collective-permute-start.3 = (f32[2,14,2048]{2,1,0:T(8,128)S(1)}, f32[2,14,2048]{2,1,0:T(8,128)S(1)}, u32[]{:S(2)}, u32[]{:S(2)}) collective-permute-start(f32[2,14,2048]{2,1,0:T(8,128)S(1)} %get-tuple-element.669), channel_id=1, source_target_pairs={{0,1},{1,2},{2,3},{3,4},{4,5},{5,6},{6,7},{7,8},{8,9},{9,10},{10,1... | collective-permute-start | bytes 688136 | tf_op jit(solution)/shard_map/while/body/eval_jaxpr/ppermute | solution.py:26
  274.2 9.8 %collective-permute-start.3 = (f32[2,14,2048]{2,1,0:T(8,128)S(1)}, f32[2,14,2048]{2,1,0:T(8,128)S(1)}, u32[]{:S(2)}, u32[]{:S(2)}) collective-permute-start(f32[2,14,2048]{2,1,0:T(8,128)S(1)} %get-tuple-element.669), channel_id=1, source_target_pairs={{0,1},{1,2},{2,3},{3,4},{4,5},{5,6},{6,7},{7,8},{8,9},{9,10},{10,1... | collective-permute-start | bytes 688136 | tf_op jit(solution)/shard_map/while/body/eval_jaxpr/ppermute | solution.py:26
  292.7 9.8 %collective-permute-start.3 = (f32[2,14,2048]{2,1,0:T(8,128)S(1)}, f32[2,14,2048]{2,1,0:T(8,128)S(1)}, u32[]{:S(2)}, u32[]{:S(2)}) collective-permute-start(f32[2,14,2048]{2,1,0:T(8,128)S(1)} %get-tuple-element.669), channel_id=1, source_target_pairs={{0,1},{1,2},{2,3},{3,4},{4,5},{5,6},{6,7},{7,8},{8,9},{9,10},{10,1... | collective-permute-start | bytes 688136 | tf_op jit(solution)/shard_map/while/body/eval_jaxpr/ppermute | solution.py:26
  311.2 9.8 %collective-permute-start.3 = (f32[2,14,2048]{2,1,0:T(8,128)S(1)}, f32[2,14,2048]{2,1,0:T(8,128)S(1)}, u32[]{:S(2)}, u32[]{:S(2)}) collective-permute-start(f32[2,14,2048]{2,1,0:T(8,128)S(1)} %get-tuple-element.669), channel_id=1, source_target_pairs={{0,1},{1,2},{2,3},{3,4},{4,5},{5,6},{6,7},{7,8},{8,9},{9,10},{10,1... | collective-permute-start | bytes 688136 | tf_op jit(solution)/shard_map/while/body/eval_jaxpr/ppermute | solution.py:26
  329.6 9.8 %collective-permute-start.3 = (f32[2,14,2048]{2,1,0:T(8,128)S(1)}, f32[2,14,2048]{2,1,0:T(8,128)S(1)}, u32[]{:S(2)}, u32[]{:S(2)}) collective-permute-start(f32[2,14,2048]{2,1,0:T(8,128)S(1)} %get-tuple-element.669), channel_id=1, source_target_pairs={{0,1},{1,2},{2,3},{3,4},{4,5},{5,6},{6,7},{7,8},{8,9},{9,10},{10,1... | collective-permute-start | bytes 688136 | tf_op jit(solution)/shard_map/while/body/eval_jaxpr/ppermute | solution.py:26
  348.1 9.8 %collective-permute-start.3 = (f32[2,14,2048]{2,1,0:T(8,128)S(1)}, f32[2,14,2048]{2,1,0:T(8,128)S(1)}, u32[]{:S(2)}, u32[]{:S(2)}) collective-permute-start(f32[2,14,2048]{2,1,0:T(8,128)S(1)} %get-tuple-element.669), channel_id=1, source_target_pairs={{0,1},{1,2},{2,3},{3,4},{4,5},{5,6},{6,7},{7,8},{8,9},{9,10},{10,1... | collective-permute-start | bytes 688136 | tf_op jit(solution)/shard_map/while/body/eval_jaxpr/ppermute | solution.py:26
  (10 other events, 206.4 us)

commit v2 on v1

v2 whole, which is shorter than its diff:
```python
import functools
import math

import jax
import jax.numpy as jnp
from jax import lax
from jax.experimental import pallas as pl
from jax.experimental.pallas import tpu as pltpu
from jax.sharding import PartitionSpec as P

TILTS = 16
HALF = 10
SHIFT = 4
HALFCOL = 64
LANE = 128

PHASE_SCALE = 0.5
CHIRP_ROW = 1.3
CHIRP_COL = 1.7
MESH = pl.DeviceIdType.MESH


def kernel_values(distance, radius, chirp_rate):
    inside = jnp.abs(distance) <= radius
    phase_arg = chirp_rate / radius * distance * distance
    weight = 1.0 / math.sqrt(2 * radius + 1)
    real_part = jnp.where(inside, jnp.cos(phase_arg) * weight, 0.0)
    imag_part = jnp.where(inside, jnp.sin(phase_arg) * weight, 0.0)
    return (real_part, imag_part)


def split_bf16(x):
    high = x.astype(jnp.bfloat16)
    low = (x - high.astype(jnp.float32)).astype(jnp.bfloat16)
    return high, low


def complex_block(real_part, imag_part):
    top = jnp.concatenate([real_part, -imag_part], axis=-1)
    bottom = jnp.concatenate([imag_part, real_part], axis=-1)
    return jnp.concatenate([top, bottom], axis=-2)


def row_bands(shifts, height):
    layers = shifts.shape[0]
    signs = jnp.concatenate([jnp.ones((layers,), jnp.int32), -jnp.ones((layers,), jnp.int32)])
    used = jnp.concatenate([shifts, shifts[::-1]]) * signs
    extent = (2 * layers, 3, height, height)
    part = lax.broadcasted_iota(jnp.int32, extent, 1)
    target = lax.broadcasted_iota(jnp.int32, extent, 2)
    source = lax.broadcasted_iota(jnp.int32, extent, 3) + (part - 1) * height
    distance = (source - target - used[:, None, None, None]).astype(jnp.float32)
    real_part, imag_part = kernel_values(distance, HALF, CHIRP_ROW)
    imag_part = imag_part * signs[:, None, None, None].astype(jnp.float32)
    return complex_block(real_part, imag_part)


def column_bands():
    extent = (3, LANE, LANE)
    part = lax.broadcasted_iota(jnp.int32, extent, 0)
    source = lax.broadcasted_iota(jnp.int32, extent, 1) + (part - 1) * LANE
    target = lax.broadcasted_iota(jnp.int32, extent, 2)
    distance = (source - target).astype(jnp.float32)
    real_part, imag_part = kernel_values(distance, HALFCOL, CHIRP_COL)
    forward = jnp.concatenate([real_part, imag_part], axis=-1)
    adjoint = jnp.concatenate([real_part, -imag_part], axis=-1)
    return jnp.stack([forward, adjoint], axis=0)


def dot3(a, x):
    a_high, a_low = split_bf16(a)
    x_high, x_low = split_bf16(x)
    f32 = jnp.float32
    return (
        jnp.dot(a_high, x_high, preferred_element_type=f32)
        + jnp.dot(a_high, x_low, preferred_element_type=f32)
        + jnp.dot(a_low, x_high, preferred_element_type=f32)
    )


def chain_kernel(rows, u0_ref, cos_ref, sin_ref, inten_ref, rband_ref, cband_ref,
                 terms_ref, field_ref, acc_ref, y_store, b_store, before, after, bmh_ref, bml_ref,
                 send_dn, send_up, recv_bf, recv_af):
    me = lax.axis_index("row")
    layers, height, columns = cos_ref.shape
    blocks = columns // LANE
    has_up = me > 0
    has_dn = me < rows - 1

    barrier = pltpu.get_barrier_semaphore()

    @pl.when(has_up)
    def _():
        pl.semaphore_signal(barrier, 1, device_id={"row": me - 1}, device_id_type=MESH)

    @pl.when(has_dn)
    def _():
        pl.semaphore_signal(barrier, 1, device_id={"row": me + 1}, device_id_type=MESH)

    peers = (me + rows - 1) // rows + (2 * rows - 2 - me) // rows
    pl.semaphore_wait(barrier, peers)

    zero_block = jnp.zeros((2 * height, LANE), jnp.bfloat16)
    for ref in (bmh_ref, bml_ref):
        ref[0] = zero_block
        ref[blocks + 1] = zero_block

    def copies(k, source):
        down = pltpu.make_async_remote_copy(
            src_ref=source, dst_ref=before.at[k], send_sem=send_dn.at[k], recv_sem=recv_bf.at[k],
            device_id={"row": me + 1}, device_id_type=MESH)
        up = pltpu.make_async_remote_copy(
            src_ref=source, dst_ref=after.at[k], send_sem=send_up.at[k], recv_sem=recv_af.at[k],
            device_id={"row": me - 1}, device_id_type=MESH)
        return down, up

    def start(k, source):
        down, up = copies(k, source)

        @pl.when(has_dn)
        def _():
            down.start()

        @pl.when(has_up)
        def _():
            up.start()

    def finish(k, source):
        down, up = copies(k, source)

        @pl.when(has_dn)
        def _():
            down.wait_send()

        @pl.when(has_up)
        def _():
            up.wait_send()

    def row_mix(k, source, z):
        down, up = copies(k, source)
        acc_ref[...] = dot3(rband_ref[k, 1], z)
        start(k, source)

        @pl.when(has_up)
        def _():
            down.wait_recv()
            acc_ref[...] += dot3(rband_ref[k, 0], before[k])

        @pl.when(has_dn)
        def _():
            up.wait_recv()
            acc_ref[...] += dot3(rband_ref[k, 2], after[k])

        return acc_ref[...]

    def col_mix(v, which):
        high, low = split_bf16(v)
        for b in range(blocks):
            bmh_ref[b + 1] = high[:, b * LANE:(b + 1) * LANE]
            bml_ref[b + 1] = low[:, b * LANE:(b + 1) * LANE]
        total = None
        f32 = jnp.float32
        for t in range(3):
            xh = bmh_ref[t:t + blocks].reshape(blocks * 2 * height, LANE)
            xl = bml_ref[t:t + blocks].reshape(blocks * 2 * height, LANE)
            wh, wl = split_bf16(cband_ref[which, t])
            part = (jnp.dot(xh, wh, preferred_element_type=f32) + jnp.dot(xh, wl, preferred_element_type=f32)
                    + jnp.dot(xl, wh, preferred_element_type=f32))
            total = part if total is None else total + part
        total = total.reshape(blocks, 2 * height, 2 * LANE)
        real_part = total[:, :height, :LANE] - total[:, height:, LANE:]
        imag_part = total[:, :height, LANE:] + total[:, height:, :LANE]
        out = jnp.concatenate([real_part, imag_part], axis=1)
        return jnp.concatenate([out[b] for b in range(blocks)], axis=1)

    field_ref[...] = u0_ref[...]

    def forward(s, carry):
        u = field_ref[...]
        c = cos_ref[s]
        sn = sin_ref[s]
        ur = u[:height]
        ui = u[height:]
        y_store[s] = jnp.concatenate([c * ur - sn * ui, c * ui + sn * ur], axis=0)
        source = y_store.at[s]
        v = row_mix(s, source, y_store[s])
        field_ref[...] = col_mix(v, 0)
        finish(s, source)
        return carry

    lax.fori_loop(0, layers, forward, 0)
    u = field_ref[...]
    ur = u[:height]
    ui = u[height:]
    errors = ur * ur + ui * ui - inten_ref[...]
    field_ref[...] = jnp.concatenate([2.0 * errors * ur, 2.0 * errors * ui], axis=0)

    def backward(j, carry):
        s = layers - 1 - j
        k = layers + j
        b_store[j] = col_mix(field_ref[...], 1)
        source = b_store.at[j]
        acc = row_mix(k, source, b_store[j])
        ar = acc[:height]
        ai = acc[height:]
        y = y_store[s]
        terms_ref[s] = PHASE_SCALE * (y[:height] * ai - y[height:] * ar)
        c = cos_ref[s]
        sn = sin_ref[s]
        field_ref[...] = jnp.concatenate([c * ar + sn * ai, c * ai - sn * ar], axis=0)
        finish(k, source)
        return carry

    lax.fori_loop(0, layers, backward, 0)


def run_chain(u0, cosines, sines, intensity, row_band, col_band, rows):
    layers, height, columns = cosines.shape
    blocks = columns // LANE
    field = (2 * height, columns)
    return pl.pallas_call(
        functools.partial(chain_kernel, rows),
        out_shape=jax.ShapeDtypeStruct((layers, height, columns), jnp.float32),
        in_specs=[pl.BlockSpec(memory_space=pltpu.VMEM)] * 6,
        out_specs=pl.BlockSpec(memory_space=pltpu.VMEM),
        scratch_shapes=[
            pltpu.VMEM(field, jnp.float32),
            pltpu.VMEM(field, jnp.float32),
            pltpu.VMEM((layers,) + field, jnp.float32),
            pltpu.VMEM((layers,) + field, jnp.float32),
            pltpu.VMEM((2 * layers,) + field, jnp.float32),
            pltpu.VMEM((2 * layers,) + field, jnp.float32),
            pltpu.VMEM((blocks + 2, 2 * height, LANE), jnp.bfloat16),
            pltpu.VMEM((blocks + 2, 2 * height, LANE), jnp.bfloat16),
            pltpu.SemaphoreType.DMA((2 * layers,)),
            pltpu.SemaphoreType.DMA((2 * layers,)),
            pltpu.SemaphoreType.DMA((2 * layers,)),
            pltpu.SemaphoreType.DMA((2 * layers,)),
        ],
        compiler_params=pltpu.CompilerParams(
            collective_id=0, has_side_effects=True, vmem_limit_bytes=56 * 1024 * 1024),
    )(u0, cosines, sines, intensity, row_band, col_band)


def plane_wave(angle, row_start, height, columns, total_rows, total_cols):
    across = angle - TILTS // 2
    along = jnp.mod(3 * angle, TILTS) - TILTS // 2
    row_index = row_start + lax.broadcasted_iota(jnp.int32, (height, columns), 0)
    col_index = lax.broadcasted_iota(jnp.int32, (height, columns), 1)
    period = total_cols * total_rows
    cycles_int = jnp.mod(across * col_index * total_rows + along * row_index * total_cols, period)
    phase_arg = 2.0 * math.pi / period * cycles_int.astype(jnp.float32)
    return jnp.concatenate([jnp.cos(phase_arg), jnp.sin(phase_arg)], axis=0)


def body(index_volume, angles, offsets, measured):
    sections = lax.axis_size("depth")
    rows = lax.axis_size("row")
    section_no = lax.axis_index("depth")
    height = index_volume.shape[1]
    columns = index_volume.shape[2]
    row_start = lax.axis_index("row") * height
    total_rows = height * rows
    angle_count = angles.shape[0]
    angle_no = section_no % angle_count
    volume = lax.all_gather(index_volume, "depth", axis=0, tiled=True)
    shifts = lax.all_gather(offsets, "depth", axis=0, tiled=True)
    intensity = lax.dynamic_index_in_dim(measured, angle_no, 0, keepdims=False).astype(jnp.float32)
    angle = lax.dynamic_index_in_dim(angles, angle_no, 0, keepdims=False)
    incident = plane_wave(angle, row_start, height, columns, total_rows, columns)
    phases = PHASE_SCALE * volume.astype(jnp.float32)
    terms = run_chain(incident, jnp.cos(phases), jnp.sin(phases), intensity,
                      row_bands(shifts, height), column_bands(), rows)
    own = lax.dynamic_index_in_dim(terms, section_no, 0, keepdims=True)
    for_partner = lax.dynamic_index_in_dim(terms, section_no ^ 1, 0, keepdims=True)
    pairs = [(i, i ^ 1) for i in range(sections)]
    received = lax.ppermute(for_partner, "depth", pairs)
    first = jnp.where(angle_no == 0, own, received)
    second = jnp.where(angle_no == 0, received, own)
    return first + second


def solution(mesh):
    in_specs = (P("depth", "row", None), P(), P("depth"), P(None, "row", None))
    out_specs = P("depth", "row", None)
    return jax.shard_map(body, mesh=mesh, in_specs=in_specs, out_specs=out_specs, check_vma=False)
```

time: 370 us -> 199 us (0.54)
  Pallas kernels: 0 us -> 126 us
  waiting for transfers between devices: 105 us -> 4.95 us
  matrix products: 100 us -> 0 us
  starting transfers between devices: 69.3 us -> 0.09 us
  local copies, waits for them, and re-layouts: 20.5 us -> 4.37 us
  loops' own time: 7.87 us -> 0 us
    pallas_call x0 -> x1, Pallas kernels: none -> 126 us  [run_chain(): pl.pallas_call(functools.partial(chain_kernel, rows), out_shape=jax.Shape...]
    ppermute x32 -> x0, waiting for transfers between devices: 100 us -> none  [the longest x16 97.9 us: halo_rows(): before = lax.ppermute(last, axis, up)]
    dot_general x128 -> x0, matrix products: 100 us -> none  [the longest x64 53.2 us: product(): jnp.einsum('ij,jc->ic', matrix, operand, precision=lax.Precision.HIGHEST)]
    ppermute x32 -> x0, starting transfers between devices: 69.2 us -> none  [the longest x16 38.5 us: halo_rows(): before = lax.ppermute(last, axis, up)]
    dynamic_slice x17 -> x1, local copies, waits for them, and re-layouts: 10.7 us -> 0.92 us  [body(): lax.dynamic_index_in_dim(terms, section_no ^ 1, 0, keepdims=True)]
    another operation x2 -> x0, loops' own time: 7.87 us -> none  [the longest x1 6.42 us: body(): adjoint, terms = lax.fori_loop(0, layers, backward_step, (adjoint, terms))]
    dynamic_update_slice x8 -> x0, other arithmetic: 5.87 us -> none  [forward_step(): stored = lax.dynamic_update_index_in_dim(stored, transmitted, layer_no, 0)]
  transfers between devices with their start and end apart: 33 -> 1, of which waited for: 33 -> 1; matrix products, arithmetic and copies ran while one was open for 4% -> 0% of each run, Pallas kernels for 0% -> 0%
where the time goes in v2:
time: 199 us
  Pallas kernels  126 us (63%)
  blocking collectives  47.6 us (24%)
  other arithmetic  13.7 us (7%)
  waiting for transfers between devices  4.95 us (2%)
  local copies, waits for them, and re-layouts  4.37 us (2%)
  between operations  2.07 us (1%)
    pallas_call x1, Pallas kernels, run_chain(): pl.pallas_call(functools.partial(chain_kernel, rows), out_shape=jax.Shape...  126 us
    all_gather x1, blocking collectives, body(): volume = lax.all_gather(index_volume, 'depth', axis=0, tiled=True)  34.9 us
    unnamed x1, blocking collectives  12.8 us
    ppermute x1, waiting for transfers between devices, body(): received = lax.ppermute(for_partner, 'depth', pairs)  4.95 us
    sin x1, other arithmetic, body(): jnp.sin(phases)  4.58 us
  transfers between devices with their start and end apart: 1, of which 1 were waited for; matrix products, arithmetic and copies ran while one was open for 0% of the time, Pallas kernels for 0%

profile of v2, /device:TPU:2, one launch (start us, length us, event | category | flops | bytes accessed | tf_op | source)
XLA Modules:
  0.0 198.9 jit_solution(15519481878306089074)
XLA Ops:
  0.0 0.7 copy-done.3
  0.7 0.6 dynamic_slice.15
  2.6 0.0 copy-done.4
  2.6 0.7 dynamic-slice
  3.3 0.8 dynamic-update-slice
  4.7 12.8 %all-reduce = s32[8]{0:T(128)S(1)} all-reduce(s32[8]{0:T(128)S(1)} %dynamic-update-slice), channel_id=1, replica_groups=mesh['depth'=8,'row'=32] {'depth'}, use_global_device_ids=true, to_apply=%add | all-reduce | flops 8 | bytes 64
  17.5 0.1 rev.3
  17.6 1.5 bitcast_convert_fusion.inten_ref
  19.1 34.9 %all_gather.6 = bf16[8,16,2048]{2,1,0:T(8,128)(2,1)S(1)} all-gather(bf16[1,16,2048]{2,1,0:T(8,128)(2,1)S(1)} %copy-done), channel_id=1, replica_groups=mesh['depth'=8,'row'=32] {'depth'}, dimensions={0}, use_global_device_ids=true | all-gather | bytes 589824 | tf_op jit(solution)/shard_map/all_gather | solution.py:266
  54.0 0.8 multiply_select_fusion.1
  54.8 4.6 %fusion = (f32[8,16,2048]{2,1,0:T(8,128)}, f32[8,16,2048]{2,1,0:T(8,128)}) fusion(bf16[8,16,2048]{2,1,0:T(8,128)(2,1)S(1)} %all_gather.6), kind=kLoop, calls=%fused_computation.1 | loop fusion | flops 524288 | bytes 2621440 | tf_op jit(solution)/shard_map/sin | solution.py:272
  59.4 0.6 copy-done.2
  60.1 0.1 add_multiply_fusion
  60.2 0.6 fusion.10
  60.7 0.7 pad_maximum_fusion.3.u0_ref
  61.5 0.1 fusion.2
  61.6 1.0 pad_maximum_fusion.cband_ref
  62.5 1.6 fusion.7
  64.1 1.2 maximum_maximum_fusion.rband_ref
  65.3 126.0 %shard_map.46 = f32[8,16,2048]{2,1,0:T(8,128)} custom-call(f32[32,2048]{1,0:T(8,128)} %pad_maximum_fusion.3.u0_ref, f32[8,16,2048]{2,1,0:T(8,128)} %get-tuple-element.6.cos_ref, f32[8,16,2048]{2,1,0:T(8,128)} %get-tuple-element.5.sin_ref, f32[16,2048]{1,0:T(8,128)} %bitcast_convert_fusion.inten_ref, f32[16,3,32,32]{3,2,1,0:T(8,128)} %maximum_maximum_fusion.rband_ref, ...), custom_call_target="tpu_custom_call" | custom-call | tf_op jit(solution)/shard_map/pallas_call | solution.py:221
  191.3 0.9 constant_dynamic-slice_fusion
  192.2 0.1 collective-permute-start
  192.3 4.9 %collective-permute-done = f32[1,16,2048]{2,1,0:T(8,128)S(1)} collective-permute-done((f32[1,16,2048]{2,1,0:T(8,128)S(1)}, f32[1,16,2048]{2,1,0:T(8,128)S(1)}, u32[]{:S(2)}, u32[]{:S(2)}) %collective-permute-start) | collective-permute-done | bytes 131104 | tf_op jit(solution)/shard_map/ppermute | solution.py:277
  197.3 1.6 select_add_fusion
  (12 shorter events, 0.0 us)
Async XLA Ops:
  0.0 0.7 copy-start.3
  1.9 0.7 copy-start.4
  17.6 1.5 copy-start
  59.4 0.7 copy-start.2
  61.5 1.0 copy-start.1
  192.2 5.1 %collective-permute-start = (f32[1,16,2048]{2,1,0:T(8,128)S(1)}, f32[1,16,2048]{2,1,0:T(8,128)S(1)}, u32[]{:S(2)}, u32[]{:S(2)}) collective-permute-start(f32[1,16,2048]{2,1,0:T(8,128)S(1)} %constant_dynamic-slice_fusion), channel_id=1, source_target_pairs={{0,32},{32,0},{64,96},{96,64},{128,160},{160,128},{192,224},{224,1... | collective-permute-start | bytes 393224 | tf_op jit(solution)/shard_map/ppermute | solution.py:277

commit v3 on v2

--- a/solution.py
+++ b/solution.py
@@ -242,6 +242,71 @@
     )(u0, cosines, sines, intensity, row_band, col_band)
 
 
+def gather_kernel(sections, vol_ref, off_ref, vol_out, off_out, vol_slots, off_slots,
+                  send_vol, send_off, recv_vol, recv_off):
+    me = lax.axis_index("depth")
+    barrier = pltpu.get_barrier_semaphore()
+    for step in range(1, sections):
+        peer = (me + step) % sections
+        pl.semaphore_signal(barrier, 1, device_id={"depth": peer}, device_id_type=MESH)
+    pl.semaphore_wait(barrier, sections - 1)
+
+    def copies(step):
+        peer = (me + step) % sections
+        source = (me + sections - step) % sections
+        out_vol = pltpu.make_async_remote_copy(
+            src_ref=vol_ref.at[0], dst_ref=vol_slots.at[me], send_sem=send_vol.at[step],
+            recv_sem=recv_vol.at[me], device_id={"depth": peer}, device_id_type=MESH)
+        out_off = pltpu.make_async_remote_copy(
+            src_ref=off_ref, dst_ref=off_slots.at[me], send_sem=send_off.at[step],
+            recv_sem=recv_off.at[me], device_id={"depth": peer}, device_id_type=MESH)
+        in_vol = pltpu.make_async_remote_copy(
+            src_ref=vol_ref.at[0], dst_ref=vol_slots.at[source], send_sem=send_vol.at[step],
+            recv_sem=recv_vol.at[source], device_id={"depth": peer}, device_id_type=MESH)
+        in_off = pltpu.make_async_remote_copy(
+            src_ref=off_ref, dst_ref=off_slots.at[source], send_sem=send_off.at[step],
+            recv_sem=recv_off.at[source], device_id={"depth": peer}, device_id_type=MESH)
+        return out_vol, out_off, in_vol, in_off
+
+    for step in range(1, sections):
+        out_vol, out_off, _, _ = copies(step)
+        out_vol.start()
+        out_off.start()
+    vol_slots[me] = vol_ref[0]
+    off_slots[me] = off_ref[...]
+    for step in range(1, sections):
+        out_vol, out_off, in_vol, in_off = copies(step)
+        in_vol.wait_recv()
+        in_off.wait_recv()
+        out_vol.wait_send()
+        out_off.wait_send()
+    vol_out[...] = vol_slots[...]
+    off_out[...] = off_slots[...]
+
+
+def gather_depth(index_volume, offsets, sections):
+    _, height, columns = index_volume.shape
+    off_tile = jnp.broadcast_to(offsets.astype(jnp.float32)[:, None], (8, LANE))
+    vol_shape = (sections, height, columns)
+    off_shape = (sections, 8, LANE)
+    return pl.pallas_call(
+        functools.partial(gather_kernel, sections),
+        out_shape=(jax.ShapeDtypeStruct(vol_shape, index_volume.dtype),
+                   jax.ShapeDtypeStruct(off_shape, jnp.float32)),
+        in_specs=[pl.BlockSpec(memory_space=pltpu.VMEM)] * 2,
+        out_specs=(pl.BlockSpec(memory_space=pltpu.VMEM),) * 2,
+        scratch_shapes=[
+            pltpu.VMEM(vol_shape, index_volume.dtype),
+            pltpu.VMEM(off_shape, jnp.float32),
+            pltpu.SemaphoreType.DMA((sections,)),
+            pltpu.SemaphoreType.DMA((sections,)),
+            pltpu.SemaphoreType.DMA((sections,)),
+            pltpu.SemaphoreType.DMA((sections,)),
+        ],
+        compiler_params=pltpu.CompilerParams(collective_id=1, has_side_effects=True),
+    )(index_volume, off_tile)
+
+
 def plane_wave(angle, row_start, height, columns, total_rows, total_cols):
     across = angle - TILTS // 2
     along = jnp.mod(3 * angle, TILTS) - TILTS // 2
@@ -263,8 +328,8 @@
     total_rows = height * rows
     angle_count = angles.shape[0]
     angle_no = section_no % angle_count
-    volume = lax.all_gather(index_volume, "depth", axis=0, tiled=True)
-    shifts = lax.all_gather(offsets, "depth", axis=0, tiled=True)
+    volume, shift_tiles = gather_depth(index_volume, offsets, sections)
+    shifts = shift_tiles[:, 0, 0].astype(jnp.int32)
     intensity = lax.dynamic_index_in_dim(measured, angle_no, 0, keepdims=False).astype(jnp.float32)
     angle = lax.dynamic_index_in_dim(angles, angle_no, 0, keepdims=False)
     incident = plane_wave(angle, row_start, height, columns, total_rows, columns)

time: 199 us -> 169 us (0.85)
  blocking collectives: 47.6 us -> 0 us
  Pallas kernels: 126 us -> 144 us
    all_gather x1 -> x0, blocking collectives: 34.9 us -> none  [body(): volume = lax.all_gather(index_volume, 'depth', axis=0, tiled=True)]
    pallas_call x0 -> x1, Pallas kernels: none -> 14.3 us  [gather_depth(): pl.pallas_call(functools.partial(gather_kernel, sections), out_shape=(jax...]
    unnamed x1 -> x0, blocking collectives: 12.8 us -> none
    pallas_call x1, Pallas kernels: 126 us -> 130 us  [run_chain(): pl.pallas_call(functools.partial(chain_kernel, rows), out_shape=jax.Shape...]
    unnamed x13 -> x8, local copies, waits for them, and re-layouts: 2.77 us -> 0.67 us
where the time goes in v3:
time: 169 us
  Pallas kernels  144 us (85%)
  other arithmetic  14.8 us (9%)
  waiting for transfers between devices  4.95 us (3%)
  local copies, waits for them, and re-layouts  2.87 us (2%)
  between operations  2.08 us (1%)
    pallas_call x1, Pallas kernels, run_chain(): pl.pallas_call(functools.partial(chain_kernel, rows), out_shape=jax.Shape...  130 us
    pallas_call x1, Pallas kernels, gather_depth(): pl.pallas_call(functools.partial(gather_kernel, sections), out_shape=(jax...  14.3 us
    ppermute x1, waiting for transfers between devices, body(): received = lax.ppermute(for_partner, 'depth', pairs)  4.95 us
    sin x1, other arithmetic, body(): jnp.sin(phases)  4.58 us
  transfers between devices with their start and end apart: 1, of which 1 were waited for; matrix products, arithmetic and copies ran while one was open for 0% of the time, Pallas kernels for 0%

profile of v3, /device:TPU:2, one launch (start us, length us, event | category | flops | bytes accessed | tf_op | source)
XLA Modules:
  0.0 168.7 jit_solution(2138192698426791438)
XLA Ops:
  0.0 0.7 copy-done.3
  0.7 0.6 dynamic_slice.15
  3.2 1.5 bitcast_convert_fusion.inten_ref
  4.8 0.6 broadcast_in_dim.20.off_ref
  5.3 14.3 %shard_map.46 = (bf16[8,16,2048]{2,1,0:T(8,128)(2,1)}, f32[8,8,128]{2,1,0:T(8,128)}) custom-call(bf16[1,16,2048]{2,1,0:T(8,128)(2,1)} %vol_ref.1, f32[8,128]{1,0:T(8,128)} %broadcast_in_dim.20.off_ref), custom_call_target="tpu_custom_call" | custom-call | tf_op jit(solution)/shard_map/pallas_call | solution.py:292
  19.6 0.0 copy-start
  19.6 1.0 convert_reduce_fusion
  20.7 0.1 rev.3
  20.8 0.8 multiply_select_fusion.1
  21.6 4.6 %fusion = (f32[8,16,2048]{2,1,0:T(8,128)}, f32[8,16,2048]{2,1,0:T(8,128)}) fusion(bf16[8,16,2048]{2,1,0:T(8,128)(2,1)S(1)} %copy-done), kind=kLoop, calls=%fused_computation.1 | loop fusion | flops 524288 | bytes 2621440 | tf_op jit(solution)/shard_map/sin | solution.py:337
  26.2 0.6 fusion.10
  26.8 0.0 copy-start.2
  26.8 0.7 pad_maximum_fusion.3.u0_ref
  27.6 0.1 add_multiply_fusion
  27.7 0.1 fusion.2
  27.7 0.0 copy-start.1
  27.7 1.0 pad_maximum_fusion.cband_ref
  28.7 1.6 fusion.7
  30.3 1.2 maximum_maximum_fusion.rband_ref
  31.4 129.7 %shard_map.47 = f32[8,16,2048]{2,1,0:T(8,128)} custom-call(f32[32,2048]{1,0:T(8,128)} %pad_maximum_fusion.3.u0_ref, f32[8,16,2048]{2,1,0:T(8,128)} %get-tuple-element.10.cos_ref, f32[8,16,2048]{2,1,0:T(8,128)} %get-tuple-element.9.sin_ref, f32[16,2048]{1,0:T(8,128)} %bitcast_convert_fusion.inten_ref, f32[16,3,32,32]{3,2,1,0:T(8,128)} %maximum_maximum_fusion.rband_ref, ...), custom_call_target="tpu_custom_call" | custom-call | tf_op jit(solution)/shard_map/pallas_call | solution.py:221
  161.2 0.9 constant_dynamic-slice_fusion
  162.1 0.1 collective-permute-start
  162.2 4.9 %collective-permute-done = f32[1,16,2048]{2,1,0:T(8,128)S(1)} collective-permute-done((f32[1,16,2048]{2,1,0:T(8,128)S(1)}, f32[1,16,2048]{2,1,0:T(8,128)S(1)}, u32[]{:S(2)}, u32[]{:S(2)}) %collective-permute-start) | collective-permute-done | bytes 131104 | tf_op jit(solution)/shard_map/ppermute | solution.py:342
  167.1 1.6 select_add_fusion
  (8 shorter events, 0.0 us)
Async XLA Ops:
  0.0 0.7 copy-start.3
  19.6 2.0 %copy-start = (bf16[8,16,2048]{2,1,0:T(8,128)(2,1)S(1)}, bf16[8,16,2048]{2,1,0:T(8,128)(2,1)}, u32[]{:S(2)}) copy-start(bf16[8,16,2048]{2,1,0:T(8,128)(2,1)} %get-tuple-element.7) | copy-start | bytes 1572868
  26.8 0.8 copy-start.2
  27.7 1.0 copy-start.1
  162.1 5.1 %collective-permute-start = (f32[1,16,2048]{2,1,0:T(8,128)S(1)}, f32[1,16,2048]{2,1,0:T(8,128)S(1)}, u32[]{:S(2)}, u32[]{:S(2)}) collective-permute-start(f32[1,16,2048]{2,1,0:T(8,128)S(1)} %constant_dynamic-slice_fusion), channel_id=1, source_target_pairs={{0,32},{32,0},{64,96},{96,64},{128,160},{160,128},{192,224},{224,1... | collective-permute-start | bytes 393224 | tf_op jit(solution)/shard_map/ppermute | solution.py:342

commit v4 on v3

--- a/solution.py
+++ b/solution.py
@@ -78,12 +78,17 @@
     )
 
 
+CHUNKS = 4
+
+
 def chain_kernel(rows, u0_ref, cos_ref, sin_ref, inten_ref, rband_ref, cband_ref,
                  terms_ref, field_ref, acc_ref, y_store, b_store, before, after, bmh_ref, bml_ref,
                  send_dn, send_up, recv_bf, recv_af):
     me = lax.axis_index("row")
     layers, height, columns = cos_ref.shape
     blocks = columns // LANE
+    width = columns // CHUNKS
+    per_chunk = blocks // CHUNKS
     has_up = me > 0
     has_dn = me < rows - 1
 
@@ -105,17 +110,19 @@
         ref[0] = zero_block
         ref[blocks + 1] = zero_block
 
-    def copies(k, source):
+    def copies(k, c, store):
+        cols = pl.ds(c * width, width)
+        slot = k * CHUNKS + c
         down = pltpu.make_async_remote_copy(
-            src_ref=source, dst_ref=before.at[k], send_sem=send_dn.at[k], recv_sem=recv_bf.at[k],
-            device_id={"row": me + 1}, device_id_type=MESH)
+            src_ref=store.at[:, cols], dst_ref=before.at[k, :, cols], send_sem=send_dn.at[slot],
+            recv_sem=recv_bf.at[slot], device_id={"row": me + 1}, device_id_type=MESH)
         up = pltpu.make_async_remote_copy(
-            src_ref=source, dst_ref=after.at[k], send_sem=send_up.at[k], recv_sem=recv_af.at[k],
-            device_id={"row": me - 1}, device_id_type=MESH)
+            src_ref=store.at[:, cols], dst_ref=after.at[k, :, cols], send_sem=send_up.at[slot],
+            recv_sem=recv_af.at[slot], device_id={"row": me - 1}, device_id_type=MESH)
         return down, up
 
-    def start(k, source):
-        down, up = copies(k, source)
+    def start(k, c, store):
+        down, up = copies(k, c, store)
 
         @pl.when(has_dn)
         def _():
@@ -125,70 +132,87 @@
         def _():
             up.start()
 
-    def finish(k, source):
-        down, up = copies(k, source)
-
-        @pl.when(has_dn)
-        def _():
-            down.wait_send()
-
-        @pl.when(has_up)
-        def _():
-            up.wait_send()
-
-    def row_mix(k, source, z):
-        down, up = copies(k, source)
-        acc_ref[...] = dot3(rband_ref[k, 1], z)
-        start(k, source)
-
-        @pl.when(has_up)
-        def _():
-            down.wait_recv()
-            acc_ref[...] += dot3(rband_ref[k, 0], before[k])
-
-        @pl.when(has_dn)
-        def _():
-            up.wait_recv()
-            acc_ref[...] += dot3(rband_ref[k, 2], after[k])
-
-        return acc_ref[...]
-
-    def col_mix(v, which):
+    def finish(k, store):
+        for c in range(CHUNKS):
+            down, up = copies(k, c, store)
+
+            @pl.when(has_dn)
+            def _():
+                down.wait_send()
+
+            @pl.when(has_up)
+            def _():
+                up.wait_send()
+
+    def produce(k, chunk_value, store):
+        for c in range(CHUNKS):
+            store[:, c * width:(c + 1) * width] = chunk_value(c)
+            if c >= 1:
+                start(k, c - 1, store)
+        acc_ref[...] = dot3(rband_ref[k, 1], store[...])
+        start(k, CHUNKS - 1, store)
+
+    def consume(k, store):
+        for c in range(CHUNKS):
+            down, up = copies(k, c, store)
+            cols = slice(c * width, (c + 1) * width)
+
+            @pl.when(has_up)
+            def _():
+                down.wait_recv()
+                acc_ref[:, cols] += dot3(rband_ref[k, 0], before[k, :, cols])
+
+            @pl.when(has_dn)
+            def _():
+                up.wait_recv()
+                acc_ref[:, cols] += dot3(rband_ref[k, 2], after[k, :, cols])
+
+    def load_blocks(v):
         high, low = split_bf16(v)
         for b in range(blocks):
             bmh_ref[b + 1] = high[:, b * LANE:(b + 1) * LANE]
             bml_ref[b + 1] = low[:, b * LANE:(b + 1) * LANE]
+
+    def col_chunk(c, which):
         total = None
         f32 = jnp.float32
+        first = c * per_chunk
         for t in range(3):
-            xh = bmh_ref[t:t + blocks].reshape(blocks * 2 * height, LANE)
-            xl = bml_ref[t:t + blocks].reshape(blocks * 2 * height, LANE)
+            xh = bmh_ref[first + t:first + t + per_chunk].reshape(per_chunk * 2 * height, LANE)
+            xl = bml_ref[first + t:first + t + per_chunk].reshape(per_chunk * 2 * height, LANE)
             wh, wl = split_bf16(cband_ref[which, t])
             part = (jnp.dot(xh, wh, preferred_element_type=f32) + jnp.dot(xh, wl, preferred_element_type=f32)
                     + jnp.dot(xl, wh, preferred_element_type=f32))
             total = part if total is None else total + part
-        total = total.reshape(blocks, 2 * height, 2 * LANE)
+        total = total.reshape(per_chunk, 2 * height, 2 * LANE)
         real_part = total[:, :height, :LANE] - total[:, height:, LANE:]
         imag_part = total[:, :height, LANE:] + total[:, height:, :LANE]
         out = jnp.concatenate([real_part, imag_part], axis=1)
-        return jnp.concatenate([out[b] for b in range(blocks)], axis=1)
-
-    field_ref[...] = u0_ref[...]
-
-    def forward(s, carry):
-        u = field_ref[...]
-        c = cos_ref[s]
-        sn = sin_ref[s]
+        return jnp.concatenate([out[b] for b in range(per_chunk)], axis=1)
+
+    def rotated(s, c, u):
+        cols = pl.ds(c * width, width)
+        cs = cos_ref[s, :, cols]
+        sn = sin_ref[s, :, cols]
         ur = u[:height]
         ui = u[height:]
-        y_store[s] = jnp.concatenate([c * ur - sn * ui, c * ui + sn * ur], axis=0)
-        source = y_store.at[s]
-        v = row_mix(s, source, y_store[s])
-        field_ref[...] = col_mix(v, 0)
-        finish(s, source)
+        return jnp.concatenate([cs * ur - sn * ui, cs * ui + sn * ur], axis=0)
+
+    produce(0, lambda c: rotated(0, c, u0_ref[:, c * width:(c + 1) * width]), y_store.at[0])
+    consume(0, y_store.at[0])
+    finish(0, y_store.at[0])
+
+    def forward(s, carry):
+        load_blocks(acc_ref[...])
+        produce(s, lambda c: rotated(s, c, col_chunk(c, 0)), y_store.at[s])
+        consume(s, y_store.at[s])
+        finish(s, y_store.at[s])
         return carry
 
-    lax.fori_loop(0, layers, forward, 0)
+    lax.fori_loop(1, layers, forward, 0)
+    load_blocks(acc_ref[...])
+    for c in range(CHUNKS):
+        field_ref[:, c * width:(c + 1) * width] = col_chunk(c, 0)
     u = field_ref[...]
     ur = u[:height]
     ui = u[height:]
@@ -198,17 +222,18 @@
     def backward(j, carry):
         s = layers - 1 - j
         k = layers + j
-        b_store[j] = col_mix(field_ref[...], 1)
-        source = b_store.at[j]
-        acc = row_mix(k, source, b_store[j])
+        load_blocks(field_ref[...])
+        produce(k, lambda c: col_chunk(c, 1), b_store.at[j])
+        consume(k, b_store.at[j])
+        acc = acc_ref[...]
         ar = acc[:height]
         ai = acc[height:]
         y = y_store[s]
         terms_ref[s] = PHASE_SCALE * (y[:height] * ai - y[height:] * ar)
-        c = cos_ref[s]
+        cs = cos_ref[s]
         sn = sin_ref[s]
-        field_ref[...] = jnp.concatenate([c * ar + sn * ai, c * ai - sn * ar], axis=0)
-        finish(k, source)
+        field_ref[...] = jnp.concatenate([cs * ar + sn * ai, cs * ai - sn * ar], axis=0)
+        finish(k, b_store.at[j])
         return carry
 
     lax.fori_loop(0, layers, backward, 0)
@@ -232,10 +257,10 @@
             pltpu.VMEM((2 * layers,) + field, jnp.float32),
             pltpu.VMEM((blocks + 2, 2 * height, LANE), jnp.bfloat16),
             pltpu.VMEM((blocks + 2, 2 * height, LANE), jnp.bfloat16),
-            pltpu.SemaphoreType.DMA((2 * layers,)),
-            pltpu.SemaphoreType.DMA((2 * layers,)),
-            pltpu.SemaphoreType.DMA((2 * layers,)),
-            pltpu.SemaphoreType.DMA((2 * layers,)),
+            pltpu.SemaphoreType.DMA((2 * layers * CHUNKS,)),
+            pltpu.SemaphoreType.DMA((2 * layers * CHUNKS,)),
+            pltpu.SemaphoreType.DMA((2 * layers * CHUNKS,)),
+            pltpu.SemaphoreType.DMA((2 * layers * CHUNKS,)),
         ],
         compiler_params=pltpu.CompilerParams(
             collective_id=0, has_side_effects=True, vmem_limit_bytes=56 * 1024 * 1024),

time: 169 us -> 159 us (0.941)
  Pallas kernels: 144 us -> 134 us
    pallas_call x1, Pallas kernels: 130 us -> 120 us  [run_chain(): pl.pallas_call(functools.partial(chain_kernel, rows), out_shape=jax.Shape...]
where the time goes in v4:
time: 159 us
  Pallas kernels  134 us (84%)
  other arithmetic  14.8 us (9%)
  waiting for transfers between devices  4.95 us (3%)
  local copies, waits for them, and re-layouts  2.87 us (2%)
  between operations  2.08 us (1%)
    pallas_call x1, Pallas kernels, run_chain(): pl.pallas_call(functools.partial(chain_kernel, rows), out_shape=jax.Shape...  120 us
    pallas_call x1, Pallas kernels, gather_depth(): pl.pallas_call(functools.partial(gather_kernel, sections), out_shape=(jax...  14.3 us
    ppermute x1, waiting for transfers between devices, body(): received = lax.ppermute(for_partner, 'depth', pairs)  4.95 us
    sin x1, other arithmetic, body(): jnp.sin(phases)  4.58 us
  transfers between devices with their start and end apart: 1, of which 1 were waited for; matrix products, arithmetic and copies ran while one was open for 0% of the time, Pallas kernels for 0%

profile of v4, /device:TPU:2, one launch (start us, length us, event | category | flops | bytes accessed | tf_op | source)
XLA Modules:
  0.0 159.0 jit_solution(601956307504898309)
XLA Ops:
  0.0 0.7 copy-done.3
  0.7 0.6 dynamic_slice.15
  3.2 1.5 bitcast_convert_fusion.inten_ref
  4.8 0.6 broadcast_in_dim.20.off_ref
  5.3 14.3 %shard_map.46 = (bf16[8,16,2048]{2,1,0:T(8,128)(2,1)}, f32[8,8,128]{2,1,0:T(8,128)}) custom-call(bf16[1,16,2048]{2,1,0:T(8,128)(2,1)} %vol_ref.1, f32[8,128]{1,0:T(8,128)} %broadcast_in_dim.20.off_ref), custom_call_target="tpu_custom_call" | custom-call | tf_op jit(solution)/shard_map/pallas_call | solution.py:317
  19.6 0.0 copy-start
  19.6 1.0 convert_reduce_fusion
  20.7 0.1 rev.3
  20.8 0.8 multiply_select_fusion.1
  21.6 4.6 %fusion = (f32[8,16,2048]{2,1,0:T(8,128)}, f32[8,16,2048]{2,1,0:T(8,128)}) fusion(bf16[8,16,2048]{2,1,0:T(8,128)(2,1)S(1)} %copy-done), kind=kLoop, calls=%fused_computation.1 | loop fusion | flops 524288 | bytes 2621440 | tf_op jit(solution)/shard_map/sin | solution.py:362
  26.2 0.6 fusion.10
  26.8 0.0 copy-start.2
  26.8 0.7 pad_maximum_fusion.3.u0_ref
  27.6 0.1 add_multiply_fusion
  27.7 0.1 fusion.2
  27.7 0.0 copy-start.1
  27.7 1.0 pad_maximum_fusion.cband_ref
  28.7 1.6 fusion.7
  30.3 1.2 maximum_maximum_fusion.rband_ref
  31.4 120.0 %shard_map.47 = f32[8,16,2048]{2,1,0:T(8,128)} custom-call(f32[32,2048]{1,0:T(8,128)} %pad_maximum_fusion.3.u0_ref, f32[8,16,2048]{2,1,0:T(8,128)} %get-tuple-element.10.cos_ref, f32[8,16,2048]{2,1,0:T(8,128)} %get-tuple-element.9.sin_ref, f32[16,2048]{1,0:T(8,128)} %bitcast_convert_fusion.inten_ref, f32[16,3,32,32]{3,2,1,0:T(8,128)} %maximum_maximum_fusion.rband_ref, ...), custom_call_target="tpu_custom_call" | custom-call | tf_op jit(solution)/shard_map/pallas_call | solution.py:246
  151.4 0.9 constant_dynamic-slice_fusion
  152.4 0.1 collective-permute-start
  152.5 4.9 %collective-permute-done = f32[1,16,2048]{2,1,0:T(8,128)S(1)} collective-permute-done((f32[1,16,2048]{2,1,0:T(8,128)S(1)}, f32[1,16,2048]{2,1,0:T(8,128)S(1)}, u32[]{:S(2)}, u32[]{:S(2)}) %collective-permute-start) | collective-permute-done | bytes 131104 | tf_op jit(solution)/shard_map/ppermute | solution.py:367
  157.4 1.6 select_add_fusion
  (8 shorter events, 0.0 us)
Async XLA Ops:
  0.0 0.7 copy-start.3
  19.6 2.0 %copy-start = (bf16[8,16,2048]{2,1,0:T(8,128)(2,1)S(1)}, bf16[8,16,2048]{2,1,0:T(8,128)(2,1)}, u32[]{:S(2)}) copy-start(bf16[8,16,2048]{2,1,0:T(8,128)(2,1)} %get-tuple-element.7) | copy-start | bytes 1572868
  26.8 0.8 copy-start.2
  27.7 1.0 copy-start.1
  152.4 5.1 %collective-permute-start = (f32[1,16,2048]{2,1,0:T(8,128)S(1)}, f32[1,16,2048]{2,1,0:T(8,128)S(1)}, u32[]{:S(2)}, u32[]{:S(2)}) collective-permute-start(f32[1,16,2048]{2,1,0:T(8,128)S(1)} %constant_dynamic-slice_fusion), channel_id=1, source_target_pairs={{0,32},{32,0},{64,96},{96,64},{128,160},{160,128},{192,224},{224,1... | collective-permute-start | bytes 393224 | tf_op jit(solution)/shard_map/ppermute | solution.py:367

commit v5 on v4

--- a/solution.py
+++ b/solution.py
@@ -82,9 +82,11 @@
 
 
 def chain_kernel(rows, u0_ref, cos_ref, sin_ref, inten_ref, rband_ref, cband_ref,
-                 terms_ref, field_ref, acc_ref, y_store, b_store, before, after, bmh_ref, bml_ref,
-                 send_dn, send_up, recv_bf, recv_af):
+                 out_ref, terms_ref, partner_ref, field_ref, acc_ref, y_store, b_store, before, after,
+                 bmh_ref, bml_ref, send_dn, send_up, recv_bf, recv_af, send_pair, recv_pair):
     me = lax.axis_index("row")
+    section = lax.axis_index("depth")
+    partner = section + 1 - 2 * (section % 2)
     layers, height, columns = cos_ref.shape
     blocks = columns // LANE
     width = columns // CHUNKS
@@ -102,8 +104,9 @@
     def _():
         pl.semaphore_signal(barrier, 1, device_id={"row": me + 1}, device_id_type=MESH)
 
+    pl.semaphore_signal(barrier, 1, device_id={"depth": partner}, device_id_type=MESH)
     peers = (me + rows - 1) // rows + (2 * rows - 2 - me) // rows
-    pl.semaphore_wait(barrier, peers)
+    pl.semaphore_wait(barrier, peers + 1)
 
     zero_block = jnp.zeros((2 * height, LANE), jnp.bfloat16)
     for ref in (bmh_ref, bml_ref):
@@ -237,6 +240,14 @@
         return carry
 
     lax.fori_loop(0, layers, backward, 0)
+    own = terms_ref[section]
+    exchange = pltpu.make_async_remote_copy(
+        src_ref=terms_ref.at[partner], dst_ref=partner_ref, send_sem=send_pair, recv_sem=recv_pair,
+        device_id={"depth": partner}, device_id_type=MESH)
+    exchange.start()
+    exchange.wait_send()
+    exchange.wait_recv()
+    out_ref[0] = own + partner_ref[...]
 
 
 def run_chain(u0, cosines, sines, intensity, row_band, col_band, rows):
@@ -245,10 +256,12 @@
     field = (2 * height, columns)
     return pl.pallas_call(
         functools.partial(chain_kernel, rows),
-        out_shape=jax.ShapeDtypeStruct((layers, height, columns), jnp.float32),
+        out_shape=jax.ShapeDtypeStruct((1, height, columns), jnp.float32),
         in_specs=[pl.BlockSpec(memory_space=pltpu.VMEM)] * 6,
         out_specs=pl.BlockSpec(memory_space=pltpu.VMEM),
         scratch_shapes=[
+            pltpu.VMEM((layers, height, columns), jnp.float32),
+            pltpu.VMEM((height, columns), jnp.float32),
             pltpu.VMEM(field, jnp.float32),
             pltpu.VMEM(field, jnp.float32),
             pltpu.VMEM((layers,) + field, jnp.float32),
@@ -261,6 +274,8 @@
             pltpu.SemaphoreType.DMA((2 * layers * CHUNKS,)),
             pltpu.SemaphoreType.DMA((2 * layers * CHUNKS,)),
             pltpu.SemaphoreType.DMA((2 * layers * CHUNKS,)),
+            pltpu.SemaphoreType.DMA,
+            pltpu.SemaphoreType.DMA,
         ],
         compiler_params=pltpu.CompilerParams(
             collective_id=0, has_side_effects=True, vmem_limit_bytes=56 * 1024 * 1024),
@@ -359,15 +374,8 @@
     angle = lax.dynamic_index_in_dim(angles, angle_no, 0, keepdims=False)
     incident = plane_wave(angle, row_start, height, columns, total_rows, columns)
     phases = PHASE_SCALE * volume.astype(jnp.float32)
-    terms = run_chain(incident, jnp.cos(phases), jnp.sin(phases), intensity,
-                      row_bands(shifts, height), column_bands(), rows)
-    own = lax.dynamic_index_in_dim(terms, section_no, 0, keepdims=True)
-    for_partner = lax.dynamic_index_in_dim(terms, section_no ^ 1, 0, keepdims=True)
-    pairs = [(i, i ^ 1) for i in range(sections)]
-    received = lax.ppermute(for_partner, "depth", pairs)
-    first = jnp.where(angle_no == 0, own, received)
-    second = jnp.where(angle_no == 0, received, own)
-    return first + second
+    return run_chain(incident, jnp.cos(phases), jnp.sin(phases), intensity,
+                     row_bands(shifts, height), column_bands(), rows)
 
 
 def solution(mesh):

time: 159 us -> 157 us (0.987)
  waiting for transfers between devices: 4.95 us -> 0 us
  Pallas kernels: 134 us -> 137 us
  other arithmetic: 14.8 us -> 13 us
    ppermute x1 -> x0, waiting for transfers between devices: 4.95 us -> none  [body(): received = lax.ppermute(for_partner, 'depth', pairs)]
    pallas_call x1, Pallas kernels: 120 us -> 122 us  [run_chain(): pl.pallas_call(functools.partial(chain_kernel, rows), out_shape=jax.Shape...]
    unnamed x8 -> x9, local copies, waits for them, and re-layouts: 0.67 us -> 2.79 us
  transfers between devices with their start and end apart: 1 -> 0, of which waited for: 1 -> 0; matrix products, arithmetic and copies ran while one was open for 0% -> 0% of each run, Pallas kernels for 0% -> 0%
where the time goes in v5:
time: 157 us; the launch traced here: 156 us
  Pallas kernels  137 us (87%)
  other arithmetic  13 us (8%)
  local copies, waits for them, and re-layouts  4.05 us (3%)
  between operations  2.06 us (1%)
    pallas_call x1, Pallas kernels, run_chain(): pl.pallas_call(functools.partial(chain_kernel, rows), out_shape=jax.Shape...  122 us
    pallas_call x1, Pallas kernels, gather_depth(): pl.pallas_call(functools.partial(gather_kernel, sections), out_shape=(jax...  14.3 us
    sin x1, other arithmetic, body(): jnp.sin(phases)  4.55 us

profile of v5, /device:TPU:2, one launch (start us, length us, event | category | flops | bytes accessed | tf_op | source)
XLA Modules:
  0.0 155.6 jit_solution(984669237560369530)
XLA Ops:
  0.7 0.0 copy-start.3
  0.7 0.6 copy-done.3
  1.3 0.6 dynamic_slice.8
  3.2 0.6 broadcast_in_dim.20.off_ref
  3.8 1.5 bitcast_convert_fusion.inten_ref
  5.3 0.6 fusion.10
  5.9 0.7 pad_maximum_fusion.3.u0_ref
  6.6 14.3 %shard_map.46 = (bf16[8,16,2048]{2,1,0:T(8,128)(2,1)}, f32[8,8,128]{2,1,0:T(8,128)}) custom-call(bf16[1,16,2048]{2,1,0:T(8,128)(2,1)} %vol_ref.1, f32[8,128]{1,0:T(8,128)} %broadcast_in_dim.20.off_ref), custom_call_target="tpu_custom_call" | custom-call | tf_op jit(solution)/shard_map/pallas_call | solution.py:332
  20.9 1.0 convert_reduce_fusion
  21.9 0.0 copy-start.2
  21.9 0.1 rev.3
  22.0 0.6 copy-done.2
  22.6 0.1 add_multiply_fusion
  22.7 0.8 multiply_select_fusion.1
  23.5 0.1 fusion.2
  23.6 0.0 copy-start.1
  23.6 0.9 pad_maximum_fusion.cband_ref
  24.5 0.0 copy-done.1
  24.5 1.6 %fusion.7 = (f32[16,3,16,16]{3,2,1,0:T(8,128)S(1)}, f32[16,3,16,16]{3,2,1,0:T(8,128)S(1)}, f32[16,3,16,16]{3,2,1,0:T(8,128)S(1)}) fusion(f32[16]{0:T(128)S(1)} %copy-done.1, s32[16]{0:T(128)S(1)} %add_multiply_fusion, s32[3]{0:T(128)S(1)} %fusion.12), kind=kLoop, calls=%fused_computation.28 | loop fusion | flops 172032 | bytes 147596 | tf_op jit(solution)/shard_map/neg | solution.py:39
  26.1 0.0 copy-start
  26.1 1.1 maximum_maximum_fusion.rband_ref
  27.3 4.5 %fusion = (f32[8,16,2048]{2,1,0:T(8,128)}, f32[8,16,2048]{2,1,0:T(8,128)}) fusion(bf16[8,16,2048]{2,1,0:T(8,128)(2,1)S(1)} %copy-done), kind=kLoop, calls=%fused_computation.1 | loop fusion | flops 524288 | bytes 2621440 | tf_op jit(solution)/shard_map/sin | solution.py:377
  31.8 122.3 %shard_map.47 = f32[1,16,2048]{2,1,0:T(8,128)} custom-call(f32[32,2048]{1,0:T(8,128)} %pad_maximum_fusion.3.u0_ref, f32[8,16,2048]{2,1,0:T(8,128)} %get-tuple-element.10.cos_ref, f32[8,16,2048]{2,1,0:T(8,128)} %get-tuple-element.9.sin_ref, f32[16,2048]{1,0:T(8,128)} %bitcast_convert_fusion.inten_ref, f32[16,3,32,32]{3,2,1,0:T(8,128)} %maximum_maximum_fusion.rband_ref, ...), custom_call_target="tpu_custom_call" | custom-call | tf_op jit(solution)/shard_map/pallas_call | solution.py:257
  154.1 1.6 %copy.7 = f32[1,16,2048]{2,1,0:T(8,128)} copy(f32[1,16,2048]{2,1,0:T(8,128)} %shard_map.47) | data formatting | bytes 262144
  (5 shorter events, 0.0 us)
Async XLA Ops:
  0.7 0.7 copy-start.3
  21.9 0.7 copy-start.2
  23.6 1.0 copy-start.1
  26.1 1.2 copy-start

commit v6 on v5

--- a/solution.py
+++ b/solution.py
@@ -147,34 +147,42 @@
             def _():
                 up.wait_send()
 
-    def produce(k, chunk_value, store):
+    def halo(k, c, store):
+        down, up = copies(k, c, store)
+        cols = pl.ds(c * width, width)
+        slot = k % 2
+
+        @pl.when(has_up)
+        def _():
+            down.wait_recv()
+            acc_ref[slot, :, cols] += dot3(rband_ref[k, 0], before[k, :, cols])
+
+        @pl.when(has_dn)
+        def _():
+            up.wait_recv()
+            acc_ref[slot, :, cols] += dot3(rband_ref[k, 2], after[k, :, cols])
+
+        return acc_ref[slot, :, cols]
+
+    def emit(k, c, store, value):
+        cols = pl.ds(c * width, width)
+        store[:, cols] = value
+        acc_ref[k % 2, :, cols] = dot3(rband_ref[k, 1], store[:, cols])
+        start(k, c, store)
+
+    def write_blocks(c, x):
+        high, low = split_bf16(x)
+        for b in range(per_chunk):
+            bmh_ref[c * per_chunk + b + 1] = high[:, b * LANE:(b + 1) * LANE]
+            bml_ref[c * per_chunk + b + 1] = low[:, b * LANE:(b + 1) * LANE]
+
+    def wave(k, store, store_next, finish_chunk, make_chunk):
         for c in range(CHUNKS):
-            store[:, c * width:(c + 1) * width] = chunk_value(c)
+            write_blocks(c, finish_chunk(c, halo(k, c, store)))
             if c >= 1:
-                start(k, c - 1, store)
-        acc_ref[...] = dot3(rband_ref[k, 1], store[...])
-        start(k, CHUNKS - 1, store)
-
-    def consume(k, store):
-        for c in range(CHUNKS):
-            down, up = copies(k, c, store)
-            cols = slice(c * width, (c + 1) * width)
-
-            @pl.when(has_up)
-            def _():
-                down.wait_recv()
-                acc_ref[:, cols] += dot3(rband_ref[k, 0], before[k, :, cols])
-
-            @pl.when(has_dn)
-            def _():
-                up.wait_recv()
-                acc_ref[:, cols] += dot3(rband_ref[k, 2], after[k, :, cols])
-
-    def load_blocks(v):
-        high, low = split_bf16(v)
-        for b in range(blocks):
-            bmh_ref[b + 1] = high[:, b * LANE:(b + 1) * LANE]
-            bml_ref[b + 1] = low[:, b * LANE:(b + 1) * LANE]
+                emit(k + 1, c - 1, store_next, make_chunk(c - 1))
+        emit(k + 1, CHUNKS - 1, store_next, make_chunk(CHUNKS - 1))
+        finish(k, store)
 
     def col_chunk(c, which):
         total = None
@@ -201,19 +209,28 @@
         ui = u[height:]
         return jnp.concatenate([cs * ur - sn * ui, cs * ui + sn * ur], axis=0)
 
-    produce(0, lambda c: rotated(0, c, u0_ref[:, c * width:(c + 1) * width]), y_store.at[0])
-    consume(0, y_store.at[0])
-    finish(0, y_store.at[0])
-
-    def forward(s, carry):
-        load_blocks(acc_ref[...])
-        produce(s, lambda c: rotated(s, c, col_chunk(c, 0)), y_store.at[s])
-        consume(s, y_store.at[s])
-        finish(s, y_store.at[s])
+    def adjoint_chunk(s, c, a):
+        cols = pl.ds(c * width, width)
+        ar = a[:height]
+        ai = a[height:]
+        y = y_store[s, :, cols]
+        terms_ref[s, :, cols] = PHASE_SCALE * (y[:height] * ai - y[height:] * ar)
+        cs = cos_ref[s, :, cols]
+        sn = sin_ref[s, :, cols]
+        return jnp.concatenate([cs * ar + sn * ai, cs * ai - sn * ar], axis=0)
+
+    for c in range(CHUNKS):
+        emit(0, c, y_store.at[0], rotated(0, c, u0_ref[:, c * width:(c + 1) * width]))
+
+    def forward(k, carry):
+        wave(k, y_store.at[k], y_store.at[k + 1], lambda c, a: a,
+             lambda c: rotated(k + 1, c, col_chunk(c, 0)))
         return carry
 
-    lax.fori_loop(1, layers, forward, 0)
-    load_blocks(acc_ref[...])
+    lax.fori_loop(0, layers - 1, forward, 0)
+    for c in range(CHUNKS):
+        write_blocks(c, halo(layers - 1, c, y_store.at[layers - 1]))
+    finish(layers - 1, y_store.at[layers - 1])
     for c in range(CHUNKS):
         field_ref[:, c * width:(c + 1) * width] = col_chunk(c, 0)
     u = field_ref[...]
@@ -221,25 +238,22 @@
     ui = u[height:]
     errors = ur * ur + ui * ui - inten_ref[...]
     field_ref[...] = jnp.concatenate([2.0 * errors * ur, 2.0 * errors * ui], axis=0)
+    for c in range(CHUNKS):
+        write_blocks(c, field_ref[:, c * width:(c + 1) * width])
+    for c in range(CHUNKS):
+        emit(layers, c, b_store.at[0], col_chunk(c, 1))
 
     def backward(j, carry):
         s = layers - 1 - j
-        k = layers + j
-        load_blocks(field_ref[...])
-        produce(k, lambda c: col_chunk(c, 1), b_store.at[j])
-        consume(k, b_store.at[j])
-        acc = acc_ref[...]
-        ar = acc[:height]
-        ai = acc[height:]
-        y = y_store[s]
-        terms_ref[s] = PHASE_SCALE * (y[:height] * ai - y[height:] * ar)
-        cs = cos_ref[s]
-        sn = sin_ref[s]
-        field_ref[...] = jnp.concatenate([cs * ar + sn * ai, cs * ai - sn * ar], axis=0)
-        finish(k, b_store.at[j])
+        wave(layers + j, b_store.at[j], b_store.at[j + 1], lambda c, a: adjoint_chunk(s, c, a),
+             lambda c: col_chunk(c, 1))
         return carry
 
-    lax.fori_loop(0, layers, backward, 0)
+    lax.fori_loop(0, layers - 1, backward, 0)
+    last = 2 * layers - 1
+    for c in range(CHUNKS):
+        adjoint_chunk(0, c, halo(last, c, b_store.at[layers - 1]))
+    finish(last, b_store.at[layers - 1])
     own = terms_ref[section]
     exchange = pltpu.make_async_remote_copy(
         src_ref=terms_ref.at[partner], dst_ref=partner_ref, send_sem=send_pair, recv_sem=recv_pair,
@@ -263,7 +277,7 @@
             pltpu.VMEM((layers, height, columns), jnp.float32),
             pltpu.VMEM((height, columns), jnp.float32),
             pltpu.VMEM(field, jnp.float32),
-            pltpu.VMEM(field, jnp.float32),
+            pltpu.VMEM((2,) + field, jnp.float32),
             pltpu.VMEM((layers,) + field, jnp.float32),
             pltpu.VMEM((layers,) + field, jnp.float32),
             pltpu.VMEM((2 * layers,) + field, jnp.float32),

time: 157 us -> 141 us (0.90)
  Pallas kernels: 137 us -> 121 us
    pallas_call x1, Pallas kernels: 122 us -> 107 us  [run_chain(): pl.pallas_call(functools.partial(chain_kernel, rows), out_shape=jax.Shape...]
where the time goes in v6:
time: 141 us; the launch traced here: 140 us
  Pallas kernels  121 us (86%)
  other arithmetic  13 us (9%)
  local copies, waits for them, and re-layouts  4.05 us (3%)
  between operations  2.06 us (1%)
    pallas_call x1, Pallas kernels, run_chain(): pl.pallas_call(functools.partial(chain_kernel, rows), out_shape=jax.Shape...  107 us
    pallas_call x1, Pallas kernels, gather_depth(): pl.pallas_call(functools.partial(gather_kernel, sections), out_shape=(jax...  14.3 us
    sin x1, other arithmetic, body(): jnp.sin(phases)  4.55 us

profile of v6, /device:TPU:2, one launch (start us, length us, event | category | flops | bytes accessed | tf_op | source)
XLA Modules:
  0.0 139.9 jit_solution(18402218228661805991)
XLA Ops:
  0.7 0.0 copy-start.3
  0.7 0.6 copy-done.3
  1.3 0.6 dynamic_slice.8
  3.2 0.6 broadcast_in_dim.20.off_ref
  3.8 1.5 %bitcast_convert_fusion.inten_ref = f32[16,2048]{1,0:T(8,128)} fusion(bf16[2,16,2048]{2,1,0:T(8,128)(2,1)} %param.7, s32[]{:T(128)S(6)} %select_n.42), kind=kLoop, calls=%fused_computation.30 | loop fusion | flops 32768 | bytes 196612 | tf_op jit(solution)/shard_map/convert_element_type | solution.py:387
  5.3 0.6 fusion.10
  5.9 0.7 pad_maximum_fusion.3.u0_ref
  6.6 14.3 %shard_map.46 = (bf16[8,16,2048]{2,1,0:T(8,128)(2,1)}, f32[8,8,128]{2,1,0:T(8,128)}) custom-call(bf16[1,16,2048]{2,1,0:T(8,128)(2,1)} %vol_ref.1, f32[8,128]{1,0:T(8,128)} %broadcast_in_dim.20.off_ref), custom_call_target="tpu_custom_call" | custom-call | tf_op jit(solution)/shard_map/pallas_call | solution.py:346
  20.9 1.0 convert_reduce_fusion
  21.9 0.0 copy-start.2
  21.9 0.1 rev.3
  22.0 0.6 copy-done.2
  22.6 0.1 add_multiply_fusion
  22.7 0.8 multiply_select_fusion.1
  23.5 0.1 fusion.2
  23.6 0.0 copy-start.1
  23.6 0.9 pad_maximum_fusion.cband_ref
  24.5 0.0 copy-done.1
  24.5 1.6 %fusion.7 = (f32[16,3,16,16]{3,2,1,0:T(8,128)S(1)}, f32[16,3,16,16]{3,2,1,0:T(8,128)S(1)}, f32[16,3,16,16]{3,2,1,0:T(8,128)S(1)}) fusion(f32[16]{0:T(128)S(1)} %copy-done.1, s32[16]{0:T(128)S(1)} %add_multiply_fusion, s32[3]{0:T(128)S(1)} %fusion.12), kind=kLoop, calls=%fused_computation.28 | loop fusion | flops 172032 | bytes 147596 | tf_op jit(solution)/shard_map/neg | solution.py:39
  26.1 0.0 copy-start
  26.1 1.1 maximum_maximum_fusion.rband_ref
  27.3 4.5 %fusion = (f32[8,16,2048]{2,1,0:T(8,128)}, f32[8,16,2048]{2,1,0:T(8,128)}) fusion(bf16[8,16,2048]{2,1,0:T(8,128)(2,1)S(1)} %copy-done), kind=kLoop, calls=%fused_computation.1 | loop fusion | flops 524288 | bytes 2621440 | tf_op jit(solution)/shard_map/sin | solution.py:391
  31.8 106.6 %shard_map.47 = f32[1,16,2048]{2,1,0:T(8,128)} custom-call(f32[32,2048]{1,0:T(8,128)} %pad_maximum_fusion.3.u0_ref, f32[8,16,2048]{2,1,0:T(8,128)} %get-tuple-element.10.cos_ref, f32[8,16,2048]{2,1,0:T(8,128)} %get-tuple-element.9.sin_ref, f32[16,2048]{1,0:T(8,128)} %bitcast_convert_fusion.inten_ref, f32[16,3,32,32]{3,2,1,0:T(8,128)} %maximum_maximum_fusion.rband_ref, ...), custom_call_target="tpu_custom_call" | custom-call | tf_op jit(solution)/shard_map/pallas_call | solution.py:271
  138.4 1.6 %copy.7 = f32[1,16,2048]{2,1,0:T(8,128)} copy(f32[1,16,2048]{2,1,0:T(8,128)} %shard_map.47) | data formatting | bytes 262144
  (5 shorter events, 0.0 us)
Async XLA Ops:
  0.7 0.7 copy-start.3
  21.9 0.7 copy-start.2
  23.6 1.0 copy-start.1
  26.1 1.2 copy-start

commit v7 on v6

--- a/solution.py
+++ b/solution.py
@@ -2,6 +2,7 @@
 import math
 
 import jax
+import numpy as np
 import jax.numpy as jnp
 from jax import lax
 from jax.experimental import pallas as pl
@@ -56,15 +57,18 @@
 
 
 def column_bands():
-    extent = (3, LANE, LANE)
-    part = lax.broadcasted_iota(jnp.int32, extent, 0)
-    source = lax.broadcasted_iota(jnp.int32, extent, 1) + (part - 1) * LANE
-    target = lax.broadcasted_iota(jnp.int32, extent, 2)
-    distance = (source - target).astype(jnp.float32)
-    real_part, imag_part = kernel_values(distance, HALFCOL, CHIRP_COL)
-    forward = jnp.concatenate([real_part, imag_part], axis=-1)
-    adjoint = jnp.concatenate([real_part, -imag_part], axis=-1)
-    return jnp.stack([forward, adjoint], axis=0)
+    part = np.arange(3)[:, None, None]
+    source = np.arange(LANE)[None, :, None] + (part - 1) * LANE
+    target = np.arange(LANE)[None, None, :]
+    distance = (source - target).astype(np.float64)
+    inside = np.abs(distance) <= HALFCOL
+    phase_arg = CHIRP_COL / HALFCOL * distance * distance
+    weight = 1.0 / math.sqrt(2 * HALFCOL + 1)
+    real_part = np.where(inside, np.cos(phase_arg) * weight, 0.0)
+    imag_part = np.where(inside, np.sin(phase_arg) * weight, 0.0)
+    forward = np.concatenate([real_part, imag_part], axis=-1)
+    adjoint = np.concatenate([real_part, -imag_part], axis=-1)
+    return jnp.asarray(np.stack([forward, adjoint], axis=0).astype(np.float32))
 
 
 def dot3(a, x):
@@ -78,7 +82,7 @@
     )
 
 
-CHUNKS = 4
+CHUNKS = 8
 
 
 def chain_kernel(rows, u0_ref, cos_ref, sin_ref, inten_ref, rband_ref, cband_ref,

time: 141 us -> 144 us (1.021)
  Pallas kernels: 121 us -> 125 us
  other arithmetic: 13 us -> 11.2 us
    pallas_call x1, Pallas kernels: 107 us -> 111 us  [run_chain(): pl.pallas_call(functools.partial(chain_kernel, rows), out_shape=jax.Shape...]
where the time goes in v7:
time: 144 us; the launch traced here: 143 us
  Pallas kernels  125 us (87%)
  other arithmetic  11.2 us (8%)
  local copies, waits for them, and re-layouts  4.62 us (3%)
  between operations  2.04 us (1%)
    pallas_call x1, Pallas kernels, run_chain(): pl.pallas_call(functools.partial(chain_kernel, rows), out_shape=jax.Shape...  111 us
    pallas_call x1, Pallas kernels, gather_depth(): pl.pallas_call(functools.partial(gather_kernel, sections), out_shape=(jax...  14.3 us
    sin x1, other arithmetic, body(): jnp.sin(phases)  4.55 us
    unnamed x9, local copies, waits for them, and re-layouts  3.36 us

profile of v7, /device:TPU:2, one launch (start us, length us, event | category | flops | bytes accessed | tf_op | source)
XLA Modules:
  0.0 143.1 jit_solution(12925662758800655760)
XLA Ops:
  0.7 0.0 copy-start.3
  0.7 0.6 copy-done.3
  1.3 0.6 dynamic_slice.8
  3.2 0.6 broadcast_in_dim.15.off_ref
  3.8 1.5 %bitcast_convert_fusion.inten_ref = f32[16,2048]{1,0:T(8,128)} fusion(bf16[2,16,2048]{2,1,0:T(8,128)(2,1)} %param.8, s32[]{:T(128)S(6)} %select_n.31), kind=kLoop, calls=%fused_computation.19 | loop fusion | flops 32768 | bytes 196612 | tf_op jit(solution)/shard_map/convert_element_type | solution.py:391
  5.3 0.6 fusion.7
  5.9 0.7 pad_maximum_fusion.u0_ref
  6.6 14.3 %shard_map.55 = (bf16[8,16,2048]{2,1,0:T(8,128)(2,1)}, f32[8,8,128]{2,1,0:T(8,128)}) custom-call(bf16[1,16,2048]{2,1,0:T(8,128)(2,1)} %vol_ref.1, f32[8,128]{1,0:T(8,128)} %broadcast_in_dim.15.off_ref), custom_call_target="tpu_custom_call" | custom-call | tf_op jit(solution)/shard_map/pallas_call | solution.py:350
  20.9 1.0 convert_reduce_fusion
  21.9 0.0 copy-start.2
  21.9 0.1 rev.3
  22.0 0.6 copy-done.2
  22.6 0.0 copy-start.1
  22.6 0.1 add_multiply_fusion
  22.7 0.6 copy-done.1
  23.2 1.6 %fusion.5 = (f32[16,3,16,16]{3,2,1,0:T(8,128)S(1)}, f32[16,3,16,16]{3,2,1,0:T(8,128)S(1)}, f32[16,3,16,16]{3,2,1,0:T(8,128)S(1)}) fusion(f32[16]{0:T(128)S(1)} %copy-done.1, s32[16]{0:T(128)S(1)} %add_multiply_fusion, s32[3]{0:T(128)S(1)} %add_multiply_fusion.1), kind=kLoop, calls=%fused_computation.18 | loop fusion | flops 172032 | bytes 147596 | tf_op jit(solution)/shard_map/neg | solution.py:40
  24.8 0.0 copy-start
  24.8 1.2 maximum_maximum_fusion.rband_ref
  26.0 0.0 copy-done
  26.0 4.5 %fusion = (f32[8,16,2048]{2,1,0:T(8,128)}, f32[8,16,2048]{2,1,0:T(8,128)}) fusion(bf16[8,16,2048]{2,1,0:T(8,128)(2,1)S(1)} %copy-done), kind=kLoop, calls=%fused_computation.1 | loop fusion | flops 524288 | bytes 2621440 | tf_op jit(solution)/shard_map/sin | solution.py:395
  30.5 110.9 %shard_map.56 = f32[1,16,2048]{2,1,0:T(8,128)} custom-call(f32[32,2048]{1,0:T(8,128)} %pad_maximum_fusion.u0_ref, f32[8,16,2048]{2,1,0:T(8,128)} %get-tuple-element.10.cos_ref, f32[8,16,2048]{2,1,0:T(8,128)} %get-tuple-element.9.sin_ref, f32[16,2048]{1,0:T(8,128)} %bitcast_convert_fusion.inten_ref, f32[16,3,32,32]{3,2,1,0:T(8,128)} %maximum_maximum_fusion.rband_ref, ...), custom_call_target="tpu_custom_call" | custom-call | tf_op jit(solution)/shard_map/pallas_call | solution.py:275
  141.5 1.6 %copy.8 = f32[1,16,2048]{2,1,0:T(8,128)} copy(f32[1,16,2048]{2,1,0:T(8,128)} %shard_map.56) | data formatting | bytes 262144
  (3 shorter events, 0.0 us)
Async XLA Ops:
  0.7 0.7 copy-start.3
  21.9 0.7 copy-start.2
  22.6 0.7 copy-start.1
  24.8 1.2 copy-start

commit v8 on v7

--- a/solution.py
+++ b/solution.py
@@ -82,7 +82,7 @@
     )
 
 
-CHUNKS = 8
+CHUNKS = 4
 
 
 def chain_kernel(rows, u0_ref, cos_ref, sin_ref, inten_ref, rband_ref, cband_ref,

time: 144 us -> 140 us (0.972)
  Pallas kernels: 125 us -> 121 us
    pallas_call x1, Pallas kernels: 111 us -> 107 us  [run_chain(): pl.pallas_call(functools.partial(chain_kernel, rows), out_shape=jax.Shape...]
where the time goes in v8:
time: 140 us; the launch traced here: 139 us
  Pallas kernels  121 us (86%)
  other arithmetic  11.2 us (8%)
  local copies, waits for them, and re-layouts  4.62 us (3%)
  between operations  2.04 us (1%)
    pallas_call x1, Pallas kernels, run_chain(): pl.pallas_call(functools.partial(chain_kernel, rows), out_shape=jax.Shape...  107 us
    pallas_call x1, Pallas kernels, gather_depth(): pl.pallas_call(functools.partial(gather_kernel, sections), out_shape=(jax...  14.3 us
    sin x1, other arithmetic, body(): jnp.sin(phases)  4.55 us
    unnamed x9, local copies, waits for them, and re-layouts  3.36 us

profile of v8, /device:TPU:2, one launch (start us, length us, event | category | flops | bytes accessed | tf_op | source)
XLA Modules:
  0.0 138.7 jit_solution(12892124910001904128)
XLA Ops:
  0.7 0.0 copy-start.3
  0.7 0.6 copy-done.3
  1.3 0.6 dynamic_slice.8
  3.2 0.6 broadcast_in_dim.15.off_ref
  3.8 1.5 %bitcast_convert_fusion.inten_ref = f32[16,2048]{1,0:T(8,128)} fusion(bf16[2,16,2048]{2,1,0:T(8,128)(2,1)} %param.8, s32[]{:T(128)S(6)} %select_n.31), kind=kLoop, calls=%fused_computation.19 | loop fusion | flops 32768 | bytes 196612 | tf_op jit(solution)/shard_map/convert_element_type | solution.py:391
  5.3 0.6 fusion.7
  5.9 0.7 pad_maximum_fusion.u0_ref
  6.6 14.3 %shard_map.55 = (bf16[8,16,2048]{2,1,0:T(8,128)(2,1)}, f32[8,8,128]{2,1,0:T(8,128)}) custom-call(bf16[1,16,2048]{2,1,0:T(8,128)(2,1)} %vol_ref.1, f32[8,128]{1,0:T(8,128)} %broadcast_in_dim.15.off_ref), custom_call_target="tpu_custom_call" | custom-call | tf_op jit(solution)/shard_map/pallas_call | solution.py:350
  20.9 1.0 convert_reduce_fusion
  21.9 0.0 copy-start.2
  21.9 0.1 rev.3
  22.0 0.6 copy-done.2
  22.6 0.0 copy-start.1
  22.6 0.1 add_multiply_fusion
  22.7 0.6 copy-done.1
  23.2 1.6 %fusion.5 = (f32[16,3,16,16]{3,2,1,0:T(8,128)S(1)}, f32[16,3,16,16]{3,2,1,0:T(8,128)S(1)}, f32[16,3,16,16]{3,2,1,0:T(8,128)S(1)}) fusion(f32[16]{0:T(128)S(1)} %copy-done.1, s32[16]{0:T(128)S(1)} %add_multiply_fusion, s32[3]{0:T(128)S(1)} %add_multiply_fusion.1), kind=kLoop, calls=%fused_computation.18 | loop fusion | flops 172032 | bytes 147596 | tf_op jit(solution)/shard_map/neg | solution.py:40
  24.8 0.0 copy-start
  24.8 1.2 maximum_maximum_fusion.rband_ref
  26.0 0.0 copy-done
  26.0 4.5 %fusion = (f32[8,16,2048]{2,1,0:T(8,128)}, f32[8,16,2048]{2,1,0:T(8,128)}) fusion(bf16[8,16,2048]{2,1,0:T(8,128)(2,1)S(1)} %copy-done), kind=kLoop, calls=%fused_computation.1 | loop fusion | flops 524288 | bytes 2621440 | tf_op jit(solution)/shard_map/sin | solution.py:395
  30.5 106.6 %shard_map.56 = f32[1,16,2048]{2,1,0:T(8,128)} custom-call(f32[32,2048]{1,0:T(8,128)} %pad_maximum_fusion.u0_ref, f32[8,16,2048]{2,1,0:T(8,128)} %get-tuple-element.10.cos_ref, f32[8,16,2048]{2,1,0:T(8,128)} %get-tuple-element.9.sin_ref, f32[16,2048]{1,0:T(8,128)} %bitcast_convert_fusion.inten_ref, f32[16,3,32,32]{3,2,1,0:T(8,128)} %maximum_maximum_fusion.rband_ref, ...), custom_call_target="tpu_custom_call" | custom-call | tf_op jit(solution)/shard_map/pallas_call | solution.py:275
  137.1 1.6 %copy.8 = f32[1,16,2048]{2,1,0:T(8,128)} copy(f32[1,16,2048]{2,1,0:T(8,128)} %shard_map.56) | data formatting | bytes 262144
  (3 shorter events, 0.0 us)
Async XLA Ops:
  0.7 0.7 copy-start.3
  21.9 0.7 copy-start.2
  22.6 0.7 copy-start.1
  24.8 1.2 copy-start

commit v9 on v8

--- a/solution.py
+++ b/solution.py
@@ -42,18 +42,24 @@
     return jnp.concatenate([top, bottom], axis=-2)
 
 
-def row_bands(shifts, height):
-    layers = shifts.shape[0]
-    signs = jnp.concatenate([jnp.ones((layers,), jnp.int32), -jnp.ones((layers,), jnp.int32)])
-    used = jnp.concatenate([shifts, shifts[::-1]]) * signs
-    extent = (2 * layers, 3, height, height)
-    part = lax.broadcasted_iota(jnp.int32, extent, 1)
-    target = lax.broadcasted_iota(jnp.int32, extent, 2)
-    source = lax.broadcasted_iota(jnp.int32, extent, 3) + (part - 1) * height
-    distance = (source - target - used[:, None, None, None]).astype(jnp.float32)
-    real_part, imag_part = kernel_values(distance, HALF, CHIRP_ROW)
-    imag_part = imag_part * signs[:, None, None, None].astype(jnp.float32)
-    return complex_block(real_part, imag_part)
+def band_table(height):
+    offsets = np.arange(-SHIFT, SHIFT + 1)[:, None, None, None]
+    part = np.arange(3)[None, :, None, None]
+    target = np.arange(height)[None, None, :, None]
+    source = np.arange(height)[None, None, None, :] + (part - 1) * height
+    tables = []
+    for sign in (1, -1):
+        distance = (source - target - sign * offsets).astype(np.float64)
+        inside = np.abs(distance) <= HALF
+        phase_arg = CHIRP_ROW / HALF * distance * distance
+        weight = 1.0 / math.sqrt(2 * HALF + 1)
+        real_part = np.where(inside, np.cos(phase_arg) * weight, 0.0)
+        imag_part = np.where(inside, np.sin(phase_arg) * weight, 0.0) * sign
+        top = np.concatenate([real_part, -imag_part], axis=-1)
+        bottom = np.concatenate([imag_part, real_part], axis=-1)
+        block = np.concatenate([top, bottom], axis=-2)
+        tables.append(block.reshape(2 * SHIFT + 1, 3 * 2 * height, 2 * height))
+    return jnp.asarray(np.stack(tables, axis=0).astype(np.float32))
 
 
 def column_bands():
@@ -85,9 +91,11 @@
 CHUNKS = 4
 
 
-def chain_kernel(rows, u0_ref, cos_ref, sin_ref, inten_ref, rband_ref, cband_ref,
+def chain_kernel(rows, sections, u0_ref, vol_ref, off_ref, inten_ref, table_ref, cband_ref,
                  out_ref, terms_ref, partner_ref, field_ref, acc_ref, y_store, b_store, before, after,
-                 bmh_ref, bml_ref, send_dn, send_up, recv_bf, recv_af, send_pair, recv_pair):
+                 bmh_ref, bml_ref, cos_ref, sin_ref, rband_ref, vol_slots, off_slots,
+                 send_dn, send_up, recv_bf, recv_af, send_pair, recv_pair,
+                 send_vol, send_off, recv_vol, recv_off):
     me = lax.axis_index("row")
     section = lax.axis_index("depth")
     partner = section + 1 - 2 * (section % 2)
@@ -108,9 +116,49 @@
     def _():
         pl.semaphore_signal(barrier, 1, device_id={"row": me + 1}, device_id_type=MESH)
 
-    pl.semaphore_signal(barrier, 1, device_id={"depth": partner}, device_id_type=MESH)
+    for step in range(1, sections):
+        peer = (section + step) % sections
+        pl.semaphore_signal(barrier, 1, device_id={"depth": peer}, device_id_type=MESH)
     peers = (me + rows - 1) // rows + (2 * rows - 2 - me) // rows
-    pl.semaphore_wait(barrier, peers + 1)
+    pl.semaphore_wait(barrier, peers + sections - 1)
+
+    def gathers(step, slot):
+        peer = (section + step) % sections
+        vol_copy = pltpu.make_async_remote_copy(
+            src_ref=vol_ref.at[0], dst_ref=vol_slots.at[slot], send_sem=send_vol.at[step],
+            recv_sem=recv_vol.at[slot], device_id={"depth": peer}, device_id_type=MESH)
+        off_copy = pltpu.make_async_remote_copy(
+            src_ref=off_ref, dst_ref=off_slots.at[slot], send_sem=send_off.at[step],
+            recv_sem=recv_off.at[slot], device_id={"depth": peer}, device_id_type=MESH)
+        return vol_copy, off_copy
+
+    for step in range(1, sections):
+        for one in gathers(step, section):
+            one.start()
+    vol_slots[section] = vol_ref[0]
+    off_slots[section] = off_ref[...]
+    part_rows = 2 * height
+
+    def prepare(s):
+        @pl.when(s != section)
+        def _():
+            for one in gathers(1, s):
+                one.wait_recv()
+
+        phase = PHASE_SCALE * vol_slots[s].astype(jnp.float32)
+        cos_ref[s] = jnp.cos(phase)
+        sin_ref[s] = jnp.sin(phase)
+        shift = off_slots[s][0:1, 0:part_rows]
+        forward_band = None
+        adjoint_band = None
+        for i in range(2 * SHIFT + 1):
+            pick = jnp.where(shift == float(i - SHIFT), 1.0, 0.0)
+            f_term = pick * table_ref[0, i]
+            a_term = pick * table_ref[1, i]
+            forward_band = f_term if forward_band is None else forward_band + f_term
+            adjoint_band = a_term if adjoint_band is None else adjoint_band + a_term
+        rband_ref[s] = forward_band
+        rband_ref[2 * layers - 1 - s] = adjoint_band
 
     zero_block = jnp.zeros((2 * height, LANE), jnp.bfloat16)
     for ref in (bmh_ref, bml_ref):
@@ -159,19 +207,19 @@
         @pl.when(has_up)
         def _():
             down.wait_recv()
-            acc_ref[slot, :, cols] += dot3(rband_ref[k, 0], before[k, :, cols])
+            acc_ref[slot, :, cols] += dot3(rband_ref[k, 0:part_rows], before[k, :, cols])
 
         @pl.when(has_dn)
         def _():
             up.wait_recv()
-            acc_ref[slot, :, cols] += dot3(rband_ref[k, 2], after[k, :, cols])
+            acc_ref[slot, :, cols] += dot3(rband_ref[k, 2 * part_rows:3 * part_rows], after[k, :, cols])
 
         return acc_ref[slot, :, cols]
 
     def emit(k, c, store, value):
         cols = pl.ds(c * width, width)
         store[:, cols] = value
-        acc_ref[k % 2, :, cols] = dot3(rband_ref[k, 1], store[:, cols])
+        acc_ref[k % 2, :, cols] = dot3(rband_ref[k, part_rows:2 * part_rows], store[:, cols])
         start(k, c, store)
 
     def write_blocks(c, x):
@@ -223,10 +271,12 @@
         sn = sin_ref[s, :, cols]
         return jnp.concatenate([cs * ar + sn * ai, cs * ai - sn * ar], axis=0)
 
+    prepare(0)
     for c in range(CHUNKS):
         emit(0, c, y_store.at[0], rotated(0, c, u0_ref[:, c * width:(c + 1) * width]))
 
     def forward(k, carry):
+        prepare(k + 1)
         wave(k, y_store.at[k], y_store.at[k + 1], lambda c, a: a,
              lambda c: rotated(k + 1, c, col_chunk(c, 0)))
         return carry
@@ -266,19 +316,25 @@
     exchange.wait_send()
     exchange.wait_recv()
     out_ref[0] = own + partner_ref[...]
-
-
-def run_chain(u0, cosines, sines, intensity, row_band, col_band, rows):
-    layers, height, columns = cosines.shape
+    for step in range(1, sections):
+        for one in gathers(step, section):
+            one.wait_send()
+
+
+def run_chain(u0, index_volume, offsets, intensity, rows, sections):
+    _, height, columns = index_volume.shape
+    layers = sections
     blocks = columns // LANE
     field = (2 * height, columns)
+    off_tile = jnp.broadcast_to(offsets.astype(jnp.float32)[:, None], (8, LANE))
+    plane = (layers, height, columns)
     return pl.pallas_call(
-        functools.partial(chain_kernel, rows),
+        functools.partial(chain_kernel, rows, sections),
         out_shape=jax.ShapeDtypeStruct((1, height, columns), jnp.float32),
         in_specs=[pl.BlockSpec(memory_space=pltpu.VMEM)] * 6,
         out_specs=pl.BlockSpec(memory_space=pltpu.VMEM),
         scratch_shapes=[
-            pltpu.VMEM((layers, height, columns), jnp.float32),
+            pltpu.VMEM(plane, jnp.float32),
             pltpu.VMEM((height, columns), jnp.float32),
             pltpu.VMEM(field, jnp.float32),
             pltpu.VMEM((2,) + field, jnp.float32),
@@ -288,16 +344,25 @@
             pltpu.VMEM((2 * layers,) + field, jnp.float32),
             pltpu.VMEM((blocks + 2, 2 * height, LANE), jnp.bfloat16),
             pltpu.VMEM((blocks + 2, 2 * height, LANE), jnp.bfloat16),
+            pltpu.VMEM(plane, jnp.float32),
+            pltpu.VMEM(plane, jnp.float32),
+            pltpu.VMEM((2 * layers, 3 * 2 * height, 2 * height), jnp.float32),
+            pltpu.VMEM(plane, index_volume.dtype),
+            pltpu.VMEM((sections, 8, LANE), jnp.float32),
             pltpu.SemaphoreType.DMA((2 * layers * CHUNKS,)),
             pltpu.SemaphoreType.DMA((2 * layers * CHUNKS,)),
             pltpu.SemaphoreType.DMA((2 * layers * CHUNKS,)),
             pltpu.SemaphoreType.DMA((2 * layers * CHUNKS,)),
             pltpu.SemaphoreType.DMA,
             pltpu.SemaphoreType.DMA,
+            pltpu.SemaphoreType.DMA((sections,)),
+            pltpu.SemaphoreType.DMA((sections,)),
+            pltpu.SemaphoreType.DMA((sections,)),
+            pltpu.SemaphoreType.DMA((sections,)),
         ],
         compiler_params=pltpu.CompilerParams(
             collective_id=0, has_side_effects=True, vmem_limit_bytes=56 * 1024 * 1024),
-    )(u0, cosines, sines, intensity, row_band, col_band)
+    )(u0, index_volume, off_tile, intensity, band_table(height), column_bands())
 
 
 def gather_kernel(sections, vol_ref, off_ref, vol_out, off_out, vol_slots, off_slots,
@@ -386,14 +451,10 @@
     total_rows = height * rows
     angle_count = angles.shape[0]
     angle_no = section_no % angle_count
-    volume, shift_tiles = gather_depth(index_volume, offsets, sections)
-    shifts = shift_tiles[:, 0, 0].astype(jnp.int32)
     intensity = lax.dynamic_index_in_dim(measured, angle_no, 0, keepdims=False).astype(jnp.float32)
     angle = lax.dynamic_index_in_dim(angles, angle_no, 0, keepdims=False)
     incident = plane_wave(angle, row_start, height, columns, total_rows, columns)
-    phases = PHASE_SCALE * volume.astype(jnp.float32)
-    return run_chain(incident, jnp.cos(phases), jnp.sin(phases), intensity,
-                     row_bands(shifts, height), column_bands(), rows)
+    return run_chain(incident, index_volume, offsets, intensity, rows, sections)
 
 
 def solution(mesh):

time: 140 us -> 124 us (0.89)
  other arithmetic: 11.2 us -> 1.97 us
  Pallas kernels: 121 us -> 115 us
    pallas_call x2 -> x1, Pallas kernels: 121 us -> 115 us  [run_chain(): pl.pallas_call(functools.partial(chain_kernel, rows, sections), out_shape...]
    sin x1 -> x0, other arithmetic: 4.55 us -> none  [body(): jnp.sin(phases)]
    neg x1 -> x0, other arithmetic: 1.59 us -> none  [complex_block(): top = jnp.concatenate([real_part, -imag_part], axis=-1)]
    unnamed x9 -> x5, local copies, waits for them, and re-layouts: 3.36 us -> 2.47 us
where the time goes in v9:
time: 124 us; the launch traced here: 122 us
  Pallas kernels  115 us (93%)
  local copies, waits for them, and re-layouts  3.65 us (3%)
  between operations  2.01 us (2%)
  other arithmetic  1.97 us (2%)
    pallas_call x1, Pallas kernels, run_chain(): pl.pallas_call(functools.partial(chain_kernel, rows, sections), out_shape...  115 us

profile of v9, /device:TPU:2, one launch (start us, length us, event | category | flops | bytes accessed | tf_op | source)
XLA Modules:
  0.0 122.3 jit_solution(15556307964509063656)
XLA Ops:
  0.0 0.0 copy-start.1
  0.0 0.7 copy-done.1
  0.7 0.6 dynamic_slice.8
  2.6 0.6 fusion.4
  3.2 0.0 copy-start
  3.2 0.7 pad_maximum_fusion.u0_ref
  3.9 0.2 copy-done
  4.1 0.7 bitcast_convert_fusion.inten_ref
  5.5 0.6 broadcast_in_dim.9.off_ref
  6.0 114.6 %shard_map.64 = f32[1,16,2048]{2,1,0:T(8,128)} custom-call(f32[32,2048]{1,0:T(8,128)} %pad_maximum_fusion.u0_ref, bf16[1,16,2048]{2,1,0:T(8,128)(2,1)} %vol_ref.1, f32[8,128]{1,0:T(8,128)} %broadcast_in_dim.9.off_ref, f32[16,2048]{1,0:T(8,128)} %bitcast_convert_fusion.inten_ref, f32[2,9,96,32]{3,2,1,0:T(8,128)} %constant.73.clone.table_ref, ...), custom_call_target="tpu_custom_call" | custom-call | tf_op jit(solution)/shard_map/pallas_call | solution.py:331
  120.7 1.6 %copy.9 = f32[1,16,2048]{2,1,0:T(8,128)} copy(f32[1,16,2048]{2,1,0:T(8,128)} %shard_map.64) | data formatting | bytes 262144
  (2 shorter events, 0.0 us)
Async XLA Ops:
  0.0 0.7 copy-start.1
  3.2 1.0 copy-start

commit v10 on v9

--- a/solution.py
+++ b/solution.py
@@ -228,8 +228,10 @@
             bmh_ref[c * per_chunk + b + 1] = high[:, b * LANE:(b + 1) * LANE]
             bml_ref[c * per_chunk + b + 1] = low[:, b * LANE:(b + 1) * LANE]
 
-    def wave(k, store, store_next, finish_chunk, make_chunk):
+    def wave(k, store, store_next, finish_chunk, make_chunk, early=None):
         for c in range(CHUNKS):
+            if c == CHUNKS - 1 and early is not None:
+                early()
             write_blocks(c, finish_chunk(c, halo(k, c, store)))
             if c >= 1:
                 emit(k + 1, c - 1, store_next, make_chunk(c - 1))
@@ -274,11 +276,16 @@
     prepare(0)
     for c in range(CHUNKS):
         emit(0, c, y_store.at[0], rotated(0, c, u0_ref[:, c * width:(c + 1) * width]))
+    prepare(1)
 
     def forward(k, carry):
-        prepare(k + 1)
+        def early():
+            @pl.when(k + 2 < layers)
+            def _():
+                prepare(k + 2)
+
         wave(k, y_store.at[k], y_store.at[k + 1], lambda c, a: a,
-             lambda c: rotated(k + 1, c, col_chunk(c, 0)))
+             lambda c: rotated(k + 1, c, col_chunk(c, 0)), early)
         return carry
 
     lax.fori_loop(0, layers - 1, forward, 0)

time: 124 us -> 127 us (1.024)
  Pallas kernels: 115 us -> 118 us
    pallas_call x1, Pallas kernels: 115 us -> 118 us  [run_chain(): pl.pallas_call(functools.partial(chain_kernel, rows, sections), out_shape...]
where the time goes in v10:
time: 127 us; the launch traced here: 126 us
  Pallas kernels  118 us (93%)
  local copies, waits for them, and re-layouts  3.65 us (3%)
  between operations  2.01 us (2%)
  other arithmetic  1.97 us (2%)
    pallas_call x1, Pallas kernels, run_chain(): pl.pallas_call(functools.partial(chain_kernel, rows, sections), out_shape...  118 us

profile of v10, /device:TPU:2, one launch (start us, length us, event | category | flops | bytes accessed | tf_op | source)
XLA Modules:
  0.0 125.7 jit_solution(7650985361925211209)
XLA Ops:
  0.0 0.0 copy-start.1
  0.0 0.7 copy-done.1
  0.7 0.6 dynamic_slice.8
  2.6 0.6 fusion.4
  3.2 0.0 copy-start
  3.2 0.7 pad_maximum_fusion.u0_ref
  3.9 0.2 copy-done
  4.1 0.7 bitcast_convert_fusion.inten_ref
  5.5 0.6 broadcast_in_dim.9.off_ref
  6.0 118.0 %shard_map.64 = f32[1,16,2048]{2,1,0:T(8,128)} custom-call(f32[32,2048]{1,0:T(8,128)} %pad_maximum_fusion.u0_ref, bf16[1,16,2048]{2,1,0:T(8,128)(2,1)} %vol_ref.1, f32[8,128]{1,0:T(8,128)} %broadcast_in_dim.9.off_ref, f32[16,2048]{1,0:T(8,128)} %bitcast_convert_fusion.inten_ref, f32[2,9,96,32]{3,2,1,0:T(8,128)} %constant.73.clone.table_ref, ...), custom_call_target="tpu_custom_call" | custom-call | tf_op jit(solution)/shard_map/pallas_call | solution.py:338
  124.1 1.6 %copy.9 = f32[1,16,2048]{2,1,0:T(8,128)} copy(f32[1,16,2048]{2,1,0:T(8,128)} %shard_map.64) | data formatting | bytes 262144
  (2 shorter events, 0.0 us)
Async XLA Ops:
  0.0 0.7 copy-start.1
  3.2 1.0 copy-start

commit v11 on v9

--- a/solution.py
+++ b/solution.py
@@ -77,8 +77,7 @@
     return jnp.asarray(np.stack([forward, adjoint], axis=0).astype(np.float32))
 
 
-def dot3(a, x):
-    a_high, a_low = split_bf16(a)
+def dot3(a_high, a_low, x):
     x_high, x_low = split_bf16(x)
     f32 = jnp.float32
     return (
@@ -95,7 +94,7 @@
                  out_ref, terms_ref, partner_ref, field_ref, acc_ref, y_store, b_store, before, after,
                  bmh_ref, bml_ref, cos_ref, sin_ref, rband_ref, vol_slots, off_slots,
                  send_dn, send_up, recv_bf, recv_af, send_pair, recv_pair,
-                 send_vol, send_off, recv_vol, recv_off):
+                 send_vol, send_off, recv_vol, recv_off, chb_ref, clb_ref, rbh_ref, rbl_ref):
     me = lax.axis_index("row")
     section = lax.axis_index("depth")
     partner = section + 1 - 2 * (section % 2)
@@ -157,9 +156,16 @@
             a_term = pick * table_ref[1, i]
             forward_band = f_term if forward_band is None else forward_band + f_term
             adjoint_band = a_term if adjoint_band is None else adjoint_band + a_term
-        rband_ref[s] = forward_band
-        rband_ref[2 * layers - 1 - s] = adjoint_band
-
+        high, low = split_bf16(forward_band)
+        rbh_ref[s] = high
+        rbl_ref[s] = low
+        high, low = split_bf16(adjoint_band)
+        rbh_ref[2 * layers - 1 - s] = high
+        rbl_ref[2 * layers - 1 - s] = low
+
+    high, low = split_bf16(cband_ref[...])
+    chb_ref[...] = high
+    clb_ref[...] = low
     zero_block = jnp.zeros((2 * height, LANE), jnp.bfloat16)
     for ref in (bmh_ref, bml_ref):
         ref[0] = zero_block
@@ -207,19 +213,19 @@
         @pl.when(has_up)
         def _():
             down.wait_recv()
-            acc_ref[slot, :, cols] += dot3(rband_ref[k, 0:part_rows], before[k, :, cols])
+            acc_ref[slot, :, cols] += dot3(rbh_ref[k, 0:part_rows], rbl_ref[k, 0:part_rows], before[k, :, cols])
 
         @pl.when(has_dn)
         def _():
             up.wait_recv()
-            acc_ref[slot, :, cols] += dot3(rband_ref[k, 2 * part_rows:3 * part_rows], after[k, :, cols])
+            acc_ref[slot, :, cols] += dot3(rbh_ref[k, 2 * part_rows:3 * part_rows], rbl_ref[k, 2 * part_rows:3 * part_rows], after[k, :, cols])
 
         return acc_ref[slot, :, cols]
 
     def emit(k, c, store, value):
         cols = pl.ds(c * width, width)
         store[:, cols] = value
-        acc_ref[k % 2, :, cols] = dot3(rband_ref[k, part_rows:2 * part_rows], store[:, cols])
+        acc_ref[k % 2, :, cols] = dot3(rbh_ref[k, part_rows:2 * part_rows], rbl_ref[k, part_rows:2 * part_rows], store[:, cols])
         start(k, c, store)
 
     def write_blocks(c, x):
@@ -243,7 +249,8 @@
         for t in range(3):
             xh = bmh_ref[first + t:first + t + per_chunk].reshape(per_chunk * 2 * height, LANE)
             xl = bml_ref[first + t:first + t + per_chunk].reshape(per_chunk * 2 * height, LANE)
-            wh, wl = split_bf16(cband_ref[which, t])
+            wh = chb_ref[which, t]
+            wl = clb_ref[which, t]
             part = (jnp.dot(xh, wh, preferred_element_type=f32) + jnp.dot(xh, wl, preferred_element_type=f32)
                     + jnp.dot(xl, wh, preferred_element_type=f32))
             total = part if total is None else total + part
@@ -359,6 +366,10 @@
             pltpu.SemaphoreType.DMA((sections,)),
             pltpu.SemaphoreType.DMA((sections,)),
             pltpu.SemaphoreType.DMA((sections,)),
+            pltpu.VMEM((2, 3, LANE, 2 * LANE), jnp.bfloat16),
+            pltpu.VMEM((2, 3, LANE, 2 * LANE), jnp.bfloat16),
+            pltpu.VMEM((2 * layers, 3 * 2 * height, 2 * height), jnp.bfloat16),
+            pltpu.VMEM((2 * layers, 3 * 2 * height, 2 * height), jnp.bfloat16),
         ],
         compiler_params=pltpu.CompilerParams(
             collective_id=0, has_side_effects=True, vmem_limit_bytes=56 * 1024 * 1024),
@@ -366,7 +377,7 @@
 
 
 def gather_kernel(sections, vol_ref, off_ref, vol_out, off_out, vol_slots, off_slots,
-                  send_vol, send_off, recv_vol, recv_off):
+                  send_vol, send_off, recv_vol, recv_off, chb_ref, clb_ref, rbh_ref, rbl_ref):
     me = lax.axis_index("depth")
     barrier = pltpu.get_barrier_semaphore()
     for step in range(1, sections):
@@ -425,6 +436,10 @@
             pltpu.SemaphoreType.DMA((sections,)),
             pltpu.SemaphoreType.DMA((sections,)),
             pltpu.SemaphoreType.DMA((sections,)),
+            pltpu.VMEM((2, 3, LANE, 2 * LANE), jnp.bfloat16),
+            pltpu.VMEM((2, 3, LANE, 2 * LANE), jnp.bfloat16),
+            pltpu.VMEM((2 * layers, 3 * 2 * height, 2 * height), jnp.bfloat16),
+            pltpu.VMEM((2 * layers, 3 * 2 * height, 2 * height), jnp.bfloat16),
         ],
         compiler_params=pltpu.CompilerParams(collective_id=1, has_side_effects=True),
     )(index_volume, off_tile)

time: 124 us -> 124 us (level)
  no operation moved by 1% of the time
where the time goes in v11:
time: 124 us; the launch traced here: 122 us
  Pallas kernels  114 us (92%)
  local copies, waits for them, and re-layouts  3.65 us (3%)
  between operations  2.01 us (2%)
  other arithmetic  1.97 us (2%)
    pallas_call x1, Pallas kernels, run_chain(): pl.pallas_call(functools.partial(chain_kernel, rows, sections), out_shape...  114 us

profile of v11, /device:TPU:2, one launch (start us, length us, event | category | flops | bytes accessed | tf_op | source)
XLA Modules:
  0.0 121.9 jit_solution(12335934203036030689)
XLA Ops:
  0.0 0.0 copy-start.1
  0.0 0.7 copy-done.1
  0.7 0.6 dynamic_slice.8
  2.6 0.6 fusion.4
  3.2 0.0 copy-start
  3.2 0.7 pad_maximum_fusion.u0_ref
  3.9 0.2 copy-done
  4.1 0.7 bitcast_convert_fusion.inten_ref
  5.5 0.6 broadcast_in_dim.9.off_ref
  6.0 114.3 %shard_map.64 = f32[1,16,2048]{2,1,0:T(8,128)} custom-call(f32[32,2048]{1,0:T(8,128)} %pad_maximum_fusion.u0_ref, bf16[1,16,2048]{2,1,0:T(8,128)(2,1)} %vol_ref.1, f32[8,128]{1,0:T(8,128)} %broadcast_in_dim.9.off_ref, f32[16,2048]{1,0:T(8,128)} %bitcast_convert_fusion.inten_ref, f32[2,9,96,32]{3,2,1,0:T(8,128)} %constant.73.clone.table_ref, ...), custom_call_target="tpu_custom_call" | custom-call | tf_op jit(solution)/shard_map/pallas_call | solution.py:338
  120.3 1.6 %copy.9 = f32[1,16,2048]{2,1,0:T(8,128)} copy(f32[1,16,2048]{2,1,0:T(8,128)} %shard_map.64) | data formatting | bytes 262144
  (2 shorter events, 0.0 us)
Async XLA Ops:
  0.0 0.7 copy-start.1
  3.2 1.0 copy-start

commit v12 on v11

--- a/solution.py
+++ b/solution.py
@@ -80,11 +80,9 @@
 def dot3(a_high, a_low, x):
     x_high, x_low = split_bf16(x)
     f32 = jnp.float32
-    return (
-        jnp.dot(a_high, x_high, preferred_element_type=f32)
-        + jnp.dot(a_high, x_low, preferred_element_type=f32)
-        + jnp.dot(a_low, x_high, preferred_element_type=f32)
-    )
+    rows = a_high.shape[0]
+    both = jnp.dot(jnp.concatenate([a_high, a_low], axis=0), x_high, preferred_element_type=f32)
+    return both[:rows] + both[rows:] + jnp.dot(a_high, x_low, preferred_element_type=f32)
 
 
 CHUNKS = 4
@@ -251,8 +249,9 @@
             xl = bml_ref[first + t:first + t + per_chunk].reshape(per_chunk * 2 * height, LANE)
             wh = chb_ref[which, t]
             wl = clb_ref[which, t]
-            part = (jnp.dot(xh, wh, preferred_element_type=f32) + jnp.dot(xh, wl, preferred_element_type=f32)
-                    + jnp.dot(xl, wh, preferred_element_type=f32))
+            count = xh.shape[0]
+            both = jnp.dot(jnp.concatenate([xh, xl], axis=0), wh, preferred_element_type=f32)
+            part = both[:count] + both[count:] + jnp.dot(xh, wl, preferred_element_type=f32)
             total = part if total is None else total + part
         total = total.reshape(per_chunk, 2 * height, 2 * LANE)
         real_part = total[:, :height, :LANE] - total[:, height:, LANE:]

time: 124 us -> 123 us (level)
  no operation moved by 1% of the time
where the time goes in v12:
time: 123 us; the launch traced here: 121 us
  Pallas kernels  114 us (93%)
  local copies, waits for them, and re-layouts  3.65 us (3%)
  between operations  2.01 us (2%)
  other arithmetic  1.97 us (2%)
    pallas_call x1, Pallas kernels, run_chain(): pl.pallas_call(functools.partial(chain_kernel, rows, sections), out_shape...  114 us
    unnamed x5, local copies, waits for them, and re-layouts  2.47 us

profile of v12, /device:TPU:2, one launch (start us, length us, event | category | flops | bytes accessed | tf_op | source)
XLA Modules:
  0.0 121.1 jit_solution(12805328856632210783)
XLA Ops:
  0.0 0.0 copy-start.1
  0.0 0.7 copy-done.1
  0.7 0.6 dynamic_slice.8
  2.6 0.6 fusion.4
  3.2 0.0 copy-start
  3.2 0.7 pad_maximum_fusion.u0_ref
  3.9 0.2 copy-done
  4.1 0.7 bitcast_convert_fusion.inten_ref
  5.5 0.6 broadcast_in_dim.9.off_ref
  6.0 113.5 %shard_map.64 = f32[1,16,2048]{2,1,0:T(8,128)} custom-call(f32[32,2048]{1,0:T(8,128)} %pad_maximum_fusion.u0_ref, bf16[1,16,2048]{2,1,0:T(8,128)(2,1)} %vol_ref.1, f32[8,128]{1,0:T(8,128)} %broadcast_in_dim.9.off_ref, f32[16,2048]{1,0:T(8,128)} %bitcast_convert_fusion.inten_ref, f32[2,9,96,32]{3,2,1,0:T(8,128)} %constant.73.clone.table_ref, ...), custom_call_target="tpu_custom_call" | custom-call | tf_op jit(solution)/shard_map/pallas_call | solution.py:337
  119.6 1.6 %copy.9 = f32[1,16,2048]{2,1,0:T(8,128)} copy(f32[1,16,2048]{2,1,0:T(8,128)} %shard_map.64) | data formatting | bytes 262144
  (2 shorter events, 0.0 us)
Async XLA Ops:
  0.0 0.7 copy-start.1
  3.2 1.0 copy-start

commit v13 on v12

--- a/solution.py
+++ b/solution.py
@@ -296,7 +296,7 @@
     u = field_ref[...]
     ur = u[:height]
     ui = u[height:]
-    errors = ur * ur + ui * ui - inten_ref[...]
+    errors = ur * ur + ui * ui - inten_ref[section % inten_ref.shape[0]].astype(jnp.float32)
     field_ref[...] = jnp.concatenate([2.0 * errors * ur, 2.0 * errors * ui], axis=0)
     for c in range(CHUNKS):
         write_blocks(c, field_ref[:, c * width:(c + 1) * width])
@@ -465,10 +465,9 @@
     total_rows = height * rows
     angle_count = angles.shape[0]
     angle_no = section_no % angle_count
-    intensity = lax.dynamic_index_in_dim(measured, angle_no, 0, keepdims=False).astype(jnp.float32)
     angle = lax.dynamic_index_in_dim(angles, angle_no, 0, keepdims=False)
     incident = plane_wave(angle, row_start, height, columns, total_rows, columns)
-    return run_chain(incident, index_volume, offsets, intensity, rows, sections)
+    return run_chain(incident, index_volume, offsets, measured, rows, sections)
 
 
 def solution(mesh):

time: 123 us -> 122 us (level)
    unnamed x5 -> x3, local copies, waits for them, and re-layouts: 2.47 us -> 2.22 us
where the time goes in v13:
time: 122 us; the launch traced here: 120 us
  Pallas kernels  113 us (93%)
  local copies, waits for them, and re-layouts  3.4 us (3%)
  between operations  2 us (2%)
  other arithmetic  1.31 us (1%)
    pallas_call x1, Pallas kernels, run_chain(): pl.pallas_call(functools.partial(chain_kernel, rows, sections), out_shape...  113 us

profile of v13, /device:TPU:2, one launch (start us, length us, event | category | flops | bytes accessed | tf_op | source)
XLA Modules:
  0.0 120.2 jit_solution(9954521850133908978)
XLA Ops:
  0.0 0.0 copy-start
  0.0 0.7 copy-done
  0.7 0.6 dynamic_slice.4
  2.6 0.6 fusion.4
  3.2 0.7 pad_maximum_fusion.u0_ref
  4.5 0.6 broadcast_in_dim.9.off_ref
  5.1 113.5 %shard_map.64 = f32[1,16,2048]{2,1,0:T(8,128)} custom-call(f32[32,2048]{1,0:T(8,128)} %pad_maximum_fusion.u0_ref, bf16[1,16,2048]{2,1,0:T(8,128)(2,1)} %vol_ref.1, f32[8,128]{1,0:T(8,128)} %broadcast_in_dim.9.off_ref, bf16[2,16,2048]{2,1,0:T(8,128)(2,1)} %inten_ref.1, f32[2,9,96,32]{3,2,1,0:T(8,128)} %constant.69.clone.table_ref, ...), custom_call_target="tpu_custom_call" | custom-call | tf_op jit(solution)/shard_map/pallas_call | solution.py:337
  118.6 1.6 %copy.9 = f32[1,16,2048]{2,1,0:T(8,128)} copy(f32[1,16,2048]{2,1,0:T(8,128)} %shard_map.64) | data formatting | bytes 262144
  (2 shorter events, 0.0 us)
Async XLA Ops:
  0.0 0.7 copy-start

commit v14 on v13

--- a/solution.py
+++ b/solution.py
@@ -92,7 +92,7 @@
                  out_ref, terms_ref, partner_ref, field_ref, acc_ref, y_store, b_store, before, after,
                  bmh_ref, bml_ref, cos_ref, sin_ref, rband_ref, vol_slots, off_slots,
                  send_dn, send_up, recv_bf, recv_af, send_pair, recv_pair,
-                 send_vol, send_off, recv_vol, recv_off, chb_ref, clb_ref, rbh_ref, rbl_ref):
+                 send_vol, send_off, recv_vol, recv_off, chb_ref, clb_ref, rbh_ref, rbl_ref, own_off):
     me = lax.axis_index("row")
     section = lax.axis_index("depth")
     partner = section + 1 - 2 * (section % 2)
@@ -103,6 +103,7 @@
     has_up = me > 0
     has_dn = me < rows - 1
 
+    own_off[...] = jnp.full(own_off.shape, off_ref[0].astype(jnp.float32), jnp.float32)
     barrier = pltpu.get_barrier_semaphore()
 
     @pl.when(has_up)
@@ -125,7 +126,7 @@
             src_ref=vol_ref.at[0], dst_ref=vol_slots.at[slot], send_sem=send_vol.at[step],
             recv_sem=recv_vol.at[slot], device_id={"depth": peer}, device_id_type=MESH)
         off_copy = pltpu.make_async_remote_copy(
-            src_ref=off_ref, dst_ref=off_slots.at[slot], send_sem=send_off.at[step],
+            src_ref=own_off, dst_ref=off_slots.at[slot], send_sem=send_off.at[step],
             recv_sem=recv_off.at[slot], device_id={"depth": peer}, device_id_type=MESH)
         return vol_copy, off_copy
 
@@ -133,7 +134,7 @@
         for one in gathers(step, section):
             one.start()
     vol_slots[section] = vol_ref[0]
-    off_slots[section] = off_ref[...]
+    off_slots[section] = own_off[...]
     part_rows = 2 * height
 
     def prepare(s):
@@ -332,12 +333,12 @@
     layers = sections
     blocks = columns // LANE
     field = (2 * height, columns)
-    off_tile = jnp.broadcast_to(offsets.astype(jnp.float32)[:, None], (8, LANE))
     plane = (layers, height, columns)
     return pl.pallas_call(
         functools.partial(chain_kernel, rows, sections),
         out_shape=jax.ShapeDtypeStruct((1, height, columns), jnp.float32),
-        in_specs=[pl.BlockSpec(memory_space=pltpu.VMEM)] * 6,
+        in_specs=[pl.BlockSpec(memory_space=pltpu.VMEM)] * 2 + [pl.BlockSpec(memory_space=pltpu.SMEM)]
+        + [pl.BlockSpec(memory_space=pltpu.VMEM)] * 3,
         out_specs=pl.BlockSpec(memory_space=pltpu.VMEM),
         scratch_shapes=[
             pltpu.VMEM(plane, jnp.float32),
@@ -369,79 +370,11 @@
             pltpu.VMEM((2, 3, LANE, 2 * LANE), jnp.bfloat16),
             pltpu.VMEM((2 * layers, 3 * 2 * height, 2 * height), jnp.bfloat16),
             pltpu.VMEM((2 * layers, 3 * 2 * height, 2 * height), jnp.bfloat16),
+            pltpu.VMEM((8, LANE), jnp.float32),
         ],
         compiler_params=pltpu.CompilerParams(
             collective_id=0, has_side_effects=True, vmem_limit_bytes=56 * 1024 * 1024),
-    )(u0, index_volume, off_tile, intensity, band_table(height), column_bands())
-
-
-def gather_kernel(sections, vol_ref, off_ref, vol_out, off_out, vol_slots, off_slots,
-                  send_vol, send_off, recv_vol, recv_off, chb_ref, clb_ref, rbh_ref, rbl_ref):
-    me = lax.axis_index("depth")
-    barrier = pltpu.get_barrier_semaphore()
-    for step in range(1, sections):
-        peer = (me + step) % sections
-        pl.semaphore_signal(barrier, 1, device_id={"depth": peer}, device_id_type=MESH)
-    pl.semaphore_wait(barrier, sections - 1)
-
-    def copies(step):
-        peer = (me + step) % sections
-        source = (me + sections - step) % sections
-        out_vol = pltpu.make_async_remote_copy(
-            src_ref=vol_ref.at[0], dst_ref=vol_slots.at[me], send_sem=send_vol.at[step],
-            recv_sem=recv_vol.at[me], device_id={"depth": peer}, device_id_type=MESH)
-        out_off = pltpu.make_async_remote_copy(
-            src_ref=off_ref, dst_ref=off_slots.at[me], send_sem=send_off.at[step],
-            recv_sem=recv_off.at[me], device_id={"depth": peer}, device_id_type=MESH)
-        in_vol = pltpu.make_async_remote_copy(
-            src_ref=vol_ref.at[0], dst_ref=vol_slots.at[source], send_sem=send_vol.at[step],
-            recv_sem=recv_vol.at[source], device_id={"depth": peer}, device_id_type=MESH)
-        in_off = pltpu.make_async_remote_copy(
-            src_ref=off_ref, dst_ref=off_slots.at[source], send_sem=send_off.at[step],
-            recv_sem=recv_off.at[source], device_id={"depth": peer}, device_id_type=MESH)
-        return out_vol, out_off, in_vol, in_off
-
-    for step in range(1, sections):
-        out_vol, out_off, _, _ = copies(step)
-        out_vol.start()
-        out_off.start()
-    vol_slots[me] = vol_ref[0]
-    off_slots[me] = off_ref[...]
-    for step in range(1, sections):
-        out_vol, out_off, in_vol, in_off = copies(step)
-        in_vol.wait_recv()
-        in_off.wait_recv()
-        out_vol.wait_send()
-        out_off.wait_send()
-    vol_out[...] = vol_slots[...]
-    off_out[...] = off_slots[...]
-
-
-def gather_depth(index_volume, offsets, sections):
-    _, height, columns = index_volume.shape
-    off_tile = jnp.broadcast_to(offsets.astype(jnp.float32)[:, None], (8, LANE))
-    vol_shape = (sections, height, columns)
-    off_shape = (sections, 8, LANE)
-    return pl.pallas_call(
-        functools.partial(gather_kernel, sections),
-        out_shape=(jax.ShapeDtypeStruct(vol_shape, index_volume.dtype),
-                   jax.ShapeDtypeStruct(off_shape, jnp.float32)),
-        in_specs=[pl.BlockSpec(memory_space=pltpu.VMEM)] * 2,
-        out_specs=(pl.BlockSpec(memory_space=pltpu.VMEM),) * 2,
-        scratch_shapes=[
-            pltpu.VMEM(vol_shape, index_volume.dtype),
-            pltpu.VMEM(off_shape, jnp.float32),
-            pltpu.SemaphoreType.DMA((sections,)),
-            pltpu.SemaphoreType.DMA((sections,)),
-            pltpu.SemaphoreType.DMA((sections,)),
-            pltpu.SemaphoreType.DMA((sections,)),
-            pltpu.VMEM((2, 3, LANE, 2 * LANE), jnp.bfloat16),
-            pltpu.VMEM((2, 3, LANE, 2 * LANE), jnp.bfloat16),
-            pltpu.VMEM((2 * layers, 3 * 2 * height, 2 * height), jnp.bfloat16),
-            pltpu.VMEM((2 * layers, 3 * 2 * height, 2 * height), jnp.bfloat16),
-        ],
-        compiler_params=pltpu.CompilerParams(collective_id=1, has_side_effects=True),
-    )(index_volume, off_tile)
+    )(u0, index_volume, offsets, intensity, band_table(height), column_bands())
 
 
 def plane_wave(angle, row_start, height, columns, total_rows, total_cols):

time: 122 us -> 121 us (level)
  no operation moved by 1% of the time
where the time goes in v14:
time: 121 us; the launch traced here: 120 us
  Pallas kernels  114 us (94%)
  local copies, waits for them, and re-layouts  2.81 us (2%)
  between operations  2 us (2%)
  other arithmetic  1.31 us (1%)
    pallas_call x1, Pallas kernels, run_chain(): pl.pallas_call(functools.partial(chain_kernel, rows, sections), out_shape...  114 us

profile of v14, /device:TPU:2, one launch (start us, length us, event | category | flops | bytes accessed | tf_op | source)
XLA Modules:
  0.0 119.7 jit_solution(11359665508324556607)
XLA Ops:
  0.0 0.0 copy-start
  0.0 0.7 copy-done
  0.7 0.6 dynamic_slice.4
  2.6 0.6 fusion.4
  3.2 0.7 pad_maximum_fusion.u0_ref
  4.5 113.6 %shard_map.64 = f32[1,16,2048]{2,1,0:T(8,128)} custom-call(f32[32,2048]{1,0:T(8,128)} %pad_maximum_fusion.u0_ref, bf16[1,16,2048]{2,1,0:T(8,128)(2,1)} %vol_ref.1, s32[1]{0:T(128)S(6)} %copy.8.off_ref, bf16[2,16,2048]{2,1,0:T(8,128)(2,1)} %inten_ref.1, f32[2,9,96,32]{3,2,1,0:T(8,128)} %constant.69.clone.table_ref, f32[2,3,128,256]{3,2,1,0:T(8,128)} %constant.70.clone.cband_ref), custom_call_target="tpu_custom_call" | custom-call | tf_op jit(solution)/shard_map/pallas_call | solution.py:337
  118.1 1.6 %copy.9 = f32[1,16,2048]{2,1,0:T(8,128)} copy(f32[1,16,2048]{2,1,0:T(8,128)} %shard_map.64) | data formatting | bytes 262144
  (2 shorter events, 0.0 us)
Async XLA Ops:
  0.0 0.7 copy-start

commit v15 on v14

--- a/solution.py
+++ b/solution.py
@@ -88,7 +88,7 @@
 CHUNKS = 4
 
 
-def chain_kernel(rows, sections, u0_ref, vol_ref, off_ref, inten_ref, table_ref, cband_ref,
+def chain_kernel(rows, sections, angle_ref, vol_ref, off_ref, inten_ref, table_ref, cband_ref,
                  out_ref, terms_ref, partner_ref, field_ref, acc_ref, y_store, b_store, before, after,
                  bmh_ref, bml_ref, cos_ref, sin_ref, rband_ref, vol_slots, off_slots,
                  send_dn, send_up, recv_bf, recv_af, send_pair, recv_pair,
@@ -104,6 +104,17 @@
     has_dn = me < rows - 1
 
     own_off[...] = jnp.full(own_off.shape, off_ref[0].astype(jnp.float32), jnp.float32)
+    angle = angle_ref[section % angle_ref.shape[0]]
+    across = angle - TILTS // 2
+    along = lax.rem(3 * angle, TILTS) - TILTS // 2
+    shape2 = (cos_ref.shape[1], cos_ref.shape[2])
+    period = shape2[0] * rows * shape2[1]
+    row_index = me * shape2[0] + lax.broadcasted_iota(jnp.int32, shape2, 0)
+    col_index = lax.broadcasted_iota(jnp.int32, shape2, 1)
+    cycles = lax.rem(across * col_index * (shape2[0] * rows) + along * row_index * shape2[1], period)
+    cycles = jnp.where(cycles < 0, cycles + period, cycles)
+    wave_arg = 2.0 * math.pi / period * cycles.astype(jnp.float32)
+    field_ref[...] = jnp.concatenate([jnp.cos(wave_arg), jnp.sin(wave_arg)], axis=0)
     barrier = pltpu.get_barrier_semaphore()
 
     @pl.when(has_up)
@@ -280,7 +291,7 @@
 
     prepare(0)
     for c in range(CHUNKS):
-        emit(0, c, y_store.at[0], rotated(0, c, u0_ref[:, c * width:(c + 1) * width]))
+        emit(0, c, y_store.at[0], rotated(0, c, field_ref[:, c * width:(c + 1) * width]))
 
     def forward(k, carry):
         prepare(k + 1)
@@ -328,7 +339,7 @@
             one.wait_send()
 
 
-def run_chain(u0, index_volume, offsets, intensity, rows, sections):
+def run_chain(angles, index_volume, offsets, intensity, rows, sections):
     _, height, columns = index_volume.shape
     layers = sections
     blocks = columns // LANE
@@ -337,8 +348,8 @@
     return pl.pallas_call(
         functools.partial(chain_kernel, rows, sections),
         out_shape=jax.ShapeDtypeStruct((1, height, columns), jnp.float32),
-        in_specs=[pl.BlockSpec(memory_space=pltpu.VMEM)] * 2 + [pl.BlockSpec(memory_space=pltpu.SMEM)]
-        + [pl.BlockSpec(memory_space=pltpu.VMEM)] * 3,
+        in_specs=[pl.BlockSpec(memory_space=pltpu.SMEM), pl.BlockSpec(memory_space=pltpu.VMEM),
+                  pl.BlockSpec(memory_space=pltpu.SMEM)] + [pl.BlockSpec(memory_space=pltpu.VMEM)] * 3,
         out_specs=pl.BlockSpec(memory_space=pltpu.VMEM),
         scratch_shapes=[
             pltpu.VMEM(plane, jnp.float32),
@@ -374,7 +385,7 @@
         ],
         compiler_params=pltpu.CompilerParams(
             collective_id=0, has_side_effects=True, vmem_limit_bytes=56 * 1024 * 1024),
-    )(u0, index_volume, offsets, intensity, band_table(height), column_bands())
+    )(angles, index_volume, offsets, intensity, band_table(height), column_bands())
 
 
 def plane_wave(angle, row_start, height, columns, total_rows, total_cols):
@@ -398,9 +409,7 @@
     total_rows = height * rows
     angle_count = angles.shape[0]
     angle_no = section_no % angle_count
-    angle = lax.dynamic_index_in_dim(angles, angle_no, 0, keepdims=False)
-    incident = plane_wave(angle, row_start, height, columns, total_rows, columns)
-    return run_chain(incident, index_volume, offsets, measured, rows, sections)
+    return run_chain(angles, index_volume, offsets, measured, rows, sections)
 
 
 def solution(mesh):

time: 121 us -> 118 us (0.975)
  between operations: 2 us -> 0.66 us
  other arithmetic: 1.31 us -> 0 us
  local copies, waits for them, and re-layouts: 2.81 us -> 1.57 us
where the time goes in v15:
time: 118 us; the launch traced here: 116 us
  Pallas kernels  114 us (97%)
  local copies, waits for them, and re-layouts  1.57 us (1%)
    pallas_call x1, Pallas kernels, run_chain(): pl.pallas_call(functools.partial(chain_kernel, rows, sections), out_shape...  114 us

profile of v15, /device:TPU:2, one launch (start us, length us, event | category | flops | bytes accessed | tf_op | source)
XLA Modules:
  0.0 116.3 jit_solution(14974731378963856557)
XLA Ops:
  0.7 114.1 %shard_map.64 = f32[1,16,2048]{2,1,0:T(8,128)} custom-call(s32[2]{0:T(128)} %angle_ref.1, bf16[1,16,2048]{2,1,0:T(8,128)(2,1)} %vol_ref.1, s32[1]{0:T(128)S(6)} %copy.8.off_ref, bf16[2,16,2048]{2,1,0:T(8,128)(2,1)} %inten_ref.1, f32[2,9,96,32]{3,2,1,0:T(8,128)} %constant.4.clone.table_ref, f32[2,3,128,256]{3,2,1,0:T(8,128)} %constant.5.clone.cband_ref), custom_call_target="tpu_custom_call" | custom-call | tf_op jit(solution)/shard_map/pallas_call | solution.py:348
  114.8 1.6 %copy.9 = f32[1,16,2048]{2,1,0:T(8,128)} copy(f32[1,16,2048]{2,1,0:T(8,128)} %shard_map.64) | data formatting | bytes 262144

commit v16 on v15

--- a/solution.py
+++ b/solution.py
@@ -104,6 +104,19 @@
     has_dn = me < rows - 1
 
     own_off[...] = jnp.full(own_off.shape, off_ref[0].astype(jnp.float32), jnp.float32)
+    barrier = pltpu.get_barrier_semaphore()
+
+    @pl.when(has_up)
+    def _():
+        pl.semaphore_signal(barrier, 1, device_id={"row": me - 1}, device_id_type=MESH)
+
+    @pl.when(has_dn)
+    def _():
+        pl.semaphore_signal(barrier, 1, device_id={"row": me + 1}, device_id_type=MESH)
+
+    for step in range(1, sections):
+        peer = (section + step) % sections
+        pl.semaphore_signal(barrier, 1, device_id={"depth": peer}, device_id_type=MESH)
     angle = angle_ref[section % angle_ref.shape[0]]
     across = angle - TILTS // 2
     along = lax.rem(3 * angle, TILTS) - TILTS // 2
@@ -115,19 +128,13 @@
     cycles = jnp.where(cycles < 0, cycles + period, cycles)
     wave_arg = 2.0 * math.pi / period * cycles.astype(jnp.float32)
     field_ref[...] = jnp.concatenate([jnp.cos(wave_arg), jnp.sin(wave_arg)], axis=0)
-    barrier = pltpu.get_barrier_semaphore()
-
-    @pl.when(has_up)
-    def _():
-        pl.semaphore_signal(barrier, 1, device_id={"row": me - 1}, device_id_type=MESH)
-
-    @pl.when(has_dn)
-    def _():
-        pl.semaphore_signal(barrier, 1, device_id={"row": me + 1}, device_id_type=MESH)
-
-    for step in range(1, sections):
-        peer = (section + step) % sections
-        pl.semaphore_signal(barrier, 1, device_id={"depth": peer}, device_id_type=MESH)
+    high, low = split_bf16(cband_ref[...])
+    chb_ref[...] = high
+    clb_ref[...] = low
+    zero_block = jnp.zeros((2 * height, LANE), jnp.bfloat16)
+    for ref in (bmh_ref, bml_ref):
+        ref[0] = zero_block
+        ref[blocks + 1] = zero_block
     peers = (me + rows - 1) // rows + (2 * rows - 2 - me) // rows
     pl.semaphore_wait(barrier, peers + sections - 1)
 
@@ -173,13 +180,6 @@
         rbh_ref[2 * layers - 1 - s] = high
         rbl_ref[2 * layers - 1 - s] = low
 
-    high, low = split_bf16(cband_ref[...])
-    chb_ref[...] = high
-    clb_ref[...] = low
-    zero_block = jnp.zeros((2 * height, LANE), jnp.bfloat16)
-    for ref in (bmh_ref, bml_ref):
-        ref[0] = zero_block
-        ref[blocks + 1] = zero_block
 
     def copies(k, c, store):
         cols = pl.ds(c * width, width)

time: 118 us -> 117 us (level)
  no operation moved by 1% of the time
where the time goes in v16:
time: 117 us; the launch traced here: 116 us
  Pallas kernels  114 us (97%)
  local copies, waits for them, and re-layouts  1.57 us (1%)
    pallas_call x1, Pallas kernels, run_chain(): pl.pallas_call(functools.partial(chain_kernel, rows, sections), out_shape...  114 us

profile of v16, /device:TPU:2, one launch (start us, length us, event | category | flops | bytes accessed | tf_op | source)
XLA Modules:
  0.0 115.8 jit_solution(15438327846147587945)
XLA Ops:
  0.7 113.6 %shard_map.64 = f32[1,16,2048]{2,1,0:T(8,128)} custom-call(s32[2]{0:T(128)} %angle_ref.1, bf16[1,16,2048]{2,1,0:T(8,128)(2,1)} %vol_ref.1, s32[1]{0:T(128)S(6)} %copy.8.off_ref, bf16[2,16,2048]{2,1,0:T(8,128)(2,1)} %inten_ref.1, f32[2,9,96,32]{3,2,1,0:T(8,128)} %constant.4.clone.table_ref, f32[2,3,128,256]{3,2,1,0:T(8,128)} %constant.5.clone.cband_ref), custom_call_target="tpu_custom_call" | custom-call | tf_op jit(solution)/shard_map/pallas_call | solution.py:348
  114.2 1.6 %copy.9 = f32[1,16,2048]{2,1,0:T(8,128)} copy(f32[1,16,2048]{2,1,0:T(8,128)} %shard_map.64) | data formatting | bytes 262144

commit v17 on v16

--- a/solution.py
+++ b/solution.py
@@ -136,31 +136,10 @@
         ref[0] = zero_block
         ref[blocks + 1] = zero_block
     peers = (me + rows - 1) // rows + (2 * rows - 2 - me) // rows
-    pl.semaphore_wait(barrier, peers + sections - 1)
-
-    def gathers(step, slot):
-        peer = (section + step) % sections
-        vol_copy = pltpu.make_async_remote_copy(
-            src_ref=vol_ref.at[0], dst_ref=vol_slots.at[slot], send_sem=send_vol.at[step],
-            recv_sem=recv_vol.at[slot], device_id={"depth": peer}, device_id_type=MESH)
-        off_copy = pltpu.make_async_remote_copy(
-            src_ref=own_off, dst_ref=off_slots.at[slot], send_sem=send_off.at[step],
-            recv_sem=recv_off.at[slot], device_id={"depth": peer}, device_id_type=MESH)
-        return vol_copy, off_copy
-
-    for step in range(1, sections):
-        for one in gathers(step, section):
-            one.start()
     vol_slots[section] = vol_ref[0]
     off_slots[section] = own_off[...]
     part_rows = 2 * height
-
-    def prepare(s):
-        @pl.when(s != section)
-        def _():
-            for one in gathers(1, s):
-                one.wait_recv()
-
+    def compute(s):
         phase = PHASE_SCALE * vol_slots[s].astype(jnp.float32)
         cos_ref[s] = jnp.cos(phase)
         sin_ref[s] = jnp.sin(phase)
@@ -179,6 +158,30 @@
         high, low = split_bf16(adjoint_band)
         rbh_ref[2 * layers - 1 - s] = high
         rbl_ref[2 * layers - 1 - s] = low
+
+    compute(section)
+    pl.semaphore_wait(barrier, peers + sections - 1)
+
+    def gathers(step, slot):
+        peer = (section + step) % sections
+        vol_copy = pltpu.make_async_remote_copy(
+            src_ref=vol_ref.at[0], dst_ref=vol_slots.at[slot], send_sem=send_vol.at[step],
+            recv_sem=recv_vol.at[slot], device_id={"depth": peer}, device_id_type=MESH)
+        off_copy = pltpu.make_async_remote_copy(
+            src_ref=own_off, dst_ref=off_slots.at[slot], send_sem=send_off.at[step],
+            recv_sem=recv_off.at[slot], device_id={"depth": peer}, device_id_type=MESH)
+        return vol_copy, off_copy
+
+    for step in range(1, sections):
+        for one in gathers(step, section):
+            one.start()
+
+    def prepare(s):
+        @pl.when(s != section)
+        def _():
+            for one in gathers(1, s):
+                one.wait_recv()
+            compute(s)
 
 
     def copies(k, c, store):

time: 117 us -> 117 us (level)
  no operation moved by 1% of the time
where the time goes in v17:
time: 117 us; the launch traced here: 116 us
  Pallas kernels  114 us (97%)
  local copies, waits for them, and re-layouts  1.57 us (1%)
    pallas_call x1, Pallas kernels, run_chain(): pl.pallas_call(functools.partial(chain_kernel, rows, sections), out_shape...  114 us

profile of v17, /device:TPU:2, one launch (start us, length us, event | category | flops | bytes accessed | tf_op | source)
XLA Modules:
  0.0 115.8 jit_solution(7058575008203014134)
XLA Ops:
  0.7 113.6 %shard_map.64 = f32[1,16,2048]{2,1,0:T(8,128)} custom-call(s32[2]{0:T(128)} %angle_ref.1, bf16[1,16,2048]{2,1,0:T(8,128)(2,1)} %vol_ref.1, s32[1]{0:T(128)S(6)} %copy.8.off_ref, bf16[2,16,2048]{2,1,0:T(8,128)(2,1)} %inten_ref.1, f32[2,9,96,32]{3,2,1,0:T(8,128)} %constant.4.clone.table_ref, f32[2,3,128,256]{3,2,1,0:T(8,128)} %constant.5.clone.cband_ref), custom_call_target="tpu_custom_call" | custom-call | tf_op jit(solution)/shard_map/pallas_call | solution.py:351
  114.2 1.6 %copy.9 = f32[1,16,2048]{2,1,0:T(8,128)} copy(f32[1,16,2048]{2,1,0:T(8,128)} %shard_map.64) | data formatting | bytes 262144

commit v18 on v17

--- a/solution.py
+++ b/solution.py
@@ -85,7 +85,7 @@
     return both[:rows] + both[rows:] + jnp.dot(a_high, x_low, preferred_element_type=f32)
 
 
-CHUNKS = 4
+CHUNKS = 2
 
 
 def chain_kernel(rows, sections, angle_ref, vol_ref, off_ref, inten_ref, table_ref, cband_ref,

time: 117 us -> 139 us (1.19)
  Pallas kernels: 114 us -> 135 us
    pallas_call x1, Pallas kernels: 114 us -> 135 us  [run_chain(): pl.pallas_call(functools.partial(chain_kernel, rows, sections), out_shape...]
where the time goes in v18:
time: 139 us; the launch traced here: 137 us
  Pallas kernels  135 us (97%)
  local copies, waits for them, and re-layouts  1.57 us (1%)
    pallas_call x1, Pallas kernels, run_chain(): pl.pallas_call(functools.partial(chain_kernel, rows, sections), out_shape...  135 us

profile of v18, /device:TPU:2, one launch (start us, length us, event | category | flops | bytes accessed | tf_op | source)
XLA Modules:
  0.0 136.9 jit_solution(12121291847041997171)
XLA Ops:
  0.7 134.7 %shard_map.64 = f32[1,16,2048]{2,1,0:T(8,128)} custom-call(s32[2]{0:T(128)} %angle_ref.1, bf16[1,16,2048]{2,1,0:T(8,128)(2,1)} %vol_ref.1, s32[1]{0:T(128)S(6)} %copy.8.off_ref, bf16[2,16,2048]{2,1,0:T(8,128)(2,1)} %inten_ref.1, f32[2,9,96,32]{3,2,1,0:T(8,128)} %constant.4.clone.table_ref, f32[2,3,128,256]{3,2,1,0:T(8,128)} %constant.5.clone.cband_ref), custom_call_target="tpu_custom_call" | custom-call | tf_op jit(solution)/shard_map/pallas_call | solution.py:351
  135.4 1.6 %copy.9 = f32[1,16,2048]{2,1,0:T(8,128)} copy(f32[1,16,2048]{2,1,0:T(8,128)} %shard_map.64) | data formatting | bytes 262144
